TPU v7x, 128 devices: a whole 4x4x4 slice. The times are simulated.
128 devices in a mesh: ang: 64 (over z, y_hi, x, core), rad: 2 (over y_lo).
Axes of the slice: x: 4, y: 4 (y_hi: 2, y_lo: 2; y = y_hi * 2 + y_lo), z: 4, core: 2. Of those that a mesh axis runs over, the one named last changes fastest.
Arguments:
- wave_function: float32 [2, 2, 256, 256, 256], P(None, None, 'ang', 'rad'), may hold values from -6 to 6
- potential: float32 [256, 256, 256], P('ang', 'rad'), may hold values from -3.140625 to 3.140625
Outputs:
- evolved: float32 [2, 2, 256, 256, 256], P(None, None, 'ang', 'rad')
All inputs are finite; a program needn't handle non-finite values.
Results may differ from a plain program's by a relative error of at most 0.00009.
Values sent between devices are 32-bit elements; how exact they have to be, the bound alone decides.
No kernel may reach another device: no remote copies, remote signals or barrier semaphores. Data moves between devices by JAX's collectives and lax.ppermute only.
A program may use at most 192 MiB of HBM per device.

v0:
```python
import math

import jax
import jax.numpy as jnp
from jax import lax
from jax.sharding import PartitionSpec as P

highest = lax.Precision.HIGHEST
radial_rate = 0.25
axial_rate = 1.5
band_weight = 0.1
angle_scale = 100000.0
inner_radius = 1.0
outer_radius = 10.0


def with_halo(x, sides, width):
    for axis, dim in sides:
        peers, length = (lax.axis_size(axis), x.shape[dim])
        up = [(i, (i + 1) % peers) for i in range(peers - 1)]
        down = [(j, i) for i, j in up]
        last = lax.slice_in_dim(x, length - width, length, axis=dim)
        first = lax.slice_in_dim(x, 0, width, axis=dim)
        before = lax.ppermute(last, axis, up)
        after = lax.ppermute(first, axis, down)
        x = jnp.concatenate([before, x, after], axis=dim)
    return x


def rotate_pair(field_pair, cosine, sine_values):
    real_part = cosine * field_pair[0] + sine_values * field_pair[1]
    imag_part = cosine * field_pair[1] - sine_values * field_pair[0]
    return jnp.stack([real_part, imag_part])


def local_stencil(field):
    extent = field.shape[-2]
    padding = [(0, 0)] * (field.ndim - 2) + [(2, 2), (0, 0)]
    padded = jnp.pad(field, padding)
    outer = padded[..., 0:extent, :] + padded[..., 4 : extent + 4, :]
    inner = padded[..., 1 : extent + 1, :] + padded[..., 3 : extent + 3, :]
    return (16.0 * inner - outer - 30.0 * field) / 12.0


def radial_laplacian(field_pair):
    rims = jnp.concatenate([field_pair[..., 0:2, :], field_pair[..., -2:, :]], axis=3)
    widened = with_halo(rims, (("rad", 3),), 2)
    below_far = widened[..., 0:1, :]
    below_near = widened[..., 1:2, :]
    above_near = widened[..., 6:7, :]
    above_far = widened[..., 7:8, :]
    low_fix = jnp.concatenate([(16.0 * below_near - below_far) / 12.0, -below_near / 12.0], axis=3)
    high_fix = jnp.concatenate([-above_near / 12.0, (16.0 * above_near - above_far) / 12.0], axis=3)
    result = local_stencil(field_pair)
    result = result.at[..., 0:2, :].add(low_fix)
    result = result.at[..., -2:, :].add(high_fix)
    return result


def radial_advance(field_pair):
    result_sum = field_pair
    summand = field_pair
    for degree in range(1, 4):
        applied = radial_laplacian(summand)
        factor = radial_rate / degree
        summand = jnp.stack([factor * applied[1], -factor * applied[0]])
        result_sum = result_sum + summand
    return result_sum


def sine_matrix(extent):
    ordinal = jnp.arange(extent, dtype=jnp.int32) + 1
    product = ordinal[:, None] * ordinal[None, :] % (2 * (extent + 1))
    return math.sqrt(2.0 / (extent + 1)) * jnp.sin(
        math.pi * product.astype(jnp.float32) / (extent + 1)
    )


def axial_advance(field_pair):
    extent = field_pair.shape[-1]
    matrix_values = sine_matrix(extent)
    ordinal = (jnp.arange(extent, dtype=jnp.int32) + 1).astype(jnp.float32)
    stiffness = axial_rate * (2.0 - 2.0 * jnp.cos(math.pi * ordinal / (extent + 1)))
    denominator = 1.0 + stiffness * stiffness
    gain_real = (1.0 - stiffness * stiffness) / denominator
    gain_imag = -2.0 * stiffness / denominator
    spectrum = jnp.matmul(field_pair, matrix_values, precision=highest)
    turned = jnp.stack(
        [
            gain_real * spectrum[0] - gain_imag * spectrum[1],
            gain_real * spectrum[1] + gain_imag * spectrum[0],
        ]
    )
    return jnp.matmul(turned, matrix_values, precision=highest)


def angle_coefficient(radius_index, radial_total):
    radius_value = (
        inner_radius
        + (outer_radius - inner_radius) * (radius_index.astype(jnp.float32) + 0.5) / radial_total
    )
    return angle_scale / (radius_value * radius_value)


def fourier_tables(extent):
    ordinal = jnp.arange(extent, dtype=jnp.int32)
    phase = (
        2.0 * math.pi * (ordinal[:, None] * ordinal[None, :] % extent).astype(jnp.float32) / extent
    )
    return (jnp.cos(phase), jnp.sin(phase))


def spectral_evolve(lines, coefficient):
    extent = lines.shape[-2]
    functions = lines.shape[1]
    cosine, sine_values = fourier_tables(extent)

    def transform(matrix_values, field):
        return jnp.stack(
            [
                jnp.dot(matrix_values, field[member], precision=highest)
                for member in range(functions)
            ]
        )

    freq_real = transform(cosine, lines[0]) + transform(sine_values, lines[1])
    freq_imag = transform(cosine, lines[1]) - transform(sine_values, lines[0])
    base_cosine = cosine[:, 1:2]
    band_value = 1.0 + 2.0 * band_weight * base_cosine
    second = coefficient * (2.0 * base_cosine - 2.0)
    denominator = band_value * band_value + second * second
    inverse_real = band_value * band_value / denominator
    inverse_imag = band_value * second / denominator
    solved_real = freq_real * inverse_real - freq_imag * inverse_imag
    solved_imag = freq_real * inverse_imag + freq_imag * inverse_real
    back_real = (transform(cosine, solved_real) - transform(sine_values, solved_imag)) / extent
    back_imag = (transform(cosine, solved_imag) + transform(sine_values, solved_real)) / extent
    return 2.0 * jnp.stack([back_real, back_imag]) - lines


def body(wave_function, potential):
    cosine = jnp.cos(potential)
    sine_values = jnp.sin(potential)
    rotated = rotate_pair(wave_function, cosine, sine_values)
    radial = radial_advance(rotated)
    axial = axial_advance(radial)
    angle_cells = axial.shape[2]
    radial_cells = axial.shape[3]
    axial_cells = axial.shape[4]
    radial_total = radial_cells * lax.axis_size("rad")
    first_radius = lax.axis_index("rad") * radial_cells
    flattened = axial.reshape(2, axial.shape[1], angle_cells, radial_cells * axial_cells)
    column_count = radial_cells * axial_cells // lax.axis_size("ang")
    first_column = lax.axis_index("ang") * column_count
    column = first_column + jnp.arange(column_count, dtype=jnp.int32)
    coefficient = angle_coefficient(first_radius + column // axial_cells, radial_total)
    evolved_lines = spectral_evolve(
        lax.all_to_all(flattened, "ang", split_axis=3, concat_axis=2, tiled=True), coefficient
    )
    angular = lax.all_to_all(evolved_lines, "ang", split_axis=2, concat_axis=3, tiled=True)
    angular = angular.reshape(axial.shape)
    return rotate_pair(angular, cosine, sine_values)


def solution(mesh):
    placed = (P(None, None, "ang", "rad", None), P("ang", "rad", None))
    return jax.shard_map(
        body,
        mesh=mesh,
        in_specs=placed,
        out_specs=P(None, None, "ang", "rad", None),
        check_vma=False,
    )
```

profile of v0, /device:TPU:1, one launch (start us, length us, event | category | flops | bytes accessed | tf_op | source)
XLA Modules:
  0.0 548.6 jit_solution(16721666798477744335)
XLA Ops:
  0.0 2.8 fusion.172
  2.8 1.8 multiply_add_fusion.3
  4.7 4.0 collective-permute-start
  8.7 1.3 collective-permute-start.1
  10.2 1.0 subtract_multiply_fusion.2
  11.4 2.0 collective-permute-done.1
  13.8 2.0 collective-permute-start.2
  15.9 1.0 subtract_multiply_fusion.1
  16.9 1.3 collective-permute-start.3
  18.3 3.2 collective-permute-done.3
  22.1 1.6 collective-permute-start.4
  23.7 1.0 subtract_multiply_fusion
  24.7 1.5 collective-permute-start.5
  26.4 3.0 collective-permute-done.5
  29.5 0.2 slice_multiply_fusion.1
  29.7 3.0 fusion
  32.8 0.3 multiply_subtract_fusion.2
  33.0 2.9 fusion.3
  35.9 45.3 %copy.22 = f32[2,2,4,128,256]{2,1,0,4,3:T(2,128)} copy(f32[2,2,4,128,256]{4,3,2,1,0:T(8,128)S(1)} %fusion.3) | data formatting | bytes 4194304 | tf_op jit(solution)/shard_map/reshape | solution.py:152
  81.2 103.9 %reshape.592 = f32[64,1,8192]{2,1,0:T(1,128)} reshape(f32[32768,2,2,4]{3,2,1,0:T(2,128)} %bitcast.66) | data formatting | bytes 4194304
  185.1 15.2 %all-to-all-start = ((f32[64,1,8192]{2,1,0:T(1,128)}), f32[64,1,8192]{2,1,0:T(1,128)S(1)}, u32[]{:S(2)}, u32[]{:S(2)}) async-start(f32[64,1,8192]{2,1,0:T(1,128)} %reshape.592), calls=%async_computation | async-start | bytes 4194304 | tf_op jit(solution)/shard_map/all_to_all | solution.py:158
  200.3 1.0 fusion.50
  201.3 1.2 fusion.20
  202.5 28.5 %all-to-all-done = f32[64,1,8192]{2,1,0:T(1,128)S(1)} async-done(((f32[64,1,8192]{2,1,0:T(1,128)}), f32[64,1,8192]{2,1,0:T(1,128)S(1)}, u32[]{:S(2)}, u32[]{:S(2)}) %all-to-all-start) | async-done | bytes 2097184 | tf_op jit(solution)/shard_map/all_to_all | solution.py:158
  231.0 1.3 copy-done.1
  232.3 0.6 broadcast.485
  232.9 7.6 %reduce.12 = f32[64,8192]{1,0:T(8,128)S(1)} reduce(f32[64,1,8192]{2,1,0:T(1,128)} %copy-done.1, f32[]{:T(128)} %broadcast.485), dimensions={1}, to_apply=%all_to_all.24.reduce_sub_computation | reduce | bytes 4194308 | tf_op jit(solution)/shard_map/all_to_all | solution.py:158
  240.5 128.1 %reshape.593 = f32[32768,2,2,4]{3,2,1,0:T(2,128)} reshape(f32[64,8192]{1,0:T(8,128)S(1)} %reduce.12) | data formatting | bytes 4194304
  368.6 71.2 %copy.14 = f32[2,2,4,64,512]{4,2,3,1,0:T(4,128)S(1)} copy(f32[2,2,4,64,512]{2,1,0,4,3:T(2,128)} %bitcast.3) | data formatting | bytes 4194304 | tf_op jit(solution)/shard_map/all_to_all | solution.py:158
  439.8 1.4 fusion.171
  441.2 2.0 squeeze.23
  443.2 3.4 convolution_bitcast_fusion.10
  446.6 3.4 convolution_bitcast_fusion.12
  450.0 2.0 squeeze.22
  452.1 3.4 convolution_bitcast_fusion.11
  455.5 3.4 convolution_bitcast_fusion.13
  458.9 2.0 squeeze.21
  460.9 3.4 convolution_bitcast_fusion.14
  464.3 3.4 convolution_bitcast_fusion.8
  467.7 2.0 squeeze.20
  469.7 3.0 convolution_bitcast_fusion.15
  472.7 2.6 convolution_bitcast_fusion.9
  475.3 2.2 multiply_subtract_fusion.1
  477.5 2.4 convolution_bitcast_fusion.4
  479.9 2.4 convolution_bitcast_fusion.5
  482.3 2.4 convolution_bitcast_fusion.6
  484.6 2.4 convolution_bitcast_fusion.7
  487.0 2.4 convolution_bitcast_fusion
  489.4 2.6 convolution_bitcast_fusion.1
  492.0 2.4 convolution_bitcast_fusion.2
  494.4 2.4 convolution_bitcast_fusion.3
  496.7 1.7 all_to_all.27
  498.4 1.9 fusion.16
  500.6 0.2 fusion.17
  500.8 1.4 copy-done
  502.2 0.5 fusion.7
  502.7 1.6 copy.15
  504.3 35.3 %all_to_all.33 = f32[2,2,256,512]{3,1,0,2:T(2,128)S(1)} all-to-all(f32[2,2,256,512]{3,1,0,2:T(2,128)S(1)} %copy.15), channel_id=1, replica_groups=mesh['ang'=64,'rad'=2] {'ang'}, dimensions={2} | all-to-all | bytes 4194304 | tf_op jit(solution)/shard_map/all_to_all | solution.py:160
  539.6 1.7 fusion.170
  541.3 0.6 copy.16
  542.1 2.8 copy.17
  544.9 1.4 squeeze.29
  546.3 0.3 multiply_add_fusion
  546.6 1.5 pad_maximum_fusion.3
  (46 shorter events, 2.0 us)
Async XLA Ops:
  4.7 6.6 %collective-permute-start = (f32[2,2,4,2,256]{4,3,2,1,0:T(2,128)S(1)}, f32[2,2,4,2,256]{4,3,2,1,0:T(2,128)S(1)}, u32[]{:S(2)}, u32[]{:S(2)}) collective-permute-start(f32[2,2,4,2,256]{4,3,2,1,0:T(2,128)S(1)} %get-tuple-element.102), channel_id=1, source_target_pairs={{0,1},{2,3},{4,5},{6,7},{8,9},{10,11},{12,13},{14,15},{16,17},{18,... | collective-permute-start | bytes 98312 | tf_op jit(solution)/shard_map/ppermute | solution.py:24
  8.7 4.7 collective-permute-start.1
  13.8 4.4 collective-permute-start.2
  16.9 4.7 collective-permute-start.3
  22.1 4.2 collective-permute-start.4
  24.7 4.7 collective-permute-start.5
  185.1 45.9 %all-to-all-start = ((f32[64,1,8192]{2,1,0:T(1,128)}), f32[64,1,8192]{2,1,0:T(1,128)S(1)}, u32[]{:S(2)}, u32[]{:S(2)}) async-start(f32[64,1,8192]{2,1,0:T(1,128)} %reshape.592), calls=%async_computation | async-start | bytes 4194304 | tf_op jit(solution)/shard_map/all_to_all | solution.py:158
  231.0 1.3 copy-start.1
  469.7 5.6 %copy-start.2 = (f32[256,512]{1,0:T(8,128)S(1)}, f32[256,512]{1,0:T(8,128)}, u32[]{:S(2)}) copy-start(f32[256,512]{1,0:T(8,128)} %get-tuple-element.120) | copy-start | bytes 1572868
  469.7 5.6 %copy-start.3 = (f32[256,512]{1,0:T(8,128)S(1)}, f32[256,512]{1,0:T(8,128)}, u32[]{:S(2)}) copy-start(f32[256,512]{1,0:T(8,128)} %get-tuple-element.121) | copy-start | bytes 1572868
  469.7 5.6 %copy-start.4 = (f32[1,256,512]{2,1,0:T(8,128)S(1)}, f32[1,256,512]{2,1,0:T(8,128)}, u32[]{:S(2)}) copy-start(f32[1,256,512]{2,1,0:T(8,128)} %convolution_bitcast_fusion.10) | copy-start | bytes 1572868
  469.7 5.6 %copy-start.5 = (f32[1,256,512]{2,1,0:T(8,128)S(1)}, f32[1,256,512]{2,1,0:T(8,128)}, u32[]{:S(2)}) copy-start(f32[1,256,512]{2,1,0:T(8,128)} %convolution_bitcast_fusion.12) | copy-start | bytes 1572868
  498.4 1.9 copy-start.6
  498.4 1.9 copy-start.7
  498.4 2.0 copy-start.8
  498.4 2.1 copy-start.9
  500.6 1.6 copy-start
where the time goes:
time: 556 us; the launch traced here: 549 us
  local copies, waits for them, and re-layouts  374 us (67%)
  matrix products  51.1 us (9%)
  waiting for transfers between devices  36.7 us (7%)
  blocking collectives  35.3 us (6%)
  starting transfers between devices  26.9 us (5%)
  other arithmetic  23.3 us (4%)
    unnamed x22, local copies, waits for them, and re-layouts  235 us
    all_to_all x3, local copies, waits for them, and re-layouts, body(): lax.all_to_all(flattened, 'ang', split_axis=3, concat_axis=2, tiled=True)  73.4 us
    reshape x1, local copies, waits for them, and re-layouts, body(): axial.reshape(2, axial.shape[1], angle_cells, radial_cells * axial_cells)  45.3 us
    dot_general x16, matrix products, transform(): jnp.dot(matrix_values, field[member], precision=highest)  45.2 us
    all_to_all x1, blocking collectives, body(): lax.all_to_all(evolved_lines, 'ang', split_axis=2, concat_axis=3, tiled=T...  35.3 us
    all_to_all x1, waiting for transfers between devices, body(): lax.all_to_all(flattened, 'ang', split_axis=3, concat_axis=2, tiled=True)  28.5 us
    all_to_all x1, starting transfers between devices, body(): lax.all_to_all(flattened, 'ang', split_axis=3, concat_axis=2, tiled=True)  15.2 us
  transfers between devices with their start and end apart: 7, of which 4 were waited for; matrix products, arithmetic and copies ran while one was open for 1% of the time, Pallas kernels for 0%

commit v1 on v0

v1 whole, which is shorter than its diff:
```python
import functools

import jax
import jax.numpy as jnp
import numpy as np
from jax import lax
from jax.experimental import pallas as pl
from jax.experimental.pallas import tpu as pltpu
from jax.sharding import PartitionSpec as P

NA = 256
NR = 256
NZ = 256
CHIPS = 32
LR = 128
f32 = jnp.float32
bf16 = jnp.bfloat16


def split(a):
    hi = np.asarray(a, np.float32).astype(jnp.bfloat16)
    lo = (np.asarray(a, np.float64) - hi.astype(np.float64)).astype(np.float32)
    return hi, lo.astype(jnp.bfloat16)


def coefficients():
    j = np.arange(NR, dtype=np.float32)
    radius = np.float32(1.0) + np.float32(9.0) * (j + np.float32(0.5)) / np.float32(NR)
    return (np.float32(100000.0) / (radius * radius)).astype(np.float64)


def radial_tables():
    lap = np.zeros((NR, NR))
    for d, c in ((0, -30.0), (1, 16.0), (2, -1.0)):
        for j in range(NR - d):
            lap[j, j + d] = c / 12.0
            lap[j + d, j] = c / 12.0
    k = 0.25 * lap
    even = np.eye(NR) - k @ k / 2.0
    odd = -k + k @ k @ k / 6.0
    main, halo = [], []
    for side in range(2):
        own = slice(LR * side, LR * side + LR)
        a, b = even[own, own], odd[own, own]
        hi, lo = split(np.block([[a, -b], [b, a]]))
        main.append(np.concatenate([hi, hi, lo], axis=1))
        rows = slice(120, 128) if side == 0 else slice(128, 136)
        cols = slice(128, 136) if side == 0 else slice(120, 128)
        a, b = even[rows, cols], odd[rows, cols]
        halo.append(np.block([[a, -b], [b, a]]))
    return np.stack(main), np.stack(halo).astype(np.float32)


def axial_tables():
    n = np.arange(1, NZ + 1)
    sine = np.sqrt(2.0 / (NZ + 1)) * np.sin(np.pi * (n[:, None] * n[None, :]) / (NZ + 1))
    s = 1.5 * (2.0 - 2.0 * np.cos(np.pi * n / (NZ + 1)))
    gain = (1.0 - 1j * s) / (1.0 + 1j * s)
    full = (sine * gain[None, :]) @ sine
    re, im = full.real, full.imag
    return split(np.block([[re, im], [-im, re]]))


def dirichlet(c, size):
    off = 0.1 - 1j * c
    mat = np.zeros((size, size), complex)
    for t in range(size):
        mat[t, t] = 1.0 + 2j * c
        if t:
            mat[t, t - 1] = off
            mat[t - 1, t] = off
    inv = np.linalg.inv(mat)
    return inv, -off * inv[:, 0]


def angle_tables():
    cell = np.zeros((2, LR, 128), np.float32)
    chip = np.zeros((2, 2, 64, 8, 128), np.float32)
    mid = np.zeros((2, 2, 32, 8, 128), np.float32)
    angle = np.arange(NA)
    second = 2.0 * np.cos(2.0 * np.pi * angle / NA) - 2.0
    for g, c in enumerate(coefficients()):
        rho = 0.1 / (0.1 - 1j * c)
        scale = 2.4 * (1.0 - rho)
        inv, p = dirichlet(c, 3)
        w0 = 2.0 * rho - 1.0
        values = [
            (p[0] + p[2]) / 2,
            (p[0] - p[2]) / 2,
            p[1],
            w0,
            (w0 + scale * (inv[0, 0] + inv[0, 2])) / 2,
            (w0 + scale * (inv[0, 0] - inv[0, 2])) / 2,
            scale * inv[0, 1],
            w0 + scale * inv[1, 1],
        ]
        side, j = divmod(g, LR)
        for k, value in enumerate(values):
            cell[side, j, 2 * k] = value.real
            cell[side, j, 2 * k + 1] = value.imag
        inv8, p8 = dirichlet(c, 7)
        core, jj = divmod(j, 64)
        sign = np.array([-1, -1, 1, 1, -1, -1, 1, 1.0])
        middle, local = p8[3], scale * inv8[3, 3]
        chip[side, core, jj, :, 0] = middle.real
        chip[side, core, jj, :, 1] = middle.imag * sign
        chip[side, core, jj, :, 2] = local.real
        chip[side, core, jj, :, 3] = local.imag * sign
        symbol = 1.0 / (1.2 + (0.1 - 1j * c) * second)
        coarse = scale * symbol.reshape(8, CHIPS).sum(0) / 8.0
        pos, r = divmod(jj, 2)
        mid[side, core, pos, 2 * r, :64] = np.repeat(coarse.real, 2)
        mid[side, core, pos, 2 * r + 1, :64] = np.repeat(coarse.imag, 2)
    return cell, chip.reshape(4, 512, 128), mid.reshape(128, 8, 128)


def fourier_tables():
    k = np.arange(CHIPS)
    q = np.arange(CHIPS)
    fwd = np.zeros((2, CHIPS, 2, CHIPS, 2, 2, 2))
    inv = np.zeros((CHIPS, 2, 2, 2, 2, CHIPS, 2))
    for n in range(2):
        phase = -2.0 * np.pi * ((k[:, None] * (q[None, :] + n)) % CHIPS) / CHIPS
        e = np.exp(1j * phase)
        for s in range(2):
            fwd[0, :, s, :, n, 0, s] = e.real
            fwd[0, :, s, :, n, 1, s] = -e.imag
            fwd[1, :, s, :, n, 0, s] = e.imag
            fwd[1, :, s, :, n, 1, s] = e.real
            d = np.conj(e).T / CHIPS
            inv[:, n, 0, s, 0, :, s] = d.real
            inv[:, n, 0, s, 1, :, s] = -d.imag
            inv[:, n, 1, s, 0, :, s] = d.imag
            inv[:, n, 1, s, 1, :, s] = d.real
    fwd = fwd.reshape(128, 256)
    inv = inv.reshape(256, 128)
    fh, fl = split(fwd)
    ih, il = split(inv)
    return np.concatenate([fh, fh, fl], axis=1), np.concatenate([ih, ih, il], axis=1)


@functools.cache
def tables():
    main, halo = radial_tables()
    ah, al = axial_tables()
    cell, chip, mid = angle_tables()
    fwd, inv = fourier_tables()
    return dict(main=main, halo=halo, ah=ah, al=al, cell=cell, chip=chip, mid=mid, fwd=fwd, inv=inv)


def dot(a, b):
    return jnp.dot(a, b, preferred_element_type=f32)


def halves(x):
    hi = x.astype(bf16)
    return hi, (x - hi.astype(f32)).astype(bf16)


def stacked(x):
    hi, lo = halves(x)
    return jnp.concatenate([hi, lo, hi], axis=0)


def times(x, high, low):
    hi, lo = halves(x)
    return dot(hi, high) + dot(lo, high) + dot(hi, low)


SIN = (
    -1.0 / 6.0,
    1.0 / 120.0,
    -1.0 / 5040.0,
    1.0 / 362880.0,
    -1.0 / 39916800.0,
    1.0 / 6227020800.0,
)
COS = (
    -1.0 / 2.0,
    1.0 / 24.0,
    -1.0 / 720.0,
    1.0 / 40320.0,
    -1.0 / 3628800.0,
    1.0 / 479001600.0,
    -1.0 / 87178291200.0,
)


def cos_sin(x):
    y = 0.5 * x
    q = y * y
    a = jnp.full_like(q, SIN[-1])
    for c in SIN[-2::-1]:
        a = a * q + c
    b = jnp.full_like(q, COS[-1])
    for c in COS[-2::-1]:
        b = b * q + c
    s = y + y * (q * a)
    c = 1.0 + q * b
    s2 = s + s
    return 1.0 - s2 * s, s2 * c


def cmul(cr, ci, x):
    return (cr * x[0] - ci * x[1], cr * x[1] + ci * x[0])


def add(x, y):
    return (x[0] + y[0], x[1] + y[1])


def sub(x, y):
    return (x[0] - y[0], x[1] - y[1])


def weights(coef, k, width):
    shape = (coef.shape[0], width)
    return tuple(jnp.broadcast_to(coef[:, i : i + 1], shape) for i in (2 * k, 2 * k + 1))


def reduce_cells(f, coef):
    width = f[0][0].shape[-1]
    s, d = add(f[1], f[3]), sub(f[1], f[3])
    even = add(cmul(*weights(coef, 0, width), s), cmul(*weights(coef, 2, width), f[2]))
    odd = cmul(*weights(coef, 1, width), d)
    return add(add(f[0], even), odd), sub(even, odd)


def advance_kernel(idx, w, pot, main, coef, f, cs, uv):
    a = pl.program_id(0)
    c, s = cos_sin(pot[0])
    cs[0, 0] = c
    cs[1, 0] = s
    for m in range(2):
        re, im = w[0, m, 0], w[1, m, 0]
        x = jnp.concatenate([c * re + s * im, c * im - s * re], axis=0)
        f[m, pl.ds(a, 1)] = dot(main[0], stacked(x)).reshape(1, 2, LR, NZ)

    @pl.when(a == 3)
    def _():
        def block(b, carry):
            rows = pl.ds(pl.multiple_of(b * 8, 8), 8)
            base = (lax.shift_right_logical(b, 3) ^ idx[1]) * 1024 + (b & 7) * 128
            k = coef[0, rows, :]
            for m in range(2):
                u, v = reduce_cells([(f[m, t, 0, rows, :], f[m, t, 1, rows, :]) for t in range(4)], k)
                for i, value in enumerate((u[0], u[1], v[0], v[1])):
                    for z in range(2):
                        uv[pl.ds(base + 8 * z + 2 * i + m, 8, stride=16), :] = value[:, 128 * z : 128 * z + 128]
            return carry

        lax.fori_loop(0, 16, block, 0)


def halo_kernel(idx, halo, table, coef, f_in, uv_in, f, uv):
    corrections = []
    parts = []
    for t in range(4):
        c, s = cos_sin(halo[4, t])
        for m in range(2):
            re, im = halo[m, t], halo[2 + m, t]
            parts.append(jnp.concatenate([c * re + s * im, c * im - s * re], axis=0))
    x = jnp.concatenate(parts, axis=1)
    out = jnp.dot(table[0], x, precision=lax.Precision.HIGHEST, preferred_element_type=f32)
    k = coef[0]
    for m in range(2):
        cells = []
        for t in range(4):
            piece = out[:, (2 * t + m) * NZ : (2 * t + m + 1) * NZ]
            cells.append((piece[:8], piece[8:]))
            f[m, t, 0] = f_in[m, t, 0] + piece[:8]
            f[m, t, 1] = f_in[m, t, 1] + piece[8:]
        u, v = reduce_cells(cells, k)
        for i, value in enumerate((u[0], u[1], v[0], v[1])):
            for z in range(2):
                rows = pl.ds(8 * z + 2 * i + m, 8, stride=16)
                uv[rows, :] = uv_in[rows, :] + value[:, 128 * z : 128 * z + 128]


def row_swap(x, shift):
    return pltpu.roll(x, shift, 2)


def first_rows(core, shape):
    row = lax.broadcasted_iota(jnp.int32, shape, 2)
    return (lax.shift_right_logical(row, 2) ^ core) == 0


def tiles(x):
    return x.reshape(x.shape[0] // 16, 2, 8, 128)


def wide(x):
    x = tiles(x)
    rows = 8 * x.shape[0]
    return jnp.concatenate([x[:, z].reshape(rows, 128) for z in range(2)], axis=1)


def narrow(x):
    rows = x.shape[0] // 8
    return jnp.stack([x[:, 128 * z : 128 * z + 128].reshape(rows, 8, 128) for z in range(2)], axis=1)


def row_weights(chip):
    return chip[0].reshape(64, 1, 8, 128)


def pair_kernel(idx, own, received, chip, uv, m_out):
    a, b = tiles(own[...]), tiles(received[...])
    mask = first_rows(idx[1], a.shape)
    ends = jnp.where(mask, a, b)
    inner = jnp.where(mask, b, a)
    inner = inner + row_swap(inner, 4)
    k = row_weights(chip)
    out = ends + k[..., 0:1] * inner + k[..., 1:2] * row_swap(inner, 2)
    uv[...] = out.reshape(uv.shape)
    m_out[...] = inner.reshape(uv.shape)


def pair_axial_kernel(idx, m, chip, ah, al, out):
    e = times(wide(m[...]), ah[...], al[...])
    row = lax.broadcasted_iota(jnp.int32, (1, 1, 8, 128), 2)
    sign = jnp.where((row & 2) == 0, -1.0, 1.0)
    x = narrow(e[:, :NZ]) + sign * row_swap(narrow(e[:, NZ:]), 2)
    k = row_weights(chip)
    x = k[..., 2:3] * x + k[..., 3:4] * row_swap(x, 2)
    out[...] = x.reshape(out.shape)


def local_kernel(idx, f, coef, ah, al, out):
    k = coef[0]
    cells = [(f[0, t, 0], f[0, t, 1]) for t in range(4)]
    s, d = add(cells[1], cells[3]), sub(cells[1], cells[3])
    even = add(cmul(*weights(k, 4, NZ), s), cmul(*weights(k, 6, NZ), cells[2]))
    odd = cmul(*weights(k, 5, NZ), d)
    parts = [
        cmul(*weights(k, 3, NZ), cells[0]),
        add(even, odd),
        add(cmul(*weights(k, 6, NZ), s), cmul(*weights(k, 7, NZ), cells[2])),
        sub(even, odd),
    ]
    x = jnp.concatenate([jnp.concatenate(p, axis=1) for p in parts], axis=0)
    y = times(x, ah[...], al[...])
    rows = cells[0][0].shape[0]
    for t in range(4):
        out[0, t, 0] = y[t * rows : (t + 1) * rows, :NZ]
        out[0, t, 1] = y[t * rows : (t + 1) * rows, NZ:]


def middle_kernel(idx, x, fwd, inv, mid, ah, al, out):
    x = x[...].reshape(CHIPS, 2, 2, 8, 128)
    x = jnp.concatenate([x[:, r, z].reshape(256, 128) for r in range(2) for z in range(2)], axis=1)
    g = dot(fwd[...], stacked(x))
    k = mid[0].T
    rows = []
    for r in range(2):
        col = slice(r * NZ, (r + 1) * NZ)
        kr, ki = weights(k[:64], r, NZ)
        rows.append(jnp.concatenate(cmul(kr, ki, (g[:64, col], g[64:, col])), axis=1))
    h = times(jnp.concatenate(rows, axis=0), ah[...], al[...])
    h = jnp.concatenate(
        [jnp.concatenate([h[64 * r : 64 * r + 64, :NZ], h[64 * r : 64 * r + 64, NZ:]], axis=0) for r in range(2)],
        axis=1,
    )
    y = dot(inv[...], stacked(h))
    y = jnp.stack([y[:, 128 * i : 128 * i + 128].reshape(CHIPS, 8, 128) for i in range(4)], axis=1)
    out[...] = y.reshape(out.shape)


def spread_kernel(idx, y, mA, chip, keep, send):
    x = tiles(y[...])
    total = x + row_swap(x, 4)
    k = row_weights(chip)
    inner = k[..., 0:1] * total + k[..., 1:2] * row_swap(total, 2) + tiles(mA[...])
    mask = first_rows(idx[1], x.shape)
    keep[...] = jnp.where(mask, x, inner).reshape(keep.shape)
    send[...] = jnp.where(mask, inner, x).reshape(keep.shape)


def finish_kernel(idx, w, keep, received, cs, coef, out, y):
    half = lax.shift_right_logical(pl.program_id(0), 1)

    @pl.when(half == idx[1])
    def _():
        y[...] = keep[...]

    @pl.when(half != idx[1])
    def _():
        y[...] = received[...]

    k = coef[0]
    rows = k.shape[0]
    for m in range(2):
        a = [
            jnp.concatenate([y[pl.ds(8 * z + 2 * i + m, rows, stride=16), :] for z in range(2)], axis=1)
            for i in range(4)
        ]
        left, right = (a[0], a[1]), (a[2], a[3])
        s, d = add(left, right), sub(left, right)
        even = cmul(*weights(k, 0, NZ), s)
        odd = cmul(*weights(k, 1, NZ), d)
        parts = [left, add(even, odd), cmul(*weights(k, 2, NZ), s), sub(even, odd)]
        for t in range(4):
            re, im = w[m, t, 0] + parts[t][0], w[m, t, 1] + parts[t][1]
            c, sn = cs[0, t], cs[1, t]
            out[0, m, t] = c * re + sn * im
            out[1, m, t] = c * im - sn * re


def call(kernel, idx, args, in_specs, out_shape, out_specs, grid=(1,), scratch=(), aliases=None, flops=0, nbytes=0):
    return pl.pallas_call(
        kernel,
        out_shape=out_shape,
        grid_spec=pltpu.PrefetchScalarGridSpec(
            num_scalar_prefetch=1, grid=grid, in_specs=in_specs, out_specs=out_specs, scratch_shapes=scratch
        ),
        input_output_aliases=aliases or {},
        compiler_params=pltpu.CompilerParams(dimension_semantics=("arbitrary",) * len(grid)),
        cost_estimate=pl.CostEstimate(flops=flops, bytes_accessed=nbytes, transcendentals=0),
        name=kernel.__name__,
    )(idx, *args)


def whole(shape):
    return pl.BlockSpec(shape, lambda *_: (0,) * len(shape))


def body(wave, potential):
    t = tables()
    rad = lax.axis_index("rad")
    ang = lax.axis_index("ang")
    core = ang % 2
    chip = ang // 2
    lane = jnp.arange(8, dtype=jnp.int32)
    edge = jnp.where(rad == 0, 15, 0)
    edge_uv = ((edge // 8) ^ core) * 8 + edge % 8
    idx = jnp.zeros(8, jnp.int32)
    for i, v in enumerate((rad, core, chip, rad * 2 + core, rad * 64 + core * 32 + chip, edge, edge_uv)):
        idx = jnp.where(lane == i, v.astype(jnp.int32), idx)

    start = jnp.where(rad == 0, 120, 0)
    rim = lax.dynamic_slice_in_dim(wave, start, 8, axis=3).reshape(4, 4, 8, NZ)
    rim_p = lax.dynamic_slice_in_dim(potential, start, 8, axis=1).reshape(1, 4, 8, NZ)
    halo = lax.ppermute(jnp.concatenate([rim, rim_p]), "rad", [(0, 1), (1, 0)])

    sds = jax.ShapeDtypeStruct
    field = sds((2, 4, 2, LR, NZ), f32)
    lines = sds((1024, 128), f32)
    f, cs, uv = call(
        advance_kernel,
        idx,
        (wave, potential, t["main"], t["cell"]),
        [
            pl.BlockSpec((2, 2, 1, LR, NZ), lambda a, i: (0, 0, a, 0, 0)),
            pl.BlockSpec((1, LR, NZ), lambda a, i: (a, 0, 0)),
            pl.BlockSpec((1, 256, 768), lambda a, i: (i[0], 0, 0)),
            pl.BlockSpec((1, LR, 128), lambda a, i: (i[0], 0, 0)),
        ],
        (field, sds((2, 4, LR, NZ), f32), sds((2048, 128), f32)),
        (
            whole(field.shape),
            pl.BlockSpec((2, 1, LR, NZ), lambda a, i: (0, a, 0, 0)),
            whole((2048, 128)),
        ),
        grid=(4,),
        flops=1 << 30,
        nbytes=5 << 20,
    )
    f, uv = call(
        halo_kernel,
        idx,
        (halo, t["halo"], t["cell"], f, uv),
        [
            whole((5, 4, 8, NZ)),
            pl.BlockSpec((1, 16, 16), lambda a, i: (i[0], 0, 0)),
            pl.BlockSpec((1, 8, 128), lambda a, i: (i[0], i[5], 0)),
            pl.BlockSpec((2, 4, 2, 8, NZ), lambda a, i: (0, 0, 0, i[5], 0)),
            pl.BlockSpec((128, 128), lambda a, i: (i[6], 0)),
        ],
        (field, sds((2048, 128), f32)),
        (
            pl.BlockSpec((2, 4, 2, 8, NZ), lambda a, i: (0, 0, 0, i[5], 0)),
            pl.BlockSpec((128, 128), lambda a, i: (i[6], 0)),
        ),
        aliases={4: 0, 5: 1},
        flops=1 << 20,
        nbytes=1 << 20,
    )
    other = [(i, i ^ 1) for i in range(2 * CHIPS)]
    groups = [[2 * q + c for q in range(CHIPS)] for c in range(2)]
    exchange = functools.partial(
        lax.all_to_all, axis_name="ang", split_axis=0, concat_axis=0, tiled=True, axis_index_groups=groups
    )
    received = lax.ppermute(uv[1024:], "ang", other)
    chip_spec = pl.BlockSpec((1, 512, 128), lambda a, i: (i[3], 0, 0))
    lines_spec = whole((1024, 128))
    UV, m = call(
        pair_kernel,
        idx,
        (uv[:1024], received, t["chip"]),
        [lines_spec, lines_spec, chip_spec],
        (lines, lines),
        (lines_spec, lines_spec),
        flops=1 << 20,
        nbytes=2 << 20,
    )
    x = exchange(UV)
    local = call(
        local_kernel,
        idx,
        (f, t["cell"], t["ah"], t["al"]),
        [
            pl.BlockSpec((1, 4, 2, 64, NZ), lambda s, j, i: (s, 0, 0, j, 0)),
            pl.BlockSpec((1, 64, 128), lambda s, j, i: (i[0], j, 0)),
            whole((512, 512)),
            whole((512, 512)),
        ],
        field,
        pl.BlockSpec((1, 4, 2, 64, NZ), lambda s, j, i: (s, 0, 0, j, 0)),
        grid=(2, 2),
        flops=3 << 30,
        nbytes=5 << 20,
    )
    mA = call(
        pair_axial_kernel,
        idx,
        (m, t["chip"], t["ah"], t["al"]),
        [lines_spec, chip_spec, whole((256, 512)), whole((256, 512))],
        lines,
        lines_spec,
        flops=1 << 29,
        nbytes=2 << 20,
    )
    y = call(
        middle_kernel,
        idx,
        (x, t["fwd"], t["inv"], t["mid"], t["ah"], t["al"]),
        [
            lines_spec,
            whole((128, 768)),
            whole((256, 384)),
            pl.BlockSpec((1, 8, 128), lambda a, i: (i[4], 0, 0)),
            whole((512, 512)),
            whole((512, 512)),
        ],
        lines,
        lines_spec,
        flops=1 << 29,
        nbytes=3 << 20,
    )
    y = exchange(y)
    keep, send = call(
        spread_kernel,
        idx,
        (y, mA, t["chip"]),
        [lines_spec, lines_spec, chip_spec],
        (lines, lines),
        (lines_spec, lines_spec),
        flops=1 << 20,
        nbytes=2 << 20,
    )
    received = lax.ppermute(send, "ang", other)
    return call(
        finish_kernel,
        idx,
        (local, keep, received, cs, t["cell"]),
        [
            pl.BlockSpec((2, 4, 2, 32, NZ), lambda a, i: (0, 0, 0, a, 0)),
            pl.BlockSpec((512, 128), lambda a, i: (a % 2, 0)),
            pl.BlockSpec((512, 128), lambda a, i: (a % 2, 0)),
            pl.BlockSpec((2, 4, 32, NZ), lambda a, i: (0, 0, a, 0)),
            pl.BlockSpec((1, 32, 128), lambda a, i: (i[0], a, 0)),
        ],
        sds(wave.shape, f32),
        pl.BlockSpec((2, 2, 4, 32, NZ), lambda a, i: (0, 0, 0, a, 0)),
        grid=(4,),
        scratch=(pltpu.VMEM((512, 128), f32),),
        flops=1 << 22,
        nbytes=6 << 20,
    )


def solution(mesh):
    placed = (P(None, None, "ang", "rad", None), P("ang", "rad", None))
    return jax.shard_map(
        body,
        mesh=mesh,
        in_specs=placed,
        out_specs=P(None, None, "ang", "rad", None),
        check_vma=False,
    )
```

time: 556 us -> 86.4 us (0.16); the launches traced: 549 us -> 85.6 us
  local copies, waits for them, and re-layouts: 374 us -> 6.81 us
  matrix products: 51.1 us -> 0 us
  Pallas kernels: 0 us -> 36 us
  waiting for transfers between devices: 36.7 us -> 9.14 us
  other arithmetic: 23.3 us -> 0.6 us
  starting transfers between devices: 26.9 us -> 11 us
  blocking collectives: 35.3 us -> 22 us
    unnamed x22 -> x8, local copies, waits for them, and re-layouts: 235 us -> 3.04 us
    all_to_all x3 -> x0, local copies, waits for them, and re-layouts: 73.4 us -> none  [body(): lax.all_to_all(flattened, 'ang', split_axis=3, concat_axis=2, tiled=True)]
    dot_general x18 -> x0, matrix products: 51.1 us -> none  [the longest x16 45.2 us: transform(): jnp.dot(matrix_values, field[member], precision=highest)]
    reshape x1, local copies, waits for them, and re-layouts: 45.3 us -> 0.76 us  [body(): lax.dynamic_slice_in_dim(potential, start, 8, axis=1).reshape(1, 4, 8, NZ)]
    pallas_call x0 -> x8, Pallas kernels: none -> 36 us  [call(): pl.pallas_call(kernel, out_shape=out_shape, grid_spec=pltpu.PrefetchScala...]
    all_to_all x1, waiting for transfers between devices: 28.5 us -> 7.6 us  [body(): y = exchange(y)]
    all_to_all x1, blocking collectives: 35.3 us -> 22 us  [body(): x = exchange(UV)]
    all_to_all x1, starting transfers between devices: 15.2 us -> 4.75 us  [body(): y = exchange(y)]
  transfers between devices with their start and end apart: 7 -> 4, of which waited for: 4 -> 2; matrix products, arithmetic and copies ran while one was open for 1% -> 1% of each run, Pallas kernels for 0% -> 21%
where the time goes in v1:
time: 86.4 us; the launch traced here: 85.6 us
  Pallas kernels  36 us (42%)
  blocking collectives  22 us (25%)
  starting transfers between devices  11 us (13%)
  waiting for transfers between devices  9.14 us (11%)
  local copies, waits for them, and re-layouts  6.81 us (8%)
    pallas_call x8, Pallas kernels, call(): pl.pallas_call(kernel, out_shape=out_shape, grid_spec=pltpu.PrefetchScala...  36 us
    all_to_all x1, blocking collectives, body(): x = exchange(UV)  22 us
    all_to_all x1, waiting for transfers between devices, body(): y = exchange(y)  7.6 us
    all_to_all x1, starting transfers between devices, body(): y = exchange(y)  4.75 us
    ppermute x1, starting transfers between devices, body(): received = lax.ppermute(send, 'ang', other)  3.13 us
    unnamed x8, local copies, waits for them, and re-layouts  3.04 us
    ppermute x1, starting transfers between devices, body(): halo = lax.ppermute(jnp.concatenate([rim, rim_p]), 'rad', [(0, 1), (1, 0)])  2.19 us
    slice x1, local copies, waits for them, and re-layouts, body(): received = lax.ppermute(uv[1024:], 'ang', other)  2.1 us
  transfers between devices with their start and end apart: 4, of which 2 were waited for; matrix products, arithmetic and copies ran while one was open for 1% of the time, Pallas kernels for 21%

profile of v1, /device:TPU:1, one launch (start us, length us, event | category | flops | bytes accessed | tf_op | source)
XLA Modules:
  0.0 85.6 jit_solution(9505625122747329598)
XLA Ops:
  0.0 0.8 dynamic-slice_bitcast_fusion
  0.8 0.9 %constant_dynamic-slice_fusion = f32[2,2,4,8,256]{4,3,2,1,0:T(8,128)S(1)} fusion(f32[2,2,4,128,256]{4,3,2,1,0:T(8,128)} %w.1, s32[]{:T(128)S(6)} %select_n.66), kind=kLoop, calls=%fused_computation.9 | loop fusion | bytes 262148 | tf_op jit(solution)/shard_map/dynamic_slice | solution.py:442
  1.7 2.2 %collective-permute-start = (f32[5,4,8,256]{3,2,1,0:T(8,128)S(1)}, f32[5,4,8,256]{3,2,1,0:T(8,128)S(1)}, u32[]{:S(2)}, u32[]{:S(2)}) collective-permute-start(f32[5,4,8,256]{3,2,1,0:T(8,128)S(1)} %pad_maximum_fusion), channel_id=1, source_target_pairs={{0,1},{1,0},{2,3},{3,2},{4,5},{5,4},{6,7},{7,6},{8,9},{9,8},{10,11... | collective-permute-start | bytes 491528 | tf_op jit(solution)/shard_map/ppermute | solution.py:444
  3.9 0.6 compare_select_fusion.6.idx
  4.5 8.2 %advance_kernel.1 = (f32[2,4,2,128,256]{4,3,2,1,0:T(8,128)}, f32[2,4,128,256]{3,2,1,0:T(8,128)}, f32[2048,128]{1,0:T(8,128)}) custom-call(s32[8]{0:T(128)} %compare_select_fusion.6.idx, f32[2,2,4,128,256]{4,3,2,1,0:T(8,128)} %w.1, f32[4,128,256]{2,1,0:T(8,128)} %pot.1, bf16[2,256,768]{2,1,0:T(8,128)(2,1)} %constant.97.clone.main, ...), custom_call_target="tpu_custom_call" | custom-call | flops 1073741824 | bytes 5242880 | tf_op jit(solution)/shard_map/advance_kernel/pallas_call | solution.py:411
  12.7 0.0 collective-permute-done.halo
  12.7 0.0 copy-start.3
  12.7 0.7 copy-done.3
  13.3 2.7 %halo_kernel.1 = (f32[2,4,2,128,256]{4,3,2,1,0:T(8,128)}, f32[2048,128]{1,0:T(8,128)}) custom-call(s32[8]{0:T(128)} %compare_select_fusion.6.idx, f32[5,4,8,256]{3,2,1,0:T(8,128)} %copy-done.3, f32[2,16,16]{2,1,0:T(8,128)} %constant.99.clone.table, f32[2,128,128]{2,1,0:T(8,128)} %constant.98.clone.coef, ...), custom_call_target="tpu_custom_call", output_to_operand_aliasing={{0}: (4, {}), {1}: (5, {})} | custom-call | flops 1048576 | bytes 1048576 | tf_op jit(solution)/shard_map/halo_kernel/pallas_call | solution.py:411
  16.0 2.1 %fusion = (f32[1024,128]{1,0:T(8,128)S(1)}, f32[1024,128]{1,0:T(8,128)}) fusion(f32[2048,128]{1,0:T(8,128)} %get-tuple-element.17), kind=kLoop, calls=%fused_computation.10 | loop fusion | bytes 2097152 | tf_op jit(solution)/shard_map/slice | solution.py:494
  18.1 0.9 %collective-permute-start.1 = (f32[1024,128]{1,0:T(8,128)S(1)}, f32[1024,128]{1,0:T(8,128)S(1)}, u32[]{:S(2)}, u32[]{:S(2)}) collective-permute-start(f32[1024,128]{1,0:T(8,128)S(1)} %get-tuple-element.23), channel_id=1, source_target_pairs={{0,2},{2,0},{4,6},{6,4},{8,10},{10,8},{12,14},{14,12},{16,18},{18,... | collective-permute-start | bytes 1572872 | tf_op jit(solution)/shard_map/ppermute | solution.py:494
  19.0 1.5 %collective-permute-done.1.received = f32[1024,128]{1,0:T(8,128)S(1)} collective-permute-done((f32[1024,128]{1,0:T(8,128)S(1)}, f32[1024,128]{1,0:T(8,128)S(1)}, u32[]{:S(2)}, u32[]{:S(2)}) %collective-permute-start.1) | collective-permute-done | bytes 524320 | tf_op jit(solution)/shard_map/ppermute | solution.py:494
  20.6 0.0 copy-start.2
  20.6 0.8 copy-done.2
  21.4 3.0 %pair_kernel.1 = (f32[1024,128]{1,0:T(8,128)}, f32[1024,128]{1,0:T(8,128)}) custom-call(s32[8]{0:T(128)} %compare_select_fusion.6.idx, f32[1024,128]{1,0:T(8,128)} %get-tuple-element.24.own, f32[1024,128]{1,0:T(8,128)} %copy-done.2, f32[4,512,128]{2,1,0:T(8,128)} %constant.100.clone.chip), custom_call_target="tpu_custom_call" | custom-call | flops 1048576 | bytes 2097152 | tf_op jit(solution)/shard_map/pair_kernel/pallas_call | solution.py:411
  24.4 22.0 %all_to_all.22 = f32[32,32,128]{2,1,0:T(8,128)} all-to-all(f32[32,32,128]{2,1,0:T(8,128)} %bitcast.10), channel_id=1, replica_groups={{0,4,8,12,16,20,24,28,32,36,40,44,48,52,56,60,64,68,72,76,80,84,88,92,9..., dimensions={0} | all-to-all | bytes 1048576 | tf_op jit(solution)/shard_map/all_to_all | solution.py:507
  46.4 4.0 %middle_kernel.1 = f32[1024,128]{1,0:T(8,128)} custom-call(s32[8]{0:T(128)} %compare_select_fusion.6.idx, f32[1024,128]{1,0:T(8,128)} %bitcast.9, bf16[128,768]{1,0:T(8,128)(2,1)} %constant.103.clone.fwd, bf16[256,384]{1,0:T(8,128)(2,1)} %constant.104.clone.inv, f32[128,8,128]{2,1,0:T(8,128)} %constant.105.clone.mid, bf16[512,512]{1,0:T(8,128)(2,1)} %constant.101.clone.ah, ...), custom_call_target="tpu_custom_call" | custom-call | flops 536870912 | bytes 3145728 | tf_op jit(solution)/shard_map/middle_kernel/pallas_call | solution.py:411
  50.3 4.7 %all-to-all-start.1 = ((f32[32,32,128]{2,1,0:T(8,128)}), f32[32,32,128]{2,1,0:T(8,128)S(1)}, u32[]{:S(2)}, u32[]{:S(2)}) async-start(f32[32,32,128]{2,1,0:T(8,128)} %bitcast.8), calls=%async_computation.1 | async-start | bytes 1048576 | tf_op jit(solution)/shard_map/all_to_all | solution.py:551
  55.1 3.3 %pair_axial_kernel.1.mA = f32[1024,128]{1,0:T(8,128)} custom-call(s32[8]{0:T(128)} %compare_select_fusion.6.idx, f32[1024,128]{1,0:T(8,128)} %get-tuple-element.19.m, f32[4,512,128]{2,1,0:T(8,128)} %constant.100.clone.chip, bf16[512,512]{1,0:T(8,128)(2,1)} %constant.101.clone.ah, bf16[512,512]{1,0:T(8,128)(2,1)} %constant.102.clone.al), custom_call_target="tpu_custom_call" | custom-call | flops 536870912 | bytes 2097152 | tf_op jit(solution)/shard_map/pair_axial_kernel/pallas_call | solution.py:411
  58.4 7.6 %all-to-all-done.1 = f32[32,32,128]{2,1,0:T(8,128)S(1)} async-done(((f32[32,32,128]{2,1,0:T(8,128)}), f32[32,32,128]{2,1,0:T(8,128)S(1)}, u32[]{:S(2)}, u32[]{:S(2)}) %all-to-all-start.1) | async-done | bytes 524320 | tf_op jit(solution)/shard_map/all_to_all | solution.py:551
  66.0 0.0 copy-start
  66.0 0.8 copy-done
  66.8 3.2 %spread_kernel.1 = (f32[1024,128]{1,0:T(8,128)}, f32[1024,128]{1,0:T(8,128)}) custom-call(s32[8]{0:T(128)} %compare_select_fusion.6.idx, f32[1024,128]{1,0:T(8,128)} %bitcast.7, f32[1024,128]{1,0:T(8,128)} %pair_axial_kernel.1.mA, f32[4,512,128]{2,1,0:T(8,128)} %constant.100.clone.chip), custom_call_target="tpu_custom_call" | custom-call | flops 1048576 | bytes 2097152 | tf_op jit(solution)/shard_map/spread_kernel/pallas_call | solution.py:411
  70.0 3.1 %collective-permute-start.2 = (f32[1024,128]{1,0:T(8,128)}, f32[1024,128]{1,0:T(8,128)S(1)}, u32[]{:S(2)}, u32[]{:S(2)}) collective-permute-start(f32[1024,128]{1,0:T(8,128)} %get-tuple-element.21), channel_id=1, source_target_pairs={{0,2},{2,0},{4,6},{6,4},{8,10},{10,8},{12,14},{14,12},{16,18},{18,... | collective-permute-start | bytes 1572872 | tf_op jit(solution)/shard_map/ppermute | solution.py:562
  73.1 6.3 %local_kernel.1.w = f32[2,4,2,128,256]{4,3,2,1,0:T(8,128)} custom-call(s32[8]{0:T(128)} %compare_select_fusion.6.idx, f32[2,4,2,128,256]{4,3,2,1,0:T(8,128)} %get-tuple-element.16.f, f32[2,128,128]{2,1,0:T(8,128)} %constant.98.clone.coef, bf16[512,512]{1,0:T(8,128)(2,1)} %constant.101.clone.ah, bf16[512,512]{1,0:T(8,128)(2,1)} %constant.102.clone.al), custom_call_target="tpu_custom_call" | custom-call | flops 3221225472 | bytes 5242880 | tf_op jit(solution)/shard_map/local_kernel/pallas_call | solution.py:411
  79.5 0.0 collective-permute-done.2.received
  79.5 0.0 copy-start.1
  79.5 0.8 copy-done.1
  80.2 5.4 %finish_kernel.1 = f32[2,2,4,128,256]{4,3,2,1,0:T(8,128)} custom-call(s32[8]{0:T(128)} %compare_select_fusion.6.idx, f32[2,4,2,128,256]{4,3,2,1,0:T(8,128)} %local_kernel.1.w, f32[1024,128]{1,0:T(8,128)} %get-tuple-element.20.keep, f32[1024,128]{1,0:T(8,128)} %copy-done.1, f32[2,4,128,256]{3,2,1,0:T(8,128)} %get-tuple-element.22.cs, ...), custom_call_target="tpu_custom_call" | custom-call | flops 4194304 | bytes 6291456 | tf_op jit(solution)/shard_map/finish_kernel/pallas_call | solution.py:411
  (1 shorter events, 0.0 us)
Async XLA Ops:
  1.7 11.0 %collective-permute-start = (f32[5,4,8,256]{3,2,1,0:T(8,128)S(1)}, f32[5,4,8,256]{3,2,1,0:T(8,128)S(1)}, u32[]{:S(2)}, u32[]{:S(2)}) collective-permute-start(f32[5,4,8,256]{3,2,1,0:T(8,128)S(1)} %pad_maximum_fusion), channel_id=1, source_target_pairs={{0,1},{1,0},{2,3},{3,2},{4,5},{5,4},{6,7},{7,6},{8,9},{9,8},{10,11... | collective-permute-start | bytes 491528 | tf_op jit(solution)/shard_map/ppermute | solution.py:444
  12.7 0.7 copy-start.3
  18.1 2.5 %collective-permute-start.1 = (f32[1024,128]{1,0:T(8,128)S(1)}, f32[1024,128]{1,0:T(8,128)S(1)}, u32[]{:S(2)}, u32[]{:S(2)}) collective-permute-start(f32[1024,128]{1,0:T(8,128)S(1)} %get-tuple-element.23), channel_id=1, source_target_pairs={{0,2},{2,0},{4,6},{6,4},{8,10},{10,8},{12,14},{14,12},{16,18},{18,... | collective-permute-start | bytes 1572872 | tf_op jit(solution)/shard_map/ppermute | solution.py:494
  20.6 0.8 copy-start.2
  50.3 15.7 %all-to-all-start.1 = ((f32[32,32,128]{2,1,0:T(8,128)}), f32[32,32,128]{2,1,0:T(8,128)S(1)}, u32[]{:S(2)}, u32[]{:S(2)}) async-start(f32[32,32,128]{2,1,0:T(8,128)} %bitcast.8), calls=%async_computation.1 | async-start | bytes 1048576 | tf_op jit(solution)/shard_map/all_to_all | solution.py:551
  66.0 0.8 copy-start
  70.0 9.5 %collective-permute-start.2 = (f32[1024,128]{1,0:T(8,128)}, f32[1024,128]{1,0:T(8,128)S(1)}, u32[]{:S(2)}, u32[]{:S(2)}) collective-permute-start(f32[1024,128]{1,0:T(8,128)} %get-tuple-element.21), channel_id=1, source_target_pairs={{0,2},{2,0},{4,6},{6,4},{8,10},{10,8},{12,14},{14,12},{16,18},{18,... | collective-permute-start | bytes 1572872 | tf_op jit(solution)/shard_map/ppermute | solution.py:562
  79.5 0.8 copy-start.1

commit v2 on v1

--- a/solution.py
+++ b/solution.py
@@ -58,7 +58,7 @@
     gain = (1.0 - 1j * s) / (1.0 + 1j * s)
     full = (sine * gain[None, :]) @ sine
     re, im = full.real, full.imag
-    return split(np.block([[re, im], [-im, re]]))
+    return split(np.stack([re, im - re, re + im]))
 
 
 def dirichlet(c, size):
@@ -167,6 +167,11 @@
     return dot(hi, high) + dot(lo, high) + dot(hi, low)
 
 
+def complex_times(re, im, high, low):
+    p, q, r = [times(x, high[i], low[i]) for i, x in enumerate((re + im, re, im))]
+    return p - r, p + q
+
+
 SIN = (
     -1.0 / 6.0,
     1.0 / 120.0,
@@ -226,8 +231,22 @@
     return add(add(f[0], even), odd), sub(even, odd)
 
 
-def advance_kernel(idx, w, pot, main, coef, f, cs, uv):
+def advance_kernel(idx, w, pot, main, coef, *refs):
+    n = (len(refs) - 6) // 2
+    sources, (f_out, cs, uv), targets = refs[:n], refs[n : n + 3], refs[n + 3 : -3]
+    f, sems, f_sems = refs[-3:]
     a = pl.program_id(0)
+    own = {1: idx[3], 2: idx[0]}
+    copies = [
+        pltpu.make_async_copy(x.at[own[i]] if i in own else x, y, sems.at[i])
+        for i, (x, y) in enumerate(zip(sources, targets))
+    ]
+
+    @pl.when(a == 0)
+    def _():
+        for copy in copies:
+            copy.start()
+
     c, s = cos_sin(pot[0])
     cs[0, 0] = c
     cs[1, 0] = s
@@ -235,6 +254,7 @@
         re, im = w[0, m, 0], w[1, m, 0]
         x = jnp.concatenate([c * re + s * im, c * im - s * re], axis=0)
         f[m, pl.ds(a, 1)] = dot(main[0], stacked(x)).reshape(1, 2, LR, NZ)
+    pltpu.make_async_copy(f.at[:, a], f_out.at[:, a], f_sems.at[a]).start()
 
     @pl.when(a == 3)
     def _():
@@ -250,31 +270,36 @@
             return carry
 
         lax.fori_loop(0, 16, block, 0)
-
-
-def halo_kernel(idx, halo, table, coef, f_in, uv_in, f, uv):
-    corrections = []
-    parts = []
+        for copy in copies:
+            copy.wait()
+        for t in range(4):
+            pltpu.make_async_copy(f.at[:, t], f_out.at[:, t], f_sems.at[t]).wait()
+
+
+def rim_kernel(idx, w, pot, out):
     for t in range(4):
-        c, s = cos_sin(halo[4, t])
+        c, s = cos_sin(pot[t])
         for m in range(2):
-            re, im = halo[m, t], halo[2 + m, t]
-            parts.append(jnp.concatenate([c * re + s * im, c * im - s * re], axis=0))
-    x = jnp.concatenate(parts, axis=1)
-    out = jnp.dot(table[0], x, precision=lax.Precision.HIGHEST, preferred_element_type=f32)
-    k = coef[0]
+            re, im = w[0, m, t], w[1, m, t]
+            x = jnp.concatenate([c * re + s * im, c * im - s * re], axis=0)
+            out[:, (2 * t + m) * NZ : (2 * t + m + 1) * NZ] = x
+
+
+def halo_kernel(idx, halo, table, coef, uv_in, corr, uv):
+    edge_uv = idx[6] * 128
+    out = jnp.dot(table[idx[0]], halo[...], precision=lax.Precision.HIGHEST, preferred_element_type=f32)
+    corr[...] = out
+    k = coef[pl.ds(pl.multiple_of(idx[5] * 8, 8), 8), :]
     for m in range(2):
         cells = []
         for t in range(4):
             piece = out[:, (2 * t + m) * NZ : (2 * t + m + 1) * NZ]
             cells.append((piece[:8], piece[8:]))
-            f[m, t, 0] = f_in[m, t, 0] + piece[:8]
-            f[m, t, 1] = f_in[m, t, 1] + piece[8:]
         u, v = reduce_cells(cells, k)
         for i, value in enumerate((u[0], u[1], v[0], v[1])):
             for z in range(2):
-                rows = pl.ds(8 * z + 2 * i + m, 8, stride=16)
-                uv[rows, :] = uv_in[rows, :] + value[:, 128 * z : 128 * z + 128]
+                line = pl.ds(edge_uv + 8 * z + 2 * i + m, 8, stride=16)
+                uv[line, :] = uv_in[line, :] + value[:, 128 * z : 128 * z + 128]
 
 
 def row_swap(x, shift):
@@ -302,7 +327,7 @@
 
 
 def row_weights(chip):
-    return chip[0].reshape(64, 1, 8, 128)
+    return chip[...].reshape(64, 1, 8, 128)
 
 
 def pair_kernel(idx, own, received, chip, uv, m_out):
@@ -318,18 +343,46 @@
 
 
 def pair_axial_kernel(idx, m, chip, ah, al, out):
-    e = times(wide(m[...]), ah[...], al[...])
+    x = wide(m[...])
     row = lax.broadcasted_iota(jnp.int32, (1, 1, 8, 128), 2)
     sign = jnp.where((row & 2) == 0, -1.0, 1.0)
-    x = narrow(e[:, :NZ]) + sign * row_swap(narrow(e[:, NZ:]), 2)
+    a = times(x, ah[0], al[0])
+    b = a + times(x, ah[1], al[1])
+    x = narrow(a) + sign * row_swap(narrow(b), 2)
     k = row_weights(chip)
     x = k[..., 2:3] * x + k[..., 3:4] * row_swap(x, 2)
     out[...] = x.reshape(out.shape)
 
 
-def local_kernel(idx, f, coef, ah, al, out):
-    k = coef[0]
-    cells = [(f[0, t, 0], f[0, t, 1]) for t in range(4)]
+def local_kernel(idx, f, coef, corr, *refs):
+    sources, out, targets = refs[:5], refs[5], refs[6:11]
+    g, sems = refs[11:]
+    ah, al = targets[:2]
+    copies = [
+        pltpu.make_async_copy(x.at[idx[4]] if i == 4 else x, y, sems.at[i])
+        for i, (x, y) in enumerate(zip(sources, targets))
+    ]
+    m, j = pl.program_id(0), pl.program_id(1)
+    step = 2 * m + j
+
+    @pl.when(step == 0)
+    def _():
+        for copy in copies:
+            copy.start()
+
+    g[...] = f[0]
+
+    for side, row in ((0, 56), (1, 0)):
+
+        @pl.when((idx[0] == side) & (j == 1 - side))
+        def _():
+            for t in range(4):
+                at = pl.ds(pl.multiple_of((2 * t + m) * NZ, NZ), NZ)
+                for c in range(2):
+                    g[t, c, row : row + 8, :] += corr[8 * c : 8 * c + 8, at]
+
+    k = coef[pl.ds(pl.multiple_of(j * 64, 64), 64), :]
+    cells = [(g[t, 0], g[t, 1]) for t in range(4)]
     s, d = add(cells[1], cells[3]), sub(cells[1], cells[3])
     even = add(cmul(*weights(k, 4, NZ), s), cmul(*weights(k, 6, NZ), cells[2]))
     odd = cmul(*weights(k, 5, NZ), d)
@@ -339,35 +392,54 @@
         add(cmul(*weights(k, 6, NZ), s), cmul(*weights(k, 7, NZ), cells[2])),
         sub(even, odd),
     ]
-    x = jnp.concatenate([jnp.concatenate(p, axis=1) for p in parts], axis=0)
-    y = times(x, ah[...], al[...])
-    rows = cells[0][0].shape[0]
+
+    @pl.when(step == 0)
+    def _():
+        for copy in copies[:2]:
+            copy.wait()
+
+    re = jnp.concatenate([p[0] for p in parts], axis=0)
+    im = jnp.concatenate([p[1] for p in parts], axis=0)
+    re, im = complex_times(re, im, ah, al)
     for t in range(4):
-        out[0, t, 0] = y[t * rows : (t + 1) * rows, :NZ]
-        out[0, t, 1] = y[t * rows : (t + 1) * rows, NZ:]
-
-
-def middle_kernel(idx, x, fwd, inv, mid, ah, al, out):
+        out[0, t, 0] = re[t * 64 : (t + 1) * 64]
+        out[0, t, 1] = im[t * 64 : (t + 1) * 64]
+
+    @pl.when(step == 3)
+    def _():
+        for copy in copies[2:]:
+            copy.wait()
+
+
+def middle_kernel(idx, x, fwd, inv, mid, ah, al, after, after_too, out):
     x = x[...].reshape(CHIPS, 2, 2, 8, 128)
     x = jnp.concatenate([x[:, r, z].reshape(256, 128) for r in range(2) for z in range(2)], axis=1)
     g = dot(fwd[...], stacked(x))
-    k = mid[0].T
+    k = mid[...].T
     rows = []
     for r in range(2):
         col = slice(r * NZ, (r + 1) * NZ)
         kr, ki = weights(k[:64], r, NZ)
-        rows.append(jnp.concatenate(cmul(kr, ki, (g[:64, col], g[64:, col])), axis=1))
-    h = times(jnp.concatenate(rows, axis=0), ah[...], al[...])
-    h = jnp.concatenate(
-        [jnp.concatenate([h[64 * r : 64 * r + 64, :NZ], h[64 * r : 64 * r + 64, NZ:]], axis=0) for r in range(2)],
-        axis=1,
-    )
+        rows.append(cmul(kr, ki, (g[:64, col], g[64:, col])))
+    re, im = complex_times(*[jnp.concatenate([p[c] for p in rows], axis=0) for c in range(2)], ah, al)
+    h = jnp.concatenate([jnp.concatenate([x[64 * r : 64 * r + 64] for x in (re, im)], axis=0) for r in range(2)], axis=1)
     y = dot(inv[...], stacked(h))
     y = jnp.stack([y[:, 128 * i : 128 * i + 128].reshape(CHIPS, 8, 128) for i in range(4)], axis=1)
     out[...] = y.reshape(out.shape)
 
 
-def spread_kernel(idx, y, mA, chip, keep, send):
+def fetch(row, w, cs, w_out, cs_out, sems):
+    rows = pl.ds(pl.multiple_of(row, 64), 64)
+    copies = [pltpu.make_async_copy(cs.at[:, :, rows, :], cs_out, sems.at[2])]
+    for m in range(2):
+        copies.append(pltpu.make_async_copy(w.at[m, :, :, rows, :], w_out.at[m], sems.at[m]))
+    return copies
+
+
+def spread_kernel(idx, y, mA, chip, w, cs, keep, send, w_out, cs_out, sems):
+    copies = fetch(idx[1] * 64, w, cs, w_out, cs_out, sems)
+    for copy in copies:
+        copy.start()
     x = tiles(y[...])
     total = x + row_swap(x, 4)
     k = row_weights(chip)
@@ -375,24 +447,19 @@
     mask = first_rows(idx[1], x.shape)
     keep[...] = jnp.where(mask, x, inner).reshape(keep.shape)
     send[...] = jnp.where(mask, inner, x).reshape(keep.shape)
-
-
-def finish_kernel(idx, w, keep, received, cs, coef, out, y):
-    half = lax.shift_right_logical(pl.program_id(0), 1)
-
-    @pl.when(half == idx[1])
-    def _():
-        y[...] = keep[...]
-
-    @pl.when(half != idx[1])
-    def _():
-        y[...] = received[...]
-
-    k = coef[0]
-    rows = k.shape[0]
+    for copy in copies:
+        copy.wait()
+
+
+def finish_kernel(half, idx, w, cs, y, coef, out):
+    j = pl.program_id(0)
+    rows = out.shape[3]
+    here = pl.ds(pl.multiple_of(j * rows, rows), rows)
+    k = coef[pl.ds(pl.multiple_of((idx[1] ^ half) * 64 + j * rows, rows), rows), :]
+    first = j * rows * 16
     for m in range(2):
         a = [
-            jnp.concatenate([y[pl.ds(8 * z + 2 * i + m, rows, stride=16), :] for z in range(2)], axis=1)
+            jnp.concatenate([y[pl.ds(first + 8 * z + 2 * i + m, rows, stride=16), :] for z in range(2)], axis=1)
             for i in range(4)
         ]
         left, right = (a[0], a[1]), (a[2], a[3])
@@ -401,10 +468,30 @@
         odd = cmul(*weights(k, 1, NZ), d)
         parts = [left, add(even, odd), cmul(*weights(k, 2, NZ), s), sub(even, odd)]
         for t in range(4):
-            re, im = w[m, t, 0] + parts[t][0], w[m, t, 1] + parts[t][1]
-            c, sn = cs[0, t], cs[1, t]
+            re, im = w[m, t, 0, here, :] + parts[t][0], w[m, t, 1, here, :] + parts[t][1]
+            c, sn = cs[0, t, here, :], cs[1, t, here, :]
             out[0, m, t] = c * re + sn * im
             out[1, m, t] = c * im - sn * re
+
+
+def finish_own_kernel(idx, w, cs, y, coef, w_all, cs_all, out, w_out, cs_out, sems):
+    copies = fetch((idx[1] ^ 1) * 64, w_all, cs_all, w_out, cs_out, sems)
+
+    @pl.when(pl.program_id(0) == 0)
+    def _():
+        for copy in copies:
+            copy.start()
+
+    finish_kernel(0, idx, w, cs, y, coef, out)
+
+    @pl.when(pl.program_id(0) == pl.num_programs(0) - 1)
+    def _():
+        for copy in copies:
+            copy.wait()
+
+
+def finish_other_kernel(idx, w, cs, y, coef, before, out):
+    finish_kernel(1, idx, w, cs, y, coef, out)
 
 
 def call(kernel, idx, args, in_specs, out_shape, out_specs, grid=(1,), scratch=(), aliases=None, flops=0, nbytes=0):
@@ -415,7 +502,9 @@
             num_scalar_prefetch=1, grid=grid, in_specs=in_specs, out_specs=out_specs, scratch_shapes=scratch
         ),
         input_output_aliases=aliases or {},
-        compiler_params=pltpu.CompilerParams(dimension_semantics=("arbitrary",) * len(grid)),
+        compiler_params=pltpu.CompilerParams(
+            dimension_semantics=("arbitrary",) * len(grid), vmem_limit_bytes=24 << 20
+        ),
         cost_estimate=pl.CostEstimate(flops=flops, bytes_accessed=nbytes, transcendentals=0),
         name=kernel.__name__,
     )(idx, *args)
@@ -423,6 +512,18 @@
 
 def whole(shape):
     return pl.BlockSpec(shape, lambda *_: (0,) * len(shape))
+
+
+VM = pl.BlockSpec(memory_space=pltpu.VMEM)
+ANY = pl.BlockSpec(memory_space=pl.ANY)
+
+
+def near(*arrays):
+    return tuple(pltpu.with_memory_space_constraint(x, pltpu.VMEM) for x in arrays)
+
+
+def far(*arrays):
+    return tuple(pltpu.with_memory_space_constraint(x, pltpu.HBM) for x in arrays)
 
 
 def body(wave, potential):
@@ -438,51 +539,56 @@
     for i, v in enumerate((rad, core, chip, rad * 2 + core, rad * 64 + core * 32 + chip, edge, edge_uv)):
         idx = jnp.where(lane == i, v.astype(jnp.int32), idx)
 
-    start = jnp.where(rad == 0, 120, 0)
-    rim = lax.dynamic_slice_in_dim(wave, start, 8, axis=3).reshape(4, 4, 8, NZ)
-    rim_p = lax.dynamic_slice_in_dim(potential, start, 8, axis=1).reshape(1, 4, 8, NZ)
-    halo = lax.ppermute(jnp.concatenate([rim, rim_p]), "rad", [(0, 1), (1, 0)])
-
-    sds = jax.ShapeDtypeStruct
-    field = sds((2, 4, 2, LR, NZ), f32)
+    sds = pltpu.VMEM
+    wave, potential = far(wave, potential)
+    rim = call(
+        rim_kernel,
+        idx,
+        (wave, potential),
+        [
+            pl.BlockSpec((2, 2, 4, 8, NZ), lambda a, i: (0, 0, 0, i[5], 0)),
+            pl.BlockSpec((4, 8, NZ), lambda a, i: (0, i[5], 0)),
+        ],
+        sds((16, 8 * NZ), f32),
+        VM,
+    )
+    halo = lax.ppermute(rim, "rad", [(0, 1), (1, 0)])
+    field = pltpu.HBM((2, 4, 2, LR, NZ), f32)
     lines = sds((1024, 128), f32)
-    f, cs, uv = call(
+    names = ("halo", "chip", "cell", "ah", "al", "fwd", "inv", "mid")
+    stored = far(*(t[k] for k in names))
+    shapes = [x.shape[1:] if k in ("chip", "cell", "mid") else x.shape for k, x in zip(names, stored)]
+    targets = tuple(sds(shape, x.dtype) for shape, x in zip(shapes, stored))
+    f, cs, uv, halo_table, chip_table, cell = call(
         advance_kernel,
         idx,
-        (wave, potential, t["main"], t["cell"]),
+        (wave, potential, *far(t["main"]), stored[2], *stored[:3]),
         [
             pl.BlockSpec((2, 2, 1, LR, NZ), lambda a, i: (0, 0, a, 0, 0)),
             pl.BlockSpec((1, LR, NZ), lambda a, i: (a, 0, 0)),
             pl.BlockSpec((1, 256, 768), lambda a, i: (i[0], 0, 0)),
             pl.BlockSpec((1, LR, 128), lambda a, i: (i[0], 0, 0)),
-        ],
-        (field, sds((2, 4, LR, NZ), f32), sds((2048, 128), f32)),
-        (
-            whole(field.shape),
-            pl.BlockSpec((2, 1, LR, NZ), lambda a, i: (0, a, 0, 0)),
-            whole((2048, 128)),
+        ]
+        + [ANY] * 3,
+        (field, pltpu.HBM((2, 4, LR, NZ), f32), sds((2048, 128), f32)) + targets[:3],
+        (ANY, pl.BlockSpec((2, 1, LR, NZ), lambda a, i: (0, a, 0, 0)), VM, VM, VM, VM),
+        grid=(4,),
+        scratch=(
+            pltpu.VMEM((2, 4, 2, LR, NZ), f32),
+            pltpu.SemaphoreType.DMA((3,)),
+            pltpu.SemaphoreType.DMA((4,)),
         ),
-        grid=(4,),
         flops=1 << 30,
         nbytes=5 << 20,
     )
-    f, uv = call(
+    corr, uv = call(
         halo_kernel,
         idx,
-        (halo, t["halo"], t["cell"], f, uv),
-        [
-            whole((5, 4, 8, NZ)),
-            pl.BlockSpec((1, 16, 16), lambda a, i: (i[0], 0, 0)),
-            pl.BlockSpec((1, 8, 128), lambda a, i: (i[0], i[5], 0)),
-            pl.BlockSpec((2, 4, 2, 8, NZ), lambda a, i: (0, 0, 0, i[5], 0)),
-            pl.BlockSpec((128, 128), lambda a, i: (i[6], 0)),
-        ],
-        (field, sds((2048, 128), f32)),
-        (
-            pl.BlockSpec((2, 4, 2, 8, NZ), lambda a, i: (0, 0, 0, i[5], 0)),
-            pl.BlockSpec((128, 128), lambda a, i: (i[6], 0)),
-        ),
-        aliases={4: 0, 5: 1},
+        near(halo, halo_table, cell, uv),
+        [VM] * 4,
+        (sds((16, 8 * NZ), f32), sds((2048, 128), f32)),
+        (VM, VM),
+        aliases={4: 1},
         flops=1 << 20,
         nbytes=1 << 20,
     )
@@ -492,89 +598,92 @@
         lax.all_to_all, axis_name="ang", split_axis=0, concat_axis=0, tiled=True, axis_index_groups=groups
     )
     received = lax.ppermute(uv[1024:], "ang", other)
-    chip_spec = pl.BlockSpec((1, 512, 128), lambda a, i: (i[3], 0, 0))
-    lines_spec = whole((1024, 128))
     UV, m = call(
         pair_kernel,
         idx,
-        (uv[:1024], received, t["chip"]),
-        [lines_spec, lines_spec, chip_spec],
+        near(uv[:1024], received, chip_table),
+        [VM] * 3,
         (lines, lines),
-        (lines_spec, lines_spec),
+        (VM, VM),
         flops=1 << 20,
         nbytes=2 << 20,
     )
     x = exchange(UV)
-    local = call(
+    field_spec = pl.BlockSpec((1, 4, 2, 64, NZ), lambda m, j, i: (m, 0, 0, j, 0))
+    w, ah, al, fwd, inv, mid = call(
         local_kernel,
         idx,
-        (f, t["cell"], t["ah"], t["al"]),
-        [
-            pl.BlockSpec((1, 4, 2, 64, NZ), lambda s, j, i: (s, 0, 0, j, 0)),
-            pl.BlockSpec((1, 64, 128), lambda s, j, i: (i[0], j, 0)),
-            whole((512, 512)),
-            whole((512, 512)),
-        ],
-        field,
-        pl.BlockSpec((1, 4, 2, 64, NZ), lambda s, j, i: (s, 0, 0, j, 0)),
+        (*far(f), *near(cell, corr), *stored[3:]),
+        [field_spec, VM, VM] + [ANY] * 5,
+        (field,) + targets[3:],
+        (field_spec,) + (VM,) * 5,
         grid=(2, 2),
+        scratch=(pltpu.VMEM((4, 2, 64, NZ), f32), pltpu.SemaphoreType.DMA((5,))),
         flops=3 << 30,
         nbytes=5 << 20,
     )
     mA = call(
         pair_axial_kernel,
         idx,
-        (m, t["chip"], t["ah"], t["al"]),
-        [lines_spec, chip_spec, whole((256, 512)), whole((256, 512))],
+        near(m, chip_table, ah, al),
+        [VM] * 4,
         lines,
-        lines_spec,
+        VM,
         flops=1 << 29,
         nbytes=2 << 20,
     )
     y = call(
         middle_kernel,
         idx,
-        (x, t["fwd"], t["inv"], t["mid"], t["ah"], t["al"]),
-        [
-            lines_spec,
-            whole((128, 768)),
-            whole((256, 384)),
-            pl.BlockSpec((1, 8, 128), lambda a, i: (i[4], 0, 0)),
-            whole((512, 512)),
-            whole((512, 512)),
-        ],
+        (*near(x, fwd, inv, mid, ah, al), *far(w), *near(mA)),
+        [VM] * 6 + [ANY, VM],
         lines,
-        lines_spec,
+        VM,
         flops=1 << 29,
         nbytes=3 << 20,
     )
     y = exchange(y)
-    keep, send = call(
+    near_half = (sds((2, 4, 2, 64, NZ), f32), sds((2, 4, 64, NZ), f32))
+    keep, send, w_own, cs_own = call(
         spread_kernel,
         idx,
-        (y, mA, t["chip"]),
-        [lines_spec, lines_spec, chip_spec],
-        (lines, lines),
-        (lines_spec, lines_spec),
+        (*near(y, mA, chip_table), *far(w, cs)),
+        [VM] * 3 + [ANY] * 2,
+        (lines, lines) + near_half,
+        (VM,) * 4,
+        scratch=(pltpu.SemaphoreType.DMA((3,)),),
         flops=1 << 20,
-        nbytes=2 << 20,
+        nbytes=5 << 20,
     )
     received = lax.ppermute(send, "ang", other)
+    size = 32
+
+    def out_spec(half):
+        return pl.BlockSpec(
+            (2, 2, 4, size, NZ), lambda a, i: (0, 0, 0, (i[1] ^ half) * (64 // size) + a, 0)
+        )
+
+    out, w_other, cs_other = call(
+        finish_own_kernel,
+        idx,
+        (*near(w_own, cs_own, keep, cell), *far(w, cs)),
+        [VM] * 4 + [ANY] * 2,
+        (pltpu.HBM(wave.shape, f32),) + near_half,
+        (out_spec(0), VM, VM),
+        grid=(64 // size,),
+        scratch=(pltpu.SemaphoreType.DMA((3,)),),
+        flops=1 << 22,
+        nbytes=6 << 20,
+    )
     return call(
-        finish_kernel,
-        idx,
-        (local, keep, received, cs, t["cell"]),
-        [
-            pl.BlockSpec((2, 4, 2, 32, NZ), lambda a, i: (0, 0, 0, a, 0)),
-            pl.BlockSpec((512, 128), lambda a, i: (a % 2, 0)),
-            pl.BlockSpec((512, 128), lambda a, i: (a % 2, 0)),
-            pl.BlockSpec((2, 4, 32, NZ), lambda a, i: (0, 0, a, 0)),
-            pl.BlockSpec((1, 32, 128), lambda a, i: (i[0], a, 0)),
-        ],
-        sds(wave.shape, f32),
-        pl.BlockSpec((2, 2, 4, 32, NZ), lambda a, i: (0, 0, 0, a, 0)),
-        grid=(4,),
-        scratch=(pltpu.VMEM((512, 128), f32),),
+        finish_other_kernel,
+        idx,
+        (*near(w_other, cs_other, received, cell), out),
+        [VM] * 4 + [ANY],
+        pltpu.HBM(wave.shape, f32),
+        out_spec(1),
+        grid=(64 // size,),
+        aliases={5: 0},
         flops=1 << 22,
         nbytes=6 << 20,
     )

time: 86.4 us -> 66.3 us (0.77)
  Pallas kernels: 36 us -> 27.5 us
  local copies, waits for them, and re-layouts: 6.81 us -> 0.07 us
  blocking collectives: 22 us -> 16.5 us
  starting transfers between devices: 11 us -> 16.5 us
  waiting for transfers between devices: 9.14 us -> 5.2 us
    pallas_call x8 -> x10, Pallas kernels: 36 us -> 27.5 us  [call(): pl.pallas_call(kernel, out_shape=out_shape, grid_spec=pltpu.PrefetchScala...]
    all_to_all x1, blocking collectives: 22 us -> 16.5 us  [body(): y = exchange(y)]
    all_to_all x1, starting transfers between devices: 4.75 us -> 10.2 us  [body(): x = exchange(UV)]
    all_to_all x1, waiting for transfers between devices: 7.6 us -> 3.66 us  [body(): x = exchange(UV)]
    unnamed x8 -> x0, local copies, waits for them, and re-layouts: 3.04 us -> none
    slice x1, local copies, waits for them, and re-layouts: 2.1 us -> 0.07 us  [body(): received = lax.ppermute(uv[1024:], 'ang', other)]
    dynamic_slice x1 -> x0, local copies, waits for them, and re-layouts: 0.91 us -> none  [body(): rim = lax.dynamic_slice_in_dim(wave, start, 8, axis=3).reshape(4, 4, 8, NZ)]
  transfers between devices with their start and end apart: 4 -> 4, of which waited for: 2 -> 2; matrix products, arithmetic and copies ran while one was open for 1% -> 0% of each run, Pallas kernels for 21% -> 28%
where the time goes in v2:
time: 66.3 us; the launch traced here: 65.9 us
  Pallas kernels  27.5 us (41%)
  starting transfers between devices  16.5 us (25%)
  blocking collectives  16.5 us (25%)
  waiting for transfers between devices  5.2 us (8%)
    pallas_call x10, Pallas kernels, call(): pl.pallas_call(kernel, out_shape=out_shape, grid_spec=pltpu.PrefetchScala...  27.5 us
    all_to_all x1, blocking collectives, body(): y = exchange(y)  16.5 us
    all_to_all x1, starting transfers between devices, body(): x = exchange(UV)  10.2 us
    all_to_all x1, waiting for transfers between devices, body(): x = exchange(UV)  3.66 us
    ppermute x1, starting transfers between devices, body(): received = lax.ppermute(send, 'ang', other)  3.02 us
    ppermute x1, starting transfers between devices, body(): halo = lax.ppermute(rim, 'rad', [(0, 1), (1, 0)])  2.19 us
    ppermute x1, waiting for transfers between devices, body(): received = lax.ppermute(uv[1024:], 'ang', other)  1.54 us
  transfers between devices with their start and end apart: 4, of which 2 were waited for; matrix products, arithmetic and copies ran while one was open for 0% of the time, Pallas kernels for 28%

profile of v2, /device:TPU:1, one launch (start us, length us, event | category | flops | bytes accessed | tf_op | source)
XLA Modules:
  0.0 65.9 jit_solution(7172877659209221433)
XLA Ops:
  0.0 1.5 %rim_kernel.1 = f32[16,2048]{1,0:T(8,128)S(1)} custom-call(s32[8]{0:T(128)S(1)} %compare_select_fusion.6.idx, f32[2,2,4,128,256]{4,3,2,1,0:T(8,128)} %w.3, f32[4,128,256]{2,1,0:T(8,128)} %pot.3), custom_call_target="tpu_custom_call" | custom-call | tf_op jit(solution)/shard_map/rim_kernel/pallas_call | solution.py:498
  1.5 2.2 %collective-permute-start = (f32[16,2048]{1,0:T(8,128)S(1)}, f32[16,2048]{1,0:T(8,128)S(1)}, u32[]{:S(2)}, u32[]{:S(2)}) collective-permute-start(f32[16,2048]{1,0:T(8,128)S(1)} %rim_kernel.1), channel_id=1, source_target_pairs={{0,1},{1,0},{2,3},{3,2},{4,5},{5,4},{6,7},{7,6},{8,9},{9,8},{10,11... | collective-permute-start | bytes 393224 | tf_op jit(solution)/shard_map/ppermute | solution.py:555
  3.7 7.2 %advance_kernel.1 = (f32[2,4,2,128,256]{4,3,2,1,0:T(8,128)}, f32[2,4,128,256]{3,2,1,0:T(8,128)}, f32[2048,128]{1,0:T(8,128)S(1)}, f32[2,16,16]{2,1,0:T(8,128)S(1...) custom-call(s32[8]{0:T(128)S(1)} %compare_select_fusion.6.idx, f32[2,2,4,128,256]{4,3,2,1,0:T(8,128)} %w.3, ...), custom_call_target="tpu_custom_call" | custom-call | flops 1073741824 | bytes 5242880 | tf_op jit(solution)/shard_map/advance_kernel/pallas_call | solution.py:498
  11.0 0.0 collective-permute-done.halo
  11.0 0.9 %halo_kernel.1 = (f32[16,2048]{1,0:T(8,128)S(1)}, f32[2048,128]{1,0:T(8,128)S(1)}) custom-call(s32[8]{0:T(128)S(1)} %compare_select_fusion.6.idx, f32[16,2048]{1,0:T(8,128)S(1)} %collective-permute-done.halo, f32[2,16,16]{2,1,0:T(8,128)S(1)} %get-tuple-element.28.table, f32[128,128]{1,0:T(8,128)S(1)} %get-tuple-element.29.coef, ...), custom_call_target="tpu_custom_call", output_to_operand_aliasing={{1}: (4, {})} | custom-call | flops 1048576 | bytes 1048576 | tf_op jit(solution)/shard_map/halo_kernel/pallas_call | solution.py:498
  11.9 0.1 fusion
  12.0 1.0 %collective-permute-start.1 = (f32[1024,128]{1,0:T(8,128)S(1)}, f32[1024,128]{1,0:T(8,128)S(1)}, u32[]{:S(2)}, u32[]{:S(2)}) collective-permute-start(f32[1024,128]{1,0:T(8,128)S(1)} %get-tuple-element.51), channel_id=1, source_target_pairs={{0,2},{2,0},{4,6},{6,4},{8,10},{10,8},{12,14},{14,12},{16,18},{18,... | collective-permute-start | bytes 1572872 | tf_op jit(solution)/shard_map/ppermute | solution.py:600
  13.0 1.5 %collective-permute-done.1.received = f32[1024,128]{1,0:T(8,128)S(1)} collective-permute-done((f32[1024,128]{1,0:T(8,128)S(1)}, f32[1024,128]{1,0:T(8,128)S(1)}, u32[]{:S(2)}, u32[]{:S(2)}) %collective-permute-start.1) | collective-permute-done | bytes 524320 | tf_op jit(solution)/shard_map/ppermute | solution.py:600
  14.6 1.6 %pair_kernel.1 = (f32[1024,128]{1,0:T(8,128)}, f32[1024,128]{1,0:T(8,128)S(1)}) custom-call(s32[8]{0:T(128)S(1)} %compare_select_fusion.6.idx, f32[1024,128]{1,0:T(8,128)S(1)} %get-tuple-element.52.own, f32[1024,128]{1,0:T(8,128)S(1)} %collective-permute-done.1.received, f32[512,128]{1,0:T(8,128)S(1)} %get-tuple-element.32.chip), custom_call_target="tpu_custom_call" | custom-call | flops 1048576 | bytes 2097152 | tf_op jit(solution)/shard_map/pair_kernel/pallas_call | solution.py:498
  16.1 10.2 %all-to-all-start = ((f32[32,32,128]{2,1,0:T(8,128)}), f32[32,32,128]{2,1,0:T(8,128)S(1)}, u32[]{:S(2)}, u32[]{:S(2)}) async-start(f32[32,32,128]{2,1,0:T(8,128)} %bitcast), calls=%async_computation | async-start | bytes 1048576 | tf_op jit(solution)/shard_map/all_to_all | solution.py:611
  26.4 6.9 %local_kernel.1 = (f32[2,4,2,128,256]{4,3,2,1,0:T(8,128)}, bf16[3,256,256]{2,1,0:T(8,128)(2,1)S(1)}, bf16[3,256,256]{2,1,0:T(8,128)(2,1)S(1)}, bf16[128,768]{1,0...) custom-call(s32[8]{0:T(128)S(1)} %compare_select_fusion.6.idx, ...), custom_call_target="tpu_custom_call" | custom-call | flops 3221225472 | bytes 5242880 | tf_op jit(solution)/shard_map/local_kernel/pallas_call | solution.py:498
  33.2 1.1 %pair_axial_kernel.1.after_too.mA = f32[1024,128]{1,0:T(8,128)S(1)} custom-call(s32[8]{0:T(128)S(1)} %compare_select_fusion.6.idx, f32[1024,128]{1,0:T(8,128)S(1)} %get-tuple-element.42.m, f32[512,128]{1,0:T(8,128)S(1)} %get-tuple-element.32.chip, bf16[3,256,256]{2,1,0:T(8,128)(2,1)S(1)} %get-tuple-element.39.ah, bf16[3,256,256]{2,1,0:T(8,128)(2,1)S(1)} %get-tuple-element.40.al), custom_call_target="tpu_custom_call" | custom-call | flops 536870912 | bytes 2097152 | tf_op jit(solution)/shard_map/pair_axial_kernel/pallas_call | solution.py:498
  34.4 3.7 %all-to-all-done = f32[32,32,128]{2,1,0:T(8,128)S(1)} async-done(((f32[32,32,128]{2,1,0:T(8,128)}), f32[32,32,128]{2,1,0:T(8,128)S(1)}, u32[]{:S(2)}, u32[]{:S(2)}) %all-to-all-start) | async-done | bytes 524320 | tf_op jit(solution)/shard_map/all_to_all | solution.py:611
  38.0 1.5 %middle_kernel.1 = f32[1024,128]{1,0:T(8,128)S(1)} custom-call(s32[8]{0:T(128)S(1)} %compare_select_fusion.6.idx, f32[1024,128]{1,0:T(8,128)S(1)} %bitcast.4, bf16[128,768]{1,0:T(8,128)(2,1)S(1)} %get-tuple-element.36.fwd, bf16[256,384]{1,0:T(8,128)(2,1)S(1)} %get-tuple-element.37.inv, f32[8,128]{1,0:T(8,128)S(1)} %get-tuple-element.38.mid, ...), custom_call_target="tpu_custom_call" | custom-call | flops 536870912 | bytes 3145728 | tf_op jit(solution)/shard_map/middle_kernel/pallas_call | solution.py:498
  39.5 16.5 %all_to_all.22 = f32[32,32,128]{2,1,0:T(8,128)S(1)} all-to-all(f32[32,32,128]{2,1,0:T(8,128)S(1)} %bitcast.6), channel_id=1, replica_groups={{0,4,8,12,16,20,24,28,32,36,40,44,48,52,56,60,64,68,72,76,80,84,88,92,9..., dimensions={0} | all-to-all | bytes 1048576 | tf_op jit(solution)/shard_map/all_to_all | solution.py:645
  56.0 1.9 %spread_kernel.1 = (f32[1024,128]{1,0:T(8,128)S(1)}, f32[1024,128]{1,0:T(8,128)S(1)}, f32[2,4,2,64,256]{4,3,2,1,0:T(8,128)S(1)}, f32[2,4,64,256]{3,2,1,0:T(8,128)S(1)}) custom-call(s32[8]{0:T(128)S(1)} %compare_select_fusion.6.idx, f32[1024,128]{1,0:T(8,128)S(1)} %bitcast.5, f32[1024,128]{1,0:T(8,128)S(1)} %pair_axial_kernel.1.after_too.mA, ...), custom_call_target="tpu_custom_call" | custom-call | flops 1048576 | bytes 5242880 | tf_op jit(solution)/shard_map/spread_kernel/pallas_call | solution.py:498
  58.0 3.0 %collective-permute-start.2 = (f32[1024,128]{1,0:T(8,128)S(1)}, f32[1024,128]{1,0:T(8,128)S(1)}, u32[]{:S(2)}, u32[]{:S(2)}) collective-permute-start(f32[1024,128]{1,0:T(8,128)S(1)} %get-tuple-element.49), channel_id=1, source_target_pairs={{0,2},{2,0},{4,6},{6,4},{8,10},{10,8},{12,14},{14,12},{16,18},{18,... | collective-permute-start | bytes 1572872 | tf_op jit(solution)/shard_map/ppermute | solution.py:658
  61.0 3.0 %finish_own_kernel.1 = (f32[2,2,4,128,256]{4,3,2,1,0:T(8,128)}, f32[2,4,2,64,256]{4,3,2,1,0:T(8,128)S(1)}, f32[2,4,64,256]{3,2,1,0:T(8,128)S(1)}) custom-call(s32[8]{0:T(128)S(1)} %compare_select_fusion.6.idx, f32[2,4,2,64,256]{4,3,2,1,0:T(8,128)S(1)} %get-tuple-element.44.w, f32[2,4,64,256]{3,2,1,0:T(8,128)S(1)} %get-tuple-element.45.cs, ...), custom_call_target="tpu_custom_call" | custom-call | flops 4194304 | bytes 6291456 | tf_op jit(solution)/shard_map/finish_own_kernel/pallas_call | solution.py:498
  64.0 0.0 collective-permute-done.2.y
  64.1 1.8 %finish_other_kernel.1 = f32[2,2,4,128,256]{4,3,2,1,0:T(8,128)} custom-call(s32[8]{0:T(128)S(1)} %compare_select_fusion.6.idx, f32[2,4,2,64,256]{4,3,2,1,0:T(8,128)S(1)} %get-tuple-element.47.w, f32[2,4,64,256]{3,2,1,0:T(8,128)S(1)} %get-tuple-element.48.cs, f32[1024,128]{1,0:T(8,128)S(1)} %collective-permute-done.2.y, ...), custom_call_target="tpu_custom_call", output_to_operand_aliasing={{}: (5, {})} | custom-call | flops 4194304 | bytes 6291456 | tf_op jit(solution)/shard_map/finish_other_kernel/pallas_call | solution.py:498
  (1 shorter events, 0.0 us)
Async XLA Ops:
  1.5 9.5 %collective-permute-start = (f32[16,2048]{1,0:T(8,128)S(1)}, f32[16,2048]{1,0:T(8,128)S(1)}, u32[]{:S(2)}, u32[]{:S(2)}) collective-permute-start(f32[16,2048]{1,0:T(8,128)S(1)} %rim_kernel.1), channel_id=1, source_target_pairs={{0,1},{1,0},{2,3},{3,2},{4,5},{5,4},{6,7},{7,6},{8,9},{9,8},{10,11... | collective-permute-start | bytes 393224 | tf_op jit(solution)/shard_map/ppermute | solution.py:555
  12.0 2.6 %collective-permute-start.1 = (f32[1024,128]{1,0:T(8,128)S(1)}, f32[1024,128]{1,0:T(8,128)S(1)}, u32[]{:S(2)}, u32[]{:S(2)}) collective-permute-start(f32[1024,128]{1,0:T(8,128)S(1)} %get-tuple-element.51), channel_id=1, source_target_pairs={{0,2},{2,0},{4,6},{6,4},{8,10},{10,8},{12,14},{14,12},{16,18},{18,... | collective-permute-start | bytes 1572872 | tf_op jit(solution)/shard_map/ppermute | solution.py:600
  16.1 21.9 %all-to-all-start = ((f32[32,32,128]{2,1,0:T(8,128)}), f32[32,32,128]{2,1,0:T(8,128)S(1)}, u32[]{:S(2)}, u32[]{:S(2)}) async-start(f32[32,32,128]{2,1,0:T(8,128)} %bitcast), calls=%async_computation | async-start | bytes 1048576 | tf_op jit(solution)/shard_map/all_to_all | solution.py:611
  58.0 6.1 %collective-permute-start.2 = (f32[1024,128]{1,0:T(8,128)S(1)}, f32[1024,128]{1,0:T(8,128)S(1)}, u32[]{:S(2)}, u32[]{:S(2)}) collective-permute-start(f32[1024,128]{1,0:T(8,128)S(1)} %get-tuple-element.49), channel_id=1, source_target_pairs={{0,2},{2,0},{4,6},{6,4},{8,10},{10,8},{12,14},{14,12},{16,18},{18,... | collective-permute-start | bytes 1572872 | tf_op jit(solution)/shard_map/ppermute | solution.py:658

commit v3 on v2

v3 whole, which is shorter than its diff:
```python
import functools

import jax
import jax.numpy as jnp
import numpy as np
from jax import lax
from jax.experimental import pallas as pl
from jax.experimental.pallas import tpu as pltpu
from jax.sharding import PartitionSpec as P

NA = 256
NR = 256
NZ = 256
CHIPS = 32
LR = 128
f32 = jnp.float32
bf16 = jnp.bfloat16
UNROLL = 2


def split(a):
    hi = np.asarray(a, np.float32).astype(jnp.bfloat16)
    lo = (np.asarray(a, np.float64) - hi.astype(np.float64)).astype(np.float32)
    return hi, lo.astype(jnp.bfloat16)


def coefficients():
    j = np.arange(NR, dtype=np.float32)
    radius = np.float32(1.0) + np.float32(9.0) * (j + np.float32(0.5)) / np.float32(NR)
    return (np.float32(100000.0) / (radius * radius)).astype(np.float64)


def radial_tables():
    lap = np.zeros((NR, NR))
    for d, c in ((0, -30.0), (1, 16.0), (2, -1.0)):
        for j in range(NR - d):
            lap[j, j + d] = c / 12.0
            lap[j + d, j] = c / 12.0
    k = 0.25 * lap
    even = np.eye(NR) - k @ k / 2.0
    odd = -k + k @ k @ k / 6.0
    main, halo = [], []
    for side in range(2):
        own = slice(LR * side, LR * side + LR)
        a, b = even[own, own], odd[own, own]
        hi, lo = split(np.block([[a, -b], [b, a]]))
        main.append(np.concatenate([hi, hi, lo], axis=1))
        rows = slice(120, 128) if side == 0 else slice(128, 136)
        cols = slice(128, 136) if side == 0 else slice(120, 128)
        a, b = even[rows, cols], odd[rows, cols]
        halo.append(np.block([[a, -b], [b, a]]))
    return np.stack(main), np.stack(halo).astype(np.float32)


def axial_tables():
    n = np.arange(1, NZ + 1)
    sine = np.sqrt(2.0 / (NZ + 1)) * np.sin(np.pi * (n[:, None] * n[None, :]) / (NZ + 1))
    s = 1.5 * (2.0 - 2.0 * np.cos(np.pi * n / (NZ + 1)))
    gain = (1.0 - 1j * s) / (1.0 + 1j * s)
    full = (sine * gain[None, :]) @ sine
    re, im = full.real, full.imag
    return split(np.stack([re, im - re, re + im]))


def dirichlet(c, size):
    off = 0.1 - 1j * c
    mat = np.zeros((size, size), complex)
    for t in range(size):
        mat[t, t] = 1.0 + 2j * c
        if t:
            mat[t, t - 1] = off
            mat[t - 1, t] = off
    inv = np.linalg.inv(mat)
    return inv, -off * inv[:, 0]


def angle_tables():
    cell = np.zeros((2, LR, 128), np.float32)
    chip = np.zeros((2, 2, 4, 64, 1, 128), np.float32)
    mid = np.zeros((2, 2, 32, 1, 128), np.float32)
    angle = np.arange(NA)
    second = 2.0 * np.cos(2.0 * np.pi * angle / NA) - 2.0
    for g, c in enumerate(coefficients()):
        rho = 0.1 / (0.1 - 1j * c)
        scale = 2.4 * (1.0 - rho)
        inv, p = dirichlet(c, 3)
        w0 = 2.0 * rho - 1.0
        values = [
            (p[0] + p[2]) / 2,
            (p[0] - p[2]) / 2,
            p[1],
            w0,
            (w0 + scale * (inv[0, 0] + inv[0, 2])) / 2,
            (w0 + scale * (inv[0, 0] - inv[0, 2])) / 2,
            scale * inv[0, 1],
            w0 + scale * inv[1, 1],
        ]
        side, j = divmod(g, LR)
        for k, value in enumerate(values):
            cell[side, j, 2 * k] = value.real
            cell[side, j, 2 * k + 1] = value.imag
        inv8, p8 = dirichlet(c, 7)
        core, jj = divmod(j, 64)
        middle, local = p8[3], scale * inv8[3, 3]
        for k, value in enumerate((middle.real, middle.imag, local.real, local.imag)):
            chip[side, core, k, jj] = value
        symbol = 1.0 / (1.2 + (0.1 - 1j * c) * second)
        coarse = scale * symbol.reshape(8, CHIPS).sum(0) / 8.0
        pos, r = divmod(jj, 2)
        mid[side, core, pos, 0, 64 * r : 64 * r + 32] = coarse.real
        mid[side, core, pos, 0, 64 * r + 32 : 64 * r + 64] = coarse.imag
    return cell, chip.reshape(4, 4, 64, 1, 128), mid.reshape(128, 1, 128)


def fourier_tables():
    k = np.arange(CHIPS)
    q = np.arange(CHIPS)
    fwd = np.zeros((2, 2, CHIPS, CHIPS, 2, 2, 2))
    inv = np.zeros((CHIPS, 2, 2, 2, 2, 2, CHIPS))
    for n in range(2):
        phase = -2.0 * np.pi * ((k[:, None] * (q[None, :] + n)) % CHIPS) / CHIPS
        e = np.exp(1j * phase)
        for s in range(2):
            fwd[0, s, :, :, n, 0, s] = e.real
            fwd[0, s, :, :, n, 1, s] = -e.imag
            fwd[1, s, :, :, n, 0, s] = e.imag
            fwd[1, s, :, :, n, 1, s] = e.real
            d = np.conj(e).T / CHIPS
            inv[:, n, 0, s, 0, s, :] = d.real
            inv[:, n, 0, s, 1, s, :] = -d.imag
            inv[:, n, 1, s, 0, s, :] = d.imag
            inv[:, n, 1, s, 1, s, :] = d.real
    fwd = fwd.reshape(128, 256)
    inv = inv.reshape(256, 128)
    fh, fl = split(fwd)
    ih, il = split(inv)
    return np.stack([fh, fl]), np.stack([ih, il])


@functools.cache
def tables():
    main, halo = radial_tables()
    ah, al = axial_tables()
    cell, chip, mid = angle_tables()
    fwd, inv = fourier_tables()
    return dict(main=main, halo=halo, ah=ah, al=al, cell=cell, chip=chip, mid=mid, fwd=fwd, inv=inv)


def dot(a, b):
    return jnp.dot(a, b, preferred_element_type=f32)


def halves(x):
    hi = x.astype(bf16)
    return hi, (x - hi.astype(f32)).astype(bf16)


def stacked(x):
    hi, lo = halves(x)
    return jnp.concatenate([hi, lo, hi], axis=0)


def times(x, high, low):
    hi, lo = halves(x)
    rows = x.shape[0]
    both = dot(jnp.concatenate([hi, lo], axis=0), high[...])
    return both[:rows] + both[rows:] + dot(hi, low[...])


def apply(table, x):
    hi, lo = halves(x)
    rows = table.shape[1]
    both = dot(table[...].reshape(2 * rows, table.shape[2]), hi)
    return both[:rows] + both[rows:] + dot(table[0], lo)


def complex_times(re, im, high, low):
    p, q, r = [times(x, high.at[i], low.at[i]) for i, x in enumerate((re + im, re, im))]
    return p - r, p + q


SIN = (-0.16666657119790096, 0.008333017866982043, -0.00019806657092710876, 2.600148052222563e-06)
COS = (
    -0.4999999955093015,
    0.041666640791225444,
    -0.0013888404392796263,
    2.476193429595472e-05,
    -2.607799377413178e-07,
)


def cos_sin(x):
    y = 0.5 * x
    q = y * y
    a = jnp.full_like(q, SIN[-1])
    for c in SIN[-2::-1]:
        a = a * q + c
    b = jnp.full_like(q, COS[-1])
    for c in COS[-2::-1]:
        b = b * q + c
    s = y + y * (q * a)
    c = 1.0 + q * b
    s2 = s + s
    return 1.0 - s2 * s, s2 * c


def cmul(cr, ci, x):
    return (cr * x[0] - ci * x[1], cr * x[1] + ci * x[0])


def add(x, y):
    return (x[0] + y[0], x[1] + y[1])


def sub(x, y):
    return (x[0] - y[0], x[1] - y[1])


def weights(coef, k, width):
    shape = (coef.shape[0], width)
    return tuple(jnp.broadcast_to(coef[:, i : i + 1], shape) for i in (2 * k, 2 * k + 1))


def reduce_cells(f, coef):
    width = f[0][0].shape[-1]
    s, d = add(f[1], f[3]), sub(f[1], f[3])
    even = add(cmul(*weights(coef, 0, width), s), cmul(*weights(coef, 2, width), f[2]))
    odd = cmul(*weights(coef, 1, width), d)
    return add(add(f[0], even), odd), sub(even, odd)


def advance_kernel(idx, w, pot, main, *refs):
    sources, (f_out, cs_out, uv), targets = refs[:8], refs[8:11], refs[11:19]
    w_in, pot_in, main_in, f, cs, sems, in_sems, out_sems = refs[19:]
    own = {1: idx[3], 2: idx[0], 7: idx[4]}
    copies = [
        pltpu.make_async_copy(x.at[own[i]] if i in own else x, y, sems.at[i])
        for i, (x, y) in enumerate(zip(sources, targets))
    ]
    fetch_main = pltpu.make_async_copy(main.at[idx[0]], main_in, in_sems.at[8])
    fetches = [
        (
            pltpu.make_async_copy(pot.at[t], pot_in.at[t], in_sems.at[t]),
            pltpu.make_async_copy(w.at[:, :, t], w_in.at[:, :, t], in_sems.at[4 + t]),
        )
        for t in range(4)
    ]
    leaving = []
    for copy in fetches[0]:
        copy.start()
    fetch_main.start()
    for pair in fetches[1:]:
        for copy in pair:
            copy.start()
    for copy in copies:
        copy.start()
    for t in range(4):
        fetches[t][0].wait()
        c, s = cos_sin(pot_in[t])
        cs[0, t] = c
        cs[1, t] = s
        fetches[t][1].wait()
        if t == 0:
            fetch_main.wait()
        for m in range(2):
            re, im = w_in[0, m, t], w_in[1, m, t]
            x = jnp.concatenate([c * re + s * im, c * im - s * re], axis=0)
            f[m, t] = dot(main_in[...], stacked(x)).reshape(2, LR, NZ)
        for j in range(2):
            rows = pl.ds(64 * j, 64)
            for m in range(2):
                leaving.append((f.at[m, t, :, rows, :], f_out.at[m, j, t]))
            leaving.append((cs.at[:, t, rows, :], cs_out.at[j, :, t]))
        first = len(leaving) - 6
        for i in range(6):
            leaving[first + i] = pltpu.make_async_copy(*leaving[first + i], out_sems.at[first + i])
            leaving[first + i].start()
    for copy in copies:
        copy.wait()
    coef = targets[2]

    def block(b, carry):
        rows = pl.ds(pl.multiple_of(b * 8, 8), 8)
        base = (lax.shift_right_logical(b, 3) ^ idx[1]) * 1024 + (b & 7) * 128
        k = coef[rows, :]
        for m in range(2):
            u, v = reduce_cells([(f[m, t, 0, rows, :], f[m, t, 1, rows, :]) for t in range(4)], k)
            for i, value in enumerate((u[0], u[1], v[0], v[1])):
                for z in range(2):
                    uv[pl.ds(base + 8 * z + 2 * i + m, 8, stride=16), :] = value[:, 128 * z : 128 * z + 128]
        return carry

    lax.fori_loop(0, 16, block, 0, unroll=UNROLL)
    for copy in leaving:
        copy.wait()


def rim_kernel(idx, w, pot, out):
    for t in range(4):
        c, s = cos_sin(pot[t])
        for m in range(2):
            re, im = w[0, m, t], w[1, m, t]
            x = jnp.concatenate([c * re + s * im, c * im - s * re], axis=0)
            out[:, (2 * t + m) * NZ : (2 * t + m + 1) * NZ] = x


def halo_part(table, halo):
    return jnp.dot(table, halo, precision=lax.Precision.HIGHEST, preferred_element_type=f32)


def halo_kernel(idx, halo, table, coef, uv_in, uv):
    edge_uv = idx[6] * 128
    out = halo_part(table[idx[0]], halo[...])
    k = coef[pl.ds(pl.multiple_of(idx[5] * 8, 8), 8), :]
    for m in range(2):
        cells = []
        for t in range(4):
            piece = out[:, (2 * t + m) * NZ : (2 * t + m + 1) * NZ]
            cells.append((piece[:8], piece[8:]))
        u, v = reduce_cells(cells, k)
        for i, value in enumerate((u[0], u[1], v[0], v[1])):
            for z in range(2):
                line = pl.ds(edge_uv + 8 * z + 2 * i + m, 8, stride=16)
                uv[line, :] = uv_in[line, :] + value[:, 128 * z : 128 * z + 128]


def row_swap(x, shift):
    return pltpu.roll(x, shift, 2)


def first_rows(core, shape):
    row = lax.broadcasted_iota(jnp.int32, shape, 2)
    return (lax.shift_right_logical(row, 2) ^ core) == 0


def tiles(x):
    return x.reshape(x.shape[0] // 16, 2, 8, 128)


def wide(x):
    x = tiles(x)
    rows = 8 * x.shape[0]
    return jnp.concatenate([x[:, z].reshape(rows, 128) for z in range(2)], axis=1)


def narrow(x):
    rows = x.shape[0] // 8
    return jnp.stack([x[:, 128 * z : 128 * z + 128].reshape(rows, 8, 128) for z in range(2)], axis=1)


def row_times(chip, k, x):
    shape = (64, 1, 8, 128)
    re = jnp.broadcast_to(chip[k].reshape(64, 1, 1, 128), shape)
    im = jnp.broadcast_to(chip[k + 1].reshape(64, 1, 1, 128), shape) * part_sign()
    return re * x + im * row_swap(x, 2)


def part_sign():
    row = lax.broadcasted_iota(jnp.int32, (1, 1, 8, 128), 2)
    return jnp.where((row & 2) == 0, -1.0, 1.0)


def pair_kernel(idx, own, received, chip, uv, m_out):
    a, b = tiles(own[...]), tiles(received[...])
    mask = first_rows(idx[1], a.shape)
    ends = jnp.where(mask, a, b)
    inner = jnp.where(mask, b, a)
    inner = inner + row_swap(inner, 4)
    low = first_rows(0, (1, 1, 8, 128))
    m_out[...] = jnp.where(low, inner[:32], inner[32:]).reshape(512, 128)
    uv[...] = (ends + row_times(chip, 0, inner)).reshape(uv.shape)


def local_kernel(idx, f, halo_far, m_rows, *refs):
    sources, after, out, mA = refs[:5], refs[5], refs[6], refs[7]
    chip, cell, chip_local, ah, al, halo, halo_table, g, sems = refs[8:]
    tables = [
        pltpu.make_async_copy(sources[0].at[idx[0]], cell, sems.at[4]),
        pltpu.make_async_copy(sources[1].at[idx[3], pl.ds(0, 2)], chip, sems.at[5]),
        pltpu.make_async_copy(sources[1].at[idx[3], pl.ds(2, 2)], chip_local, sems.at[10]),
        pltpu.make_async_copy(sources[2], ah, sems.at[6]),
        pltpu.make_async_copy(sources[3], al, sems.at[7]),
        pltpu.make_async_copy(sources[4], halo_table, sems.at[8]),
        pltpu.make_async_copy(halo_far, halo, sems.at[9]),
    ]
    copies = [pltpu.make_async_copy(f.at[m, j], g.at[m, j], sems.at[2 * m + j]) for m in range(2) for j in range(2)]
    for copy in tables + copies:
        copy.start()
    for copy in tables:
        copy.wait()

    halo[...] = halo_part(halo_table[idx[0]], halo[...])

    x = wide(m_rows[...])
    a = times(x, ah.at[0], al.at[0])
    b = a + times(x, ah.at[1], al.at[1])
    b = narrow(b)
    b = jnp.where(part_sign() < 0, -row_swap(b, 6), row_swap(b, 2))
    x = narrow(a) + b
    other, low = row_swap(x, 4), first_rows(0, (1, 1, 8, 128))
    x = jnp.concatenate([jnp.where(low, x, other), jnp.where(low, other, x)], axis=0)
    mA[...] = row_times(chip_local, 0, x).reshape(mA.shape)

    for m in range(2):
        for j in range(2):
            copies[2 * m + j].wait()

            @pl.when(idx[0] == 1 - j)
            def _():
                row = 56 * j
                for t in range(4):
                    at = slice((2 * t + m) * NZ, (2 * t + m + 1) * NZ)
                    for c in range(2):
                        g[m, j, t, c, row : row + 8, :] += halo[8 * c : 8 * c + 8, at]

            k = cell[64 * j : 64 * j + 64, :]
            cells = [(g[m, j, t, 0], g[m, j, t, 1]) for t in range(4)]
            s, d = add(cells[1], cells[3]), sub(cells[1], cells[3])
            even = add(cmul(*weights(k, 4, NZ), s), cmul(*weights(k, 6, NZ), cells[2]))
            odd = cmul(*weights(k, 5, NZ), d)
            parts = [
                cmul(*weights(k, 3, NZ), cells[0]),
                add(even, odd),
                add(cmul(*weights(k, 6, NZ), s), cmul(*weights(k, 7, NZ), cells[2])),
                sub(even, odd),
            ]
            re = jnp.concatenate([p[0] for p in parts], axis=0)
            im = jnp.concatenate([p[1] for p in parts], axis=0)
            re, im = complex_times(re, im, ah, al)
            for t in range(4):
                out[m, t, 0, 64 * j : 64 * j + 64, :] = re[t * 64 : (t + 1) * 64]
                out[m, t, 1, 64 * j : 64 * j + 64, :] = im[t * 64 : (t + 1) * 64]


def middle_kernel(idx, x, fwd, inv, mid, ah, al, out, y, sems):
    x = x[...].reshape(CHIPS, 4, 8, 128)
    x = jnp.concatenate([x[:, i].reshape(256, 128) for i in range(4)], axis=1)
    g = apply(fwd, x)
    k = jnp.broadcast_to(mid[...], (8, 128)).T
    rows = []
    for r in range(2):
        col = slice(r * NZ, (r + 1) * NZ)
        kr, ki = [
            jnp.concatenate([jnp.broadcast_to(k[64 * r + 32 * c : 64 * r + 32 * c + 32, 0:1], (32, NZ))] * 2, axis=0)
            for c in range(2)
        ]
        rows.append(cmul(kr, ki, (g[:64, col], g[64:, col])))
    re, im = complex_times(*[jnp.concatenate([p[c] for p in rows], axis=0) for c in range(2)], ah, al)
    copies = []
    for r in range(2):
        h = jnp.concatenate([x[64 * r : 64 * r + 64] for x in (re, im)], axis=0)
        part = apply(inv, h)
        for z in range(2):
            y[:, 2 * r + z] = part[:, 128 * z : 128 * z + 128].reshape(CHIPS, 8, 128)
        lines = pl.ds(2 * r, 2)
        copies.append(pltpu.make_async_copy(y.at[:, lines], out.at[:, lines], sems.at[r]))
        copies[-1].start()
    for copy in copies:
        copy.wait()


def fetch(row, cs, cs_out, sem):
    return pltpu.make_async_copy(cs.at[row], cs_out, sem)


def spread_kernel(idx, y, mA, chip, after, cs, cell_far, keep, send, cs_own, cs_other, cell, sems):
    copies = [fetch(idx[1] ^ i, cs, x, sems.at[i]) for i, x in enumerate((cs_own, cs_other))]
    copies.append(pltpu.make_async_copy(cell_far.at[idx[0]], cell, sems.at[2]))
    for copy in copies:
        copy.start()
    x = tiles(y[...])
    total = x + row_swap(x, 4)
    inner = row_times(chip, 0, total) + tiles(mA[...])
    mask = first_rows(idx[1], x.shape)
    keep[...] = jnp.where(mask, x, inner).reshape(keep.shape)
    send[...] = jnp.where(mask, inner, x).reshape(keep.shape)
    for copy in copies:
        copy.wait()


CHUNK = 16


def finish_kernel(half, idx, w, cs, y, coef, out, o, sems):
    place = (idx[1] ^ half) * 64

    def leave(n):
        rows = pl.ds(pl.multiple_of(n * CHUNK, CHUNK), CHUNK)
        there = pl.ds(pl.multiple_of(place + n * CHUNK, CHUNK), CHUNK)
        return pltpu.make_async_copy(o.at[:, :, :, rows, :], out.at[:, :, :, there, :], sems.at[n])

    for n in range(64 // CHUNK):
        here = slice(n * CHUNK, (n + 1) * CHUNK)
        there = pl.ds(pl.multiple_of(place + n * CHUNK, CHUNK), CHUNK)
        k = coef[there, :]
        for m in range(2):
            a = [
                jnp.concatenate(
                    [y[pl.ds(n * CHUNK * 16 + 8 * z + 2 * i + m, CHUNK, stride=16), :] for z in range(2)], axis=1
                )
                for i in range(4)
            ]
            left, right = (a[0], a[1]), (a[2], a[3])
            s, d = add(left, right), sub(left, right)
            even = cmul(*weights(k, 0, NZ), s)
            odd = cmul(*weights(k, 1, NZ), d)
            parts = [left, add(even, odd), cmul(*weights(k, 2, NZ), s), sub(even, odd)]
            for t in range(4):
                re, im = w[m, t, 0, there, :] + parts[t][0], w[m, t, 1, there, :] + parts[t][1]
                c, sn = cs[0, t, here, :], cs[1, t, here, :]
                o[0, m, t, here, :] = c * re + sn * im
                o[1, m, t, here, :] = c * im - sn * re
        leave(n).start()
    for n in range(64 // CHUNK):
        leave(n).wait()


def finish_own_kernel(idx, w, cs, y, coef, out, o, sems):
    finish_kernel(0, idx, w, cs, y, coef, out, o, sems)


def finish_other_kernel(idx, w, cs, y, coef, before, out, o, sems):
    finish_kernel(1, idx, w, cs, y, coef, out, o, sems)


def call(kernel, idx, args, in_specs, out_shape, out_specs, grid=(1,), scratch=(), aliases=None, flops=0, nbytes=0):
    return pl.pallas_call(
        kernel,
        out_shape=out_shape,
        grid_spec=pltpu.PrefetchScalarGridSpec(
            num_scalar_prefetch=1, grid=grid, in_specs=in_specs, out_specs=out_specs, scratch_shapes=scratch
        ),
        input_output_aliases=aliases or {},
        compiler_params=pltpu.CompilerParams(
            dimension_semantics=("arbitrary",) * len(grid), vmem_limit_bytes=24 << 20
        ),
        cost_estimate=pl.CostEstimate(flops=flops, bytes_accessed=nbytes, transcendentals=0),
        name=kernel.__name__,
    )(idx, *args)


def whole(shape):
    return pl.BlockSpec(shape, lambda *_: (0,) * len(shape))


VM = pl.BlockSpec(memory_space=pltpu.VMEM)
ANY = pl.BlockSpec(memory_space=pl.ANY)


def near(*arrays):
    return tuple(pltpu.with_memory_space_constraint(x, pltpu.VMEM) for x in arrays)


def far(*arrays):
    return tuple(pltpu.with_memory_space_constraint(x, pltpu.HBM) for x in arrays)


def body(wave, potential):
    t = tables()
    rad = lax.axis_index("rad")
    ang = lax.axis_index("ang")
    core = ang % 2
    chip = ang // 2
    lane = jnp.arange(8, dtype=jnp.int32)
    edge = jnp.where(rad == 0, 15, 0)
    edge_uv = ((edge // 8) ^ core) * 8 + edge % 8
    idx = jnp.zeros(8, jnp.int32)
    for i, v in enumerate((rad, core, chip, rad * 2 + core, rad * 64 + core * 32 + chip, edge, edge_uv)):
        idx = jnp.where(lane == i, v.astype(jnp.int32), idx)

    sds = pltpu.VMEM
    wave, potential = far(wave, potential)
    rim = call(
        rim_kernel,
        idx,
        (wave, potential),
        [
            pl.BlockSpec((2, 2, 4, 8, NZ), lambda a, i: (0, 0, 0, i[5], 0)),
            pl.BlockSpec((4, 8, NZ), lambda a, i: (0, i[5], 0)),
        ],
        sds((16, 8 * NZ), f32),
        VM,
    )
    halo = lax.ppermute(rim, "rad", [(0, 1), (1, 0)])
    field = pltpu.HBM((2, 4, 2, LR, NZ), f32)
    lines = sds((1024, 128), f32)
    names = ("halo", "chip", "cell", "ah", "al", "fwd", "inv", "mid")
    stored = far(*(t[k] for k in names))
    shapes = [x.shape[1:] if k in ("chip", "cell", "mid") else x.shape for k, x in zip(names, stored)]
    targets = tuple(sds(shape, x.dtype) for shape, x in zip(shapes, stored))
    f, cs, uv, halo_table, chip_table, cell, ah, al, fwd, inv, mid = call(
        advance_kernel,
        idx,
        (wave, potential, *far(t["main"]), *stored),
        [ANY] * (3 + len(stored)),
        (
            pltpu.HBM((2, 2, 4, 2, 64, NZ), f32),
            pltpu.HBM((2, 2, 4, 64, NZ), f32),
            sds((2048, 128), f32),
        )
        + targets,
        (ANY, ANY, VM) + (VM,) * len(stored),
        scratch=(
            pltpu.VMEM((2, 2, 4, LR, NZ), f32),
            pltpu.VMEM((4, LR, NZ), f32),
            pltpu.VMEM((256, 768), bf16),
            pltpu.VMEM((2, 4, 2, LR, NZ), f32),
            pltpu.VMEM((2, 4, LR, NZ), f32),
            pltpu.SemaphoreType.DMA((len(stored),)),
            pltpu.SemaphoreType.DMA((9,)),
            pltpu.SemaphoreType.DMA((24,)),
        ),
        flops=1 << 30,
        nbytes=5 << 20,
    )
    uv = call(
        halo_kernel,
        idx,
        near(halo, halo_table, cell, uv),
        [VM] * 4,
        sds((2048, 128), f32),
        VM,
        aliases={4: 0},
        flops=1 << 20,
        nbytes=1 << 20,
    )
    other = [(i, i ^ 1) for i in range(2 * CHIPS)]
    groups = [[2 * q + c for q in range(CHIPS)] for c in range(2)]
    exchange = functools.partial(
        lax.all_to_all, axis_name="ang", split_axis=0, concat_axis=0, tiled=True, axis_index_groups=groups
    )
    received = lax.ppermute(uv[1024:], "ang", other)
    UV, m = call(
        pair_kernel,
        idx,
        near(uv[:1024], received, chip_table),
        [VM] * 3,
        (lines, sds((512, 128), f32)),
        (VM, VM),
        flops=1 << 20,
        nbytes=2 << 20,
    )
    x = exchange(UV)
    y = call(
        middle_kernel,
        idx,
        near(x, fwd, inv, mid, ah, al),
        [VM] * 6,
        pltpu.HBM((CHIPS, 4, 8, 128), f32),
        ANY,
        scratch=(pltpu.VMEM((CHIPS, 4, 8, 128), f32), pltpu.SemaphoreType.DMA((2,))),
        flops=1 << 29,
        nbytes=3 << 20,
    ).reshape(lines.shape)
    w, mA, chip_table = call(
        local_kernel,
        idx,
        (*far(f, halo), *near(m), *[stored[i] for i in (2, 1, 3, 4, 0)], *far(y)),
        [ANY, ANY, VM] + [ANY] * 6,
        (sds(field.shape, f32), lines, sds((2, 64, 1, 128), f32)),
        (VM,) * 3,
        scratch=(
            pltpu.VMEM((LR, 128), f32),
            pltpu.VMEM((2, 64, 1, 128), f32),
            pltpu.VMEM(stored[3].shape, bf16),
            pltpu.VMEM(stored[4].shape, bf16),
            pltpu.VMEM((16, 8 * NZ), f32),
            pltpu.VMEM((2, 16, 16), f32),
            pltpu.VMEM((2, 2, 4, 2, 64, NZ), f32),
            pltpu.SemaphoreType.DMA((11,)),
        ),
        flops=3 << 30,
        nbytes=5 << 20,
    )
    y = exchange(y)
    near_cs = sds((2, 4, 64, NZ), f32)
    keep, send, cs_own, cs_other, cell = call(
        spread_kernel,
        idx,
        (*near(y, mA, chip_table, w), *far(cs), stored[2]),
        [VM] * 4 + [ANY] * 2,
        (lines, lines, near_cs, near_cs, targets[2]),
        (VM,) * 5,
        scratch=(pltpu.SemaphoreType.DMA((3,)),),
        flops=1 << 20,
        nbytes=5 << 20,
    )
    received = lax.ppermute(send, "ang", other)
    scratch = (pltpu.VMEM((2, 2, 4, 64, NZ), f32), pltpu.SemaphoreType.DMA((64 // CHUNK,)))
    whole_out = pltpu.HBM(wave.shape, f32)
    work = dict(flops=1 << 22, nbytes=6 << 20)
    out = call(
        finish_own_kernel, idx, near(w, cs_own, keep, cell), [VM] * 4, whole_out, ANY, scratch=scratch, **work
    )
    return call(
        finish_other_kernel,
        idx,
        (*near(w, cs_other, received, cell), out),
        [VM] * 4 + [ANY],
        whole_out,
        ANY,
        scratch=scratch,
        aliases={5: 0},
        **work,
    )


def solution(mesh):
    placed = (P(None, None, "ang", "rad", None), P("ang", "rad", None))
    return jax.shard_map(
        body,
        mesh=mesh,
        in_specs=placed,
        out_specs=P(None, None, "ang", "rad", None),
        check_vma=False,
    )
```

time: 66.3 us -> 61.9 us (0.934)
  Pallas kernels: 27.5 us -> 21.5 us
  starting transfers between devices: 16.5 us -> 11.2 us
  blocking collectives: 16.5 us -> 21.7 us
  waiting for transfers between devices: 5.2 us -> 7.11 us
    pallas_call x10 -> x9, Pallas kernels: 27.5 us -> 21.5 us  [call(): pl.pallas_call(kernel, out_shape=out_shape, grid_spec=pltpu.PrefetchScala...]
    all_to_all x1, starting transfers between devices: 10.2 us -> 4.75 us  [body(): y = exchange(y)]
    all_to_all x1, blocking collectives: 16.5 us -> 21.7 us  [body(): x = exchange(UV)]
    all_to_all x1, waiting for transfers between devices: 3.66 us -> 5.57 us  [body(): y = exchange(y)]
  transfers between devices with their start and end apart: 4 -> 4, of which waited for: 2 -> 2; matrix products, arithmetic and copies ran while one was open for 0% -> 0% of each run, Pallas kernels for 28% -> 20%
where the time goes in v3:
time: 61.9 us; the launch traced here: 61.7 us
  blocking collectives  21.7 us (35%)
  Pallas kernels  21.5 us (35%)
  starting transfers between devices  11.2 us (18%)
  waiting for transfers between devices  7.11 us (11%)
    all_to_all x1, blocking collectives, body(): x = exchange(UV)  21.7 us
    pallas_call x9, Pallas kernels, call(): pl.pallas_call(kernel, out_shape=out_shape, grid_spec=pltpu.PrefetchScala...  21.5 us
    all_to_all x1, waiting for transfers between devices, body(): y = exchange(y)  5.57 us
    all_to_all x1, starting transfers between devices, body(): y = exchange(y)  4.75 us
    ppermute x1, starting transfers between devices, body(): received = lax.ppermute(send, 'ang', other)  3.22 us
    ppermute x1, starting transfers between devices, body(): halo = lax.ppermute(rim, 'rad', [(0, 1), (1, 0)])  2.19 us
    ppermute x1, waiting for transfers between devices, body(): received = lax.ppermute(uv[1024:], 'ang', other)  1.54 us
  transfers between devices with their start and end apart: 4, of which 2 were waited for; matrix products, arithmetic and copies ran while one was open for 0% of the time, Pallas kernels for 20%

profile of v3, /device:TPU:1, one launch (start us, length us, event | category | flops | bytes accessed | tf_op | source)
XLA Modules:
  0.0 61.7 jit_solution(7903329401888048135)
XLA Ops:
  0.0 1.5 %rim_kernel.1 = f32[16,2048]{1,0:T(8,128)S(1)} custom-call(s32[8]{0:T(128)S(1)} %compare_select_fusion.6.idx, f32[2,2,4,128,256]{4,3,2,1,0:T(8,128)} %w.3, f32[4,128,256]{2,1,0:T(8,128)} %pot.3), custom_call_target="tpu_custom_call" | custom-call | tf_op jit(solution)/shard_map/rim_kernel/pallas_call | solution.py:527
  1.5 2.2 %collective-permute-start = (f32[16,2048]{1,0:T(8,128)S(1)}, f32[16,2048]{1,0:T(8,128)S(1)}, u32[]{:S(2)}, u32[]{:S(2)}) collective-permute-start(f32[16,2048]{1,0:T(8,128)S(1)} %rim_kernel.1), channel_id=1, source_target_pairs={{0,1},{1,0},{2,3},{3,2},{4,5},{5,4},{6,7},{7,6},{8,9},{9,8},{10,11... | collective-permute-start | bytes 393224 | tf_op jit(solution)/shard_map/ppermute | solution.py:584
  3.7 5.2 %advance_kernel.1 = (f32[2,2,4,2,64,256]{5,4,3,2,1,0:T(8,128)}, f32[2,2,4,64,256]{4,3,2,1,0:T(8,128)}, f32[2048,128]{1,0:T(8,128)S(1)}, f32[2,16,16]{2,1,0:T(8,1...) custom-call(s32[8]{0:T(128)S(1)} %compare_select_fusion.6.idx, ...), custom_call_target="tpu_custom_call" | custom-call | flops 1073741824 | bytes 5242880 | tf_op jit(solution)/shard_map/advance_kernel/pallas_call | solution.py:527
  8.9 0.0 collective-permute-done.halo.halo_far
  8.9 0.0 copy-start
  8.9 0.9 %halo_kernel.1 = f32[2048,128]{1,0:T(8,128)S(1)} custom-call(s32[8]{0:T(128)S(1)} %compare_select_fusion.6.idx, f32[16,2048]{1,0:T(8,128)S(1)} %collective-permute-done.halo.halo_far, f32[2,16,16]{2,1,0:T(8,128)S(1)} %get-tuple-element.27.table, f32[128,128]{1,0:T(8,128)S(1)} %get-tuple-element.28.coef, ...), custom_call_target="tpu_custom_call", output_to_operand_aliasing={{}: (4, {})} | custom-call | flops 1048576 | bytes 1048576 | tf_op jit(solution)/shard_map/halo_kernel/pallas_call | solution.py:527
  9.9 0.1 fusion
  9.9 0.0 copy-done
  10.0 1.0 %collective-permute-start.1 = (f32[1024,128]{1,0:T(8,128)S(1)}, f32[1024,128]{1,0:T(8,128)S(1)}, u32[]{:S(2)}, u32[]{:S(2)}) collective-permute-start(f32[1024,128]{1,0:T(8,128)S(1)} %get-tuple-element.47), channel_id=1, source_target_pairs={{0,2},{2,0},{4,6},{6,4},{8,10},{10,8},{12,14},{14,12},{16,18},{18,... | collective-permute-start | bytes 1572872 | tf_op jit(solution)/shard_map/ppermute | solution.py:632
  11.0 1.5 %collective-permute-done.1.received = f32[1024,128]{1,0:T(8,128)S(1)} collective-permute-done((f32[1024,128]{1,0:T(8,128)S(1)}, f32[1024,128]{1,0:T(8,128)S(1)}, u32[]{:S(2)}, u32[]{:S(2)}) %collective-permute-start.1) | collective-permute-done | bytes 524320 | tf_op jit(solution)/shard_map/ppermute | solution.py:632
  12.5 0.7 %pair_kernel.1 = (f32[1024,128]{1,0:T(8,128)S(1)}, f32[512,128]{1,0:T(8,128)S(1)}) custom-call(s32[8]{0:T(128)S(1)} %compare_select_fusion.6.idx, f32[1024,128]{1,0:T(8,128)S(1)} %get-tuple-element.48.own, f32[1024,128]{1,0:T(8,128)S(1)} %collective-permute-done.1.received, f32[4,64,1,128]{3,2,1,0:T(1,128)S(1)} %get-tuple-element.30.chip), custom_call_target="tpu_custom_call" | custom-call | flops 1048576 | bytes 2097152 | tf_op jit(solution)/shard_map/pair_kernel/pallas_call | solution.py:527
  13.3 21.7 %all_to_all.22 = f32[32,32,128]{2,1,0:T(8,128)S(1)} all-to-all(f32[32,32,128]{2,1,0:T(8,128)S(1)} %bitcast.7), channel_id=1, replica_groups={{0,4,8,12,16,20,24,28,32,36,40,44,48,52,56,60,64,68,72,76,80,84,88,92,9..., dimensions={0} | all-to-all | bytes 1048576 | tf_op jit(solution)/shard_map/all_to_all | solution.py:643
  35.0 2.3 %middle_kernel.1 = f32[32,4,8,128]{3,2,1,0:T(8,128)} custom-call(s32[8]{0:T(128)S(1)} %compare_select_fusion.6.idx, f32[1024,128]{1,0:T(8,128)S(1)} %bitcast.6, bf16[2,128,256]{2,1,0:T(8,128)(2,1)S(1)} %get-tuple-element.33.fwd, bf16[2,256,128]{2,1,0:T(8,128)(2,1)S(1)} %get-tuple-element.34.inv, f32[1,128]{1,0:T(1,128)S(1)} %get-tuple-element.35.mid, ...), custom_call_target="tpu_custom_call" | custom-call | flops 536870912 | bytes 3145728 | tf_op jit(solution)/shard_map/middle_kernel/pallas_call | solution.py:527
  37.3 4.7 %all-to-all-start.1 = ((f32[32,32,128]{2,1,0:T(8,128)}), f32[32,32,128]{2,1,0:T(8,128)S(1)}, u32[]{:S(2)}, u32[]{:S(2)}) async-start(f32[32,32,128]{2,1,0:T(8,128)} %bitcast.8), calls=%async_computation.1 | async-start | bytes 1048576 | tf_op jit(solution)/shard_map/all_to_all | solution.py:675
  42.1 5.3 %local_kernel.1 = (f32[2,4,2,128,256]{4,3,2,1,0:T(8,128)S(1)}, f32[1024,128]{1,0:T(8,128)S(1)}, f32[2,64,1,128]{3,2,1,0:T(1,128)S(1)}) custom-call(s32[8]{0:T(128)S(1)} %compare_select_fusion.6.idx, f32[2,2,4,2,64,256]{5,4,3,2,1,0:T(8,128)} %get-tuple-element.26.f, f32[16,2048]{1,0:T(8,128)} %copy-done, f32[512,128]{1,0:T(8,128)S(1)} %get-tuple-element.31.m_rows, ...), custom_call_target="tpu_custom_call" | custom-call | flops 3221225472 | bytes 5242880 | tf_op jit(solution)/shard_map/local_kernel/pallas_call | solution.py:527
  47.4 5.6 %all-to-all-done.1 = f32[32,32,128]{2,1,0:T(8,128)S(1)} async-done(((f32[32,32,128]{2,1,0:T(8,128)}), f32[32,32,128]{2,1,0:T(8,128)S(1)}, u32[]{:S(2)}, u32[]{:S(2)}) %all-to-all-start.1) | async-done | bytes 524320 | tf_op jit(solution)/shard_map/all_to_all | solution.py:675
  53.0 1.8 %spread_kernel.1 = (f32[1024,128]{1,0:T(8,128)S(1)}, f32[1024,128]{1,0:T(8,128)S(1)}, f32[2,4,64,256]{3,2,1,0:T(8,128)S(1)}, f32[2,4,64,256]{3,2,1,0:T(8,128)S(1)}, f32[128,128]{1,0:T(8,128)S(1)}) custom-call(s32[8]{0:T(128)S(1)} %compare_select_fusion.6.idx, f32[1024,128]{1,0:T(8,128)S(1)} %bitcast.5, f32[1024,128]{1,0:T(8,128)S(1)} %get-tuple-element.39.mA, ...), custom_call_target="tpu_custom_call" | custom-call | flops 1048576 | bytes 5242880 | tf_op jit(solution)/shard_map/spread_kernel/pallas_call | solution.py:527
  54.7 3.2 %collective-permute-start.2 = (f32[1024,128]{1,0:T(8,128)S(1)}, f32[1024,128]{1,0:T(8,128)S(1)}, u32[]{:S(2)}, u32[]{:S(2)}) collective-permute-start(f32[1024,128]{1,0:T(8,128)S(1)} %get-tuple-element.43), channel_id=1, source_target_pairs={{0,2},{2,0},{4,6},{6,4},{8,10},{10,8},{12,14},{14,12},{16,18},{18,... | collective-permute-start | bytes 1572872 | tf_op jit(solution)/shard_map/ppermute | solution.py:688
  58.0 1.8 %finish_own_kernel.1.before = f32[2,2,4,128,256]{4,3,2,1,0:T(8,128)} custom-call(s32[8]{0:T(128)S(1)} %compare_select_fusion.6.idx, f32[2,4,2,128,256]{4,3,2,1,0:T(8,128)S(1)} %get-tuple-element.38.after.w, f32[2,4,64,256]{3,2,1,0:T(8,128)S(1)} %get-tuple-element.45.cs, f32[1024,128]{1,0:T(8,128)S(1)} %get-tuple-element.46.y, ...), custom_call_target="tpu_custom_call" | custom-call | flops 4194304 | bytes 6291456 | tf_op jit(solution)/shard_map/finish_own_kernel/pallas_call | solution.py:527
  59.8 0.0 collective-permute-done.2.y
  59.8 1.8 %finish_other_kernel.1 = f32[2,2,4,128,256]{4,3,2,1,0:T(8,128)} custom-call(s32[8]{0:T(128)S(1)} %compare_select_fusion.6.idx, f32[2,4,2,128,256]{4,3,2,1,0:T(8,128)S(1)} %get-tuple-element.38.after.w, f32[2,4,64,256]{3,2,1,0:T(8,128)S(1)} %get-tuple-element.42.cs, f32[1024,128]{1,0:T(8,128)S(1)} %collective-permute-done.2.y, ...), custom_call_target="tpu_custom_call", output_to_operand_aliasing={{}: (5, {})} | custom-call | flops 4194304 | bytes 6291456 | tf_op jit(solution)/shard_map/finish_other_kernel/pallas_call | solution.py:527
  (1 shorter events, 0.0 us)
Async XLA Ops:
  1.5 7.4 %collective-permute-start = (f32[16,2048]{1,0:T(8,128)S(1)}, f32[16,2048]{1,0:T(8,128)S(1)}, u32[]{:S(2)}, u32[]{:S(2)}) collective-permute-start(f32[16,2048]{1,0:T(8,128)S(1)} %rim_kernel.1), channel_id=1, source_target_pairs={{0,1},{1,0},{2,3},{3,2},{4,5},{5,4},{6,7},{7,6},{8,9},{9,8},{10,11... | collective-permute-start | bytes 393224 | tf_op jit(solution)/shard_map/ppermute | solution.py:584
  8.9 1.0 %copy-start = (f32[16,2048]{1,0:T(8,128)}, f32[16,2048]{1,0:T(8,128)S(1)}, u32[]{:S(2)}) copy-start(f32[16,2048]{1,0:T(8,128)S(1)} %collective-permute-done.halo.halo_far) | copy-start | bytes 393220
  10.0 2.6 %collective-permute-start.1 = (f32[1024,128]{1,0:T(8,128)S(1)}, f32[1024,128]{1,0:T(8,128)S(1)}, u32[]{:S(2)}, u32[]{:S(2)}) collective-permute-start(f32[1024,128]{1,0:T(8,128)S(1)} %get-tuple-element.47), channel_id=1, source_target_pairs={{0,2},{2,0},{4,6},{6,4},{8,10},{10,8},{12,14},{14,12},{16,18},{18,... | collective-permute-start | bytes 1572872 | tf_op jit(solution)/shard_map/ppermute | solution.py:632
  37.3 15.7 %all-to-all-start.1 = ((f32[32,32,128]{2,1,0:T(8,128)}), f32[32,32,128]{2,1,0:T(8,128)S(1)}, u32[]{:S(2)}, u32[]{:S(2)}) async-start(f32[32,32,128]{2,1,0:T(8,128)} %bitcast.8), calls=%async_computation.1 | async-start | bytes 1048576 | tf_op jit(solution)/shard_map/all_to_all | solution.py:675
  54.7 5.1 %collective-permute-start.2 = (f32[1024,128]{1,0:T(8,128)S(1)}, f32[1024,128]{1,0:T(8,128)S(1)}, u32[]{:S(2)}, u32[]{:S(2)}) collective-permute-start(f32[1024,128]{1,0:T(8,128)S(1)} %get-tuple-element.43), channel_id=1, source_target_pairs={{0,2},{2,0},{4,6},{6,4},{8,10},{10,8},{12,14},{14,12},{16,18},{18,... | collective-permute-start | bytes 1572872 | tf_op jit(solution)/shard_map/ppermute | solution.py:688

commit v4 on v3

--- a/solution.py
+++ b/solution.py
@@ -229,15 +229,14 @@
     return add(add(f[0], even), odd), sub(even, odd)
 
 
-def advance_kernel(idx, w, pot, main, *refs):
+def advance_kernel(idx, w, pot, w0, pot0, main_in, *refs):
     sources, (f_out, cs_out, uv), targets = refs[:8], refs[8:11], refs[11:19]
-    w_in, pot_in, main_in, f, cs, sems, in_sems, out_sems = refs[19:]
+    w_in, pot_in, f, cs, staged, sems, in_sems, out_sems = refs[19:]
     own = {1: idx[3], 2: idx[0], 7: idx[4]}
     copies = [
         pltpu.make_async_copy(x.at[own[i]] if i in own else x, y, sems.at[i])
         for i, (x, y) in enumerate(zip(sources, targets))
     ]
-    fetch_main = pltpu.make_async_copy(main.at[idx[0]], main_in, in_sems.at[8])
     fetches = [
         (
             pltpu.make_async_copy(pot.at[t], pot_in.at[t], in_sems.at[t]),
@@ -246,31 +245,44 @@
         for t in range(4)
     ]
     leaving = []
-    for copy in fetches[0]:
-        copy.start()
-    fetch_main.start()
     for pair in fetches[1:]:
         for copy in pair:
             copy.start()
     for copy in copies:
         copy.start()
-    for t in range(4):
-        fetches[t][0].wait()
-        c, s = cos_sin(pot_in[t])
-        cs[0, t] = c
-        cs[1, t] = s
-        fetches[t][1].wait()
+
+    def rotate(t):
+        for row in range(0, LR, 16):
+            rows, imag = slice(row, row + 16), slice(LR + row, LR + row + 16)
+            c, s = cos_sin(pot_in[t, rows, :] if t else pot0[rows, :])
+            cs[0, t, rows, :] = c
+            cs[1, t, rows, :] = s
+            for m in range(2):
+                re, im = [w_in[i, m, t, rows, :] if t else w0[i, m, rows, :] for i in range(2)]
+                for at, x in ((rows, c * re + s * im), (imag, c * im - s * re)):
+                    staged[t % 2, m, 0, at, :], staged[t % 2, m, 1, at, :] = halves(x)
+
+    def multiply(t):
+        for m in range(2):
+            hi, lo = staged[t % 2, m, 0], staged[t % 2, m, 1]
+            x = jnp.concatenate([hi, lo, hi], axis=0)
+            f[m, t] = dot(main_in[...], x).reshape(2, LR, NZ)
+
+    for t in range(5):
+        if 0 < t < 4:
+            for copy in fetches[t]:
+                copy.wait()
+        if t > 0:
+            multiply(t - 1)
+        if t < 4:
+            rotate(t)
         if t == 0:
-            fetch_main.wait()
-        for m in range(2):
-            re, im = w_in[0, m, t], w_in[1, m, t]
-            x = jnp.concatenate([c * re + s * im, c * im - s * re], axis=0)
-            f[m, t] = dot(main_in[...], stacked(x)).reshape(2, LR, NZ)
+            continue
         for j in range(2):
             rows = pl.ds(64 * j, 64)
             for m in range(2):
-                leaving.append((f.at[m, t, :, rows, :], f_out.at[m, j, t]))
-            leaving.append((cs.at[:, t, rows, :], cs_out.at[j, :, t]))
+                leaving.append((f.at[m, t - 1, :, rows, :], f_out.at[m, j, t - 1]))
+            leaving.append((cs.at[:, t - 1, rows, :], cs_out.at[j, :, t - 1]))
         first = len(leaving) - 6
         for i in range(6):
             leaving[first + i] = pltpu.make_async_copy(*leaving[first + i], out_sems.at[first + i])
@@ -295,13 +307,28 @@
         copy.wait()
 
 
-def rim_kernel(idx, w, pot, out):
+def rim_kernel(idx, w, pot, main, out, w0, pot0, main_in, w_rim, pot_rim, sems):
+    rows = pl.ds(pl.multiple_of(idx[5] * 8, 8), 8)
+    pairs = (
+        (pot.at[:, rows, :], pot_rim),
+        (w.at[:, :, :, rows, :], w_rim),
+        (pot.at[0], pot0),
+        (w.at[:, :, 0], w0),
+        (main.at[idx[0]], main_in),
+    )
+    copies = [pltpu.make_async_copy(a, b, sems.at[i]) for i, (a, b) in enumerate(pairs)]
+    for copy in copies:
+        copy.start()
+    for copy in copies[:2]:
+        copy.wait()
     for t in range(4):
-        c, s = cos_sin(pot[t])
+        c, s = cos_sin(pot_rim[t])
         for m in range(2):
-            re, im = w[0, m, t], w[1, m, t]
+            re, im = w_rim[0, m, t], w_rim[1, m, t]
             x = jnp.concatenate([c * re + s * im, c * im - s * re], axis=0)
             out[:, (2 * t + m) * NZ : (2 * t + m + 1) * NZ] = x
+    for copy in copies[2:]:
+        copy.wait()
 
 
 def halo_part(table, halo):
@@ -570,16 +597,18 @@
 
     sds = pltpu.VMEM
     wave, potential = far(wave, potential)
-    rim = call(
+    rim, w0, pot0, main = call(
         rim_kernel,
         idx,
-        (wave, potential),
-        [
-            pl.BlockSpec((2, 2, 4, 8, NZ), lambda a, i: (0, 0, 0, i[5], 0)),
-            pl.BlockSpec((4, 8, NZ), lambda a, i: (0, i[5], 0)),
-        ],
-        sds((16, 8 * NZ), f32),
-        VM,
+        (wave, potential, *far(t["main"])),
+        [ANY] * 3,
+        (sds((16, 8 * NZ), f32), sds((2, 2, LR, NZ), f32), sds((LR, NZ), f32), sds((256, 768), bf16)),
+        (VM,) * 4,
+        scratch=(
+            pltpu.VMEM((2, 2, 4, 8, NZ), f32),
+            pltpu.VMEM((4, 8, NZ), f32),
+            pltpu.SemaphoreType.DMA((5,)),
+        ),
     )
     halo = lax.ppermute(rim, "rad", [(0, 1), (1, 0)])
     field = pltpu.HBM((2, 4, 2, LR, NZ), f32)
@@ -591,8 +620,8 @@
     f, cs, uv, halo_table, chip_table, cell, ah, al, fwd, inv, mid = call(
         advance_kernel,
         idx,
-        (wave, potential, *far(t["main"]), *stored),
-        [ANY] * (3 + len(stored)),
+        (wave, potential, *near(w0, pot0, main), *stored),
+        [ANY] * 2 + [VM] * 3 + [ANY] * len(stored),
         (
             pltpu.HBM((2, 2, 4, 2, 64, NZ), f32),
             pltpu.HBM((2, 2, 4, 64, NZ), f32),
@@ -603,9 +632,9 @@
         scratch=(
             pltpu.VMEM((2, 2, 4, LR, NZ), f32),
             pltpu.VMEM((4, LR, NZ), f32),
-            pltpu.VMEM((256, 768), bf16),
             pltpu.VMEM((2, 4, 2, LR, NZ), f32),
             pltpu.VMEM((2, 4, LR, NZ), f32),
+            pltpu.VMEM((2, 2, 2, 256, NZ), bf16),
             pltpu.SemaphoreType.DMA((len(stored),)),
             pltpu.SemaphoreType.DMA((9,)),
             pltpu.SemaphoreType.DMA((24,)),

time: 61.9 us -> 62 us (level)
  transfers between devices with their start and end apart: 4 -> 4, of which waited for: 2 -> 2; matrix products, arithmetic and copies ran while one was open for 0% -> 0% of each run, Pallas kernels for 20% -> 19%
where the time goes in v4:
time: 62 us; the launch traced here: 61.7 us
  blocking collectives  21.7 us (35%)
  Pallas kernels  21.5 us (35%)
  starting transfers between devices  11.2 us (18%)
  waiting for transfers between devices  7.11 us (11%)
    all_to_all x1, blocking collectives, body(): x = exchange(UV)  21.7 us
    pallas_call x9, Pallas kernels, call(): pl.pallas_call(kernel, out_shape=out_shape, grid_spec=pltpu.PrefetchScala...  21.5 us
    all_to_all x1, waiting for transfers between devices, body(): y = exchange(y)  5.57 us
    all_to_all x1, starting transfers between devices, body(): y = exchange(y)  4.76 us
    ppermute x1, starting transfers between devices, body(): received = lax.ppermute(send, 'ang', other)  3.22 us
    ppermute x1, starting transfers between devices, body(): halo = lax.ppermute(rim, 'rad', [(0, 1), (1, 0)])  2.19 us
    ppermute x1, waiting for transfers between devices, body(): received = lax.ppermute(uv[1024:], 'ang', other)  1.54 us
  transfers between devices with their start and end apart: 4, of which 2 were waited for; matrix products, arithmetic and copies ran while one was open for 0% of the time, Pallas kernels for 19%

profile of v4, /device:TPU:1, one launch (start us, length us, event | category | flops | bytes accessed | tf_op | source)
XLA Modules:
  0.0 61.7 jit_solution(4299660564505383753)
XLA Ops:
  0.0 1.9 %rim_kernel.1 = (f32[16,2048]{1,0:T(8,128)S(1)}, f32[2,2,128,256]{3,2,1,0:T(8,128)S(1)}, f32[128,256]{1,0:T(8,128)S(1)}, bf16[256,768]{1,0:T(8,128)(2,1)S(1)}) custom-call(s32[8]{0:T(128)S(1)} %compare_select_fusion.6.idx, f32[2,2,4,128,256]{4,3,2,1,0:T(8,128)} %w.3, f32[4,128,256]{2,1,0:T(8,128)} %pot.3, bf16[2,256,768]{2,1,0:T(8,128)(2,1)} %constant.93.clone.main), custom_call_target="tpu_custom_call" | custom-call | tf_op jit(solution)/shard_map/rim_kernel/pallas_call | solution.py:554
  1.9 2.2 %collective-permute-start = (f32[16,2048]{1,0:T(8,128)S(1)}, f32[16,2048]{1,0:T(8,128)S(1)}, u32[]{:S(2)}, u32[]{:S(2)}) collective-permute-start(f32[16,2048]{1,0:T(8,128)S(1)} %get-tuple-element.34), channel_id=1, source_target_pairs={{0,1},{1,0},{2,3},{3,2},{4,5},{5,4},{6,7},{7,6},{8,9},{9,8},{10,11... | collective-permute-start | bytes 393224 | tf_op jit(solution)/shard_map/ppermute | solution.py:613
  4.1 4.8 %advance_kernel.1 = (f32[2,2,4,2,64,256]{5,4,3,2,1,0:T(8,128)}, f32[2,2,4,64,256]{4,3,2,1,0:T(8,128)}, f32[2048,128]{1,0:T(8,128)S(1)}, f32[2,16,16]{2,1,0:T(8,1...) custom-call(s32[8]{0:T(128)S(1)} %compare_select_fusion.6.idx, ...), custom_call_target="tpu_custom_call" | custom-call | flops 1073741824 | bytes 5242880 | tf_op jit(solution)/shard_map/advance_kernel/pallas_call | solution.py:554
  8.9 0.0 collective-permute-done.halo.halo_far
  9.0 0.0 copy-start
  9.0 0.9 %halo_kernel.1 = f32[2048,128]{1,0:T(8,128)S(1)} custom-call(s32[8]{0:T(128)S(1)} %compare_select_fusion.6.idx, f32[16,2048]{1,0:T(8,128)S(1)} %collective-permute-done.halo.halo_far, f32[2,16,16]{2,1,0:T(8,128)S(1)} %get-tuple-element.35.table, f32[128,128]{1,0:T(8,128)S(1)} %get-tuple-element.36.coef, ...), custom_call_target="tpu_custom_call", output_to_operand_aliasing={{}: (4, {})} | custom-call | flops 1048576 | bytes 1048576 | tf_op jit(solution)/shard_map/halo_kernel/pallas_call | solution.py:554
  9.9 0.1 fusion
  10.0 0.0 copy-done
  10.0 1.0 %collective-permute-start.1 = (f32[1024,128]{1,0:T(8,128)S(1)}, f32[1024,128]{1,0:T(8,128)S(1)}, u32[]{:S(2)}, u32[]{:S(2)}) collective-permute-start(f32[1024,128]{1,0:T(8,128)S(1)} %get-tuple-element.55), channel_id=1, source_target_pairs={{0,2},{2,0},{4,6},{6,4},{8,10},{10,8},{12,14},{14,12},{16,18},{18,... | collective-permute-start | bytes 1572872 | tf_op jit(solution)/shard_map/ppermute | solution.py:661
  11.0 1.5 %collective-permute-done.1.received = f32[1024,128]{1,0:T(8,128)S(1)} collective-permute-done((f32[1024,128]{1,0:T(8,128)S(1)}, f32[1024,128]{1,0:T(8,128)S(1)}, u32[]{:S(2)}, u32[]{:S(2)}) %collective-permute-start.1) | collective-permute-done | bytes 524320 | tf_op jit(solution)/shard_map/ppermute | solution.py:661
  12.6 0.7 %pair_kernel.1 = (f32[1024,128]{1,0:T(8,128)S(1)}, f32[512,128]{1,0:T(8,128)S(1)}) custom-call(s32[8]{0:T(128)S(1)} %compare_select_fusion.6.idx, f32[1024,128]{1,0:T(8,128)S(1)} %get-tuple-element.56.own, f32[1024,128]{1,0:T(8,128)S(1)} %collective-permute-done.1.received, f32[4,64,1,128]{3,2,1,0:T(1,128)S(1)} %get-tuple-element.38.chip), custom_call_target="tpu_custom_call" | custom-call | flops 1048576 | bytes 2097152 | tf_op jit(solution)/shard_map/pair_kernel/pallas_call | solution.py:554
  13.3 21.7 %all_to_all.22 = f32[32,32,128]{2,1,0:T(8,128)S(1)} all-to-all(f32[32,32,128]{2,1,0:T(8,128)S(1)} %bitcast.7), channel_id=1, replica_groups={{0,4,8,12,16,20,24,28,32,36,40,44,48,52,56,60,64,68,72,76,80,84,88,92,9..., dimensions={0} | all-to-all | bytes 1048576 | tf_op jit(solution)/shard_map/all_to_all | solution.py:672
  35.0 2.3 %middle_kernel.1 = f32[32,4,8,128]{3,2,1,0:T(8,128)} custom-call(s32[8]{0:T(128)S(1)} %compare_select_fusion.6.idx, f32[1024,128]{1,0:T(8,128)S(1)} %bitcast.6, bf16[2,128,256]{2,1,0:T(8,128)(2,1)S(1)} %get-tuple-element.41.fwd, bf16[2,256,128]{2,1,0:T(8,128)(2,1)S(1)} %get-tuple-element.42.inv, f32[1,128]{1,0:T(1,128)S(1)} %get-tuple-element.43.mid, ...), custom_call_target="tpu_custom_call" | custom-call | flops 536870912 | bytes 3145728 | tf_op jit(solution)/shard_map/middle_kernel/pallas_call | solution.py:554
  37.3 4.8 %all-to-all-start.1 = ((f32[32,32,128]{2,1,0:T(8,128)}), f32[32,32,128]{2,1,0:T(8,128)S(1)}, u32[]{:S(2)}, u32[]{:S(2)}) async-start(f32[32,32,128]{2,1,0:T(8,128)} %bitcast.8), calls=%async_computation.1 | async-start | bytes 1048576 | tf_op jit(solution)/shard_map/all_to_all | solution.py:704
  42.1 5.3 %local_kernel.1 = (f32[2,4,2,128,256]{4,3,2,1,0:T(8,128)S(1)}, f32[1024,128]{1,0:T(8,128)S(1)}, f32[2,64,1,128]{3,2,1,0:T(1,128)S(1)}) custom-call(s32[8]{0:T(128)S(1)} %compare_select_fusion.6.idx, f32[2,2,4,2,64,256]{5,4,3,2,1,0:T(8,128)} %get-tuple-element.33.f, f32[16,2048]{1,0:T(8,128)} %copy-done, f32[512,128]{1,0:T(8,128)S(1)} %get-tuple-element.39.m_rows, ...), custom_call_target="tpu_custom_call" | custom-call | flops 3221225472 | bytes 5242880 | tf_op jit(solution)/shard_map/local_kernel/pallas_call | solution.py:554
  47.4 5.6 %all-to-all-done.1 = f32[32,32,128]{2,1,0:T(8,128)S(1)} async-done(((f32[32,32,128]{2,1,0:T(8,128)}), f32[32,32,128]{2,1,0:T(8,128)S(1)}, u32[]{:S(2)}, u32[]{:S(2)}) %all-to-all-start.1) | async-done | bytes 524320 | tf_op jit(solution)/shard_map/all_to_all | solution.py:704
  53.0 1.8 %spread_kernel.1 = (f32[1024,128]{1,0:T(8,128)S(1)}, f32[1024,128]{1,0:T(8,128)S(1)}, f32[2,4,64,256]{3,2,1,0:T(8,128)S(1)}, f32[2,4,64,256]{3,2,1,0:T(8,128)S(1)}, f32[128,128]{1,0:T(8,128)S(1)}) custom-call(s32[8]{0:T(128)S(1)} %compare_select_fusion.6.idx, f32[1024,128]{1,0:T(8,128)S(1)} %bitcast.5, f32[1024,128]{1,0:T(8,128)S(1)} %get-tuple-element.47.mA, ...), custom_call_target="tpu_custom_call" | custom-call | flops 1048576 | bytes 5242880 | tf_op jit(solution)/shard_map/spread_kernel/pallas_call | solution.py:554
  54.8 3.2 %collective-permute-start.2 = (f32[1024,128]{1,0:T(8,128)S(1)}, f32[1024,128]{1,0:T(8,128)S(1)}, u32[]{:S(2)}, u32[]{:S(2)}) collective-permute-start(f32[1024,128]{1,0:T(8,128)S(1)} %get-tuple-element.51), channel_id=1, source_target_pairs={{0,2},{2,0},{4,6},{6,4},{8,10},{10,8},{12,14},{14,12},{16,18},{18,... | collective-permute-start | bytes 1572872 | tf_op jit(solution)/shard_map/ppermute | solution.py:717
  58.0 1.8 %finish_own_kernel.1.before = f32[2,2,4,128,256]{4,3,2,1,0:T(8,128)} custom-call(s32[8]{0:T(128)S(1)} %compare_select_fusion.6.idx, f32[2,4,2,128,256]{4,3,2,1,0:T(8,128)S(1)} %get-tuple-element.46.after.w, f32[2,4,64,256]{3,2,1,0:T(8,128)S(1)} %get-tuple-element.53.cs, f32[1024,128]{1,0:T(8,128)S(1)} %get-tuple-element.54.y, ...), custom_call_target="tpu_custom_call" | custom-call | flops 4194304 | bytes 6291456 | tf_op jit(solution)/shard_map/finish_own_kernel/pallas_call | solution.py:554
  59.8 0.0 collective-permute-done.2.y
  59.8 1.8 %finish_other_kernel.1 = f32[2,2,4,128,256]{4,3,2,1,0:T(8,128)} custom-call(s32[8]{0:T(128)S(1)} %compare_select_fusion.6.idx, f32[2,4,2,128,256]{4,3,2,1,0:T(8,128)S(1)} %get-tuple-element.46.after.w, f32[2,4,64,256]{3,2,1,0:T(8,128)S(1)} %get-tuple-element.50.cs, f32[1024,128]{1,0:T(8,128)S(1)} %collective-permute-done.2.y, ...), custom_call_target="tpu_custom_call", output_to_operand_aliasing={{}: (5, {})} | custom-call | flops 4194304 | bytes 6291456 | tf_op jit(solution)/shard_map/finish_other_kernel/pallas_call | solution.py:554
  (1 shorter events, 0.0 us)
Async XLA Ops:
  1.9 7.0 %collective-permute-start = (f32[16,2048]{1,0:T(8,128)S(1)}, f32[16,2048]{1,0:T(8,128)S(1)}, u32[]{:S(2)}, u32[]{:S(2)}) collective-permute-start(f32[16,2048]{1,0:T(8,128)S(1)} %get-tuple-element.34), channel_id=1, source_target_pairs={{0,1},{1,0},{2,3},{3,2},{4,5},{5,4},{6,7},{7,6},{8,9},{9,8},{10,11... | collective-permute-start | bytes 393224 | tf_op jit(solution)/shard_map/ppermute | solution.py:613
  9.0 1.0 %copy-start = (f32[16,2048]{1,0:T(8,128)}, f32[16,2048]{1,0:T(8,128)S(1)}, u32[]{:S(2)}) copy-start(f32[16,2048]{1,0:T(8,128)S(1)} %collective-permute-done.halo.halo_far) | copy-start | bytes 393220
  10.0 2.6 %collective-permute-start.1 = (f32[1024,128]{1,0:T(8,128)S(1)}, f32[1024,128]{1,0:T(8,128)S(1)}, u32[]{:S(2)}, u32[]{:S(2)}) collective-permute-start(f32[1024,128]{1,0:T(8,128)S(1)} %get-tuple-element.55), channel_id=1, source_target_pairs={{0,2},{2,0},{4,6},{6,4},{8,10},{10,8},{12,14},{14,12},{16,18},{18,... | collective-permute-start | bytes 1572872 | tf_op jit(solution)/shard_map/ppermute | solution.py:661
  37.3 15.7 %all-to-all-start.1 = ((f32[32,32,128]{2,1,0:T(8,128)}), f32[32,32,128]{2,1,0:T(8,128)S(1)}, u32[]{:S(2)}, u32[]{:S(2)}) async-start(f32[32,32,128]{2,1,0:T(8,128)} %bitcast.8), calls=%async_computation.1 | async-start | bytes 1048576 | tf_op jit(solution)/shard_map/all_to_all | solution.py:704
  54.8 5.1 %collective-permute-start.2 = (f32[1024,128]{1,0:T(8,128)S(1)}, f32[1024,128]{1,0:T(8,128)S(1)}, u32[]{:S(2)}, u32[]{:S(2)}) collective-permute-start(f32[1024,128]{1,0:T(8,128)S(1)} %get-tuple-element.51), channel_id=1, source_target_pairs={{0,2},{2,0},{4,6},{6,4},{8,10},{10,8},{12,14},{14,12},{16,18},{18,... | collective-permute-start | bytes 1572872 | tf_op jit(solution)/shard_map/ppermute | solution.py:717

commit v5 on v3

--- a/solution.py
+++ b/solution.py
@@ -231,7 +231,7 @@
 
 def advance_kernel(idx, w, pot, main, *refs):
     sources, (f_out, cs_out, uv), targets = refs[:8], refs[8:11], refs[11:19]
-    w_in, pot_in, main_in, f, cs, sems, in_sems, out_sems = refs[19:]
+    w_in, pot_in, main_in, f, cs, staged, sems, in_sems, out_sems = refs[19:]
     own = {1: idx[3], 2: idx[0], 7: idx[4]}
     copies = [
         pltpu.make_async_copy(x.at[own[i]] if i in own else x, y, sems.at[i])
@@ -254,23 +254,41 @@
             copy.start()
     for copy in copies:
         copy.start()
-    for t in range(4):
-        fetches[t][0].wait()
-        c, s = cos_sin(pot_in[t])
-        cs[0, t] = c
-        cs[1, t] = s
-        fetches[t][1].wait()
+
+    def rotate(t):
+        for row in range(0, LR, 16):
+            rows, imag = slice(row, row + 16), slice(LR + row, LR + row + 16)
+            c, s = cos_sin(pot_in[t, rows, :])
+            cs[0, t, rows, :] = c
+            cs[1, t, rows, :] = s
+            for m in range(2):
+                re, im = w_in[0, m, t, rows, :], w_in[1, m, t, rows, :]
+                for at, x in ((rows, c * re + s * im), (imag, c * im - s * re)):
+                    staged[t % 2, m, 0, at, :], staged[t % 2, m, 1, at, :] = halves(x)
+
+    def multiply(t):
+        for m in range(2):
+            hi, lo = staged[t % 2, m, 0], staged[t % 2, m, 1]
+            x = jnp.concatenate([hi, lo, hi], axis=0)
+            f[m, t] = dot(main_in[...], x).reshape(2, LR, NZ)
+
+    for t in range(5):
+        if t < 4:
+            for copy in fetches[t]:
+                copy.wait()
+        if t == 1:
+            fetch_main.wait()
+        if t > 0:
+            multiply(t - 1)
+        if t < 4:
+            rotate(t)
         if t == 0:
-            fetch_main.wait()
-        for m in range(2):
-            re, im = w_in[0, m, t], w_in[1, m, t]
-            x = jnp.concatenate([c * re + s * im, c * im - s * re], axis=0)
-            f[m, t] = dot(main_in[...], stacked(x)).reshape(2, LR, NZ)
+            continue
         for j in range(2):
             rows = pl.ds(64 * j, 64)
             for m in range(2):
-                leaving.append((f.at[m, t, :, rows, :], f_out.at[m, j, t]))
-            leaving.append((cs.at[:, t, rows, :], cs_out.at[j, :, t]))
+                leaving.append((f.at[m, t - 1, :, rows, :], f_out.at[m, j, t - 1]))
+            leaving.append((cs.at[:, t - 1, rows, :], cs_out.at[j, :, t - 1]))
         first = len(leaving) - 6
         for i in range(6):
             leaving[first + i] = pltpu.make_async_copy(*leaving[first + i], out_sems.at[first + i])
@@ -463,64 +481,84 @@
     return pltpu.make_async_copy(cs.at[row], cs_out, sem)
 
 
-def spread_kernel(idx, y, mA, chip, after, cs, cell_far, keep, send, cs_own, cs_other, cell, sems):
-    copies = [fetch(idx[1] ^ i, cs, x, sems.at[i]) for i, x in enumerate((cs_own, cs_other))]
-    copies.append(pltpu.make_async_copy(cell_far.at[idx[0]], cell, sems.at[2]))
-    for copy in copies:
-        copy.start()
+def spread_kernel(idx, y, mA, chip, after, keep, send):
     x = tiles(y[...])
     total = x + row_swap(x, 4)
     inner = row_times(chip, 0, total) + tiles(mA[...])
     mask = first_rows(idx[1], x.shape)
     keep[...] = jnp.where(mask, x, inner).reshape(keep.shape)
     send[...] = jnp.where(mask, inner, x).reshape(keep.shape)
+
+
+CHUNK = 16
+
+
+CHUNK = 16
+
+
+def gather_half(half, idx, w, y, coef, n):
+    there = pl.ds(pl.multiple_of((idx[1] ^ half) * 64 + n * CHUNK, CHUNK), CHUNK)
+    k = coef[there, :]
+    for m in range(2):
+        a = [
+            jnp.concatenate(
+                [y[pl.ds(n * CHUNK * 16 + 8 * z + 2 * i + m, CHUNK, stride=16), :] for z in range(2)], axis=1
+            )
+            for i in range(4)
+        ]
+        left, right = (a[0], a[1]), (a[2], a[3])
+        s, d = add(left, right), sub(left, right)
+        even = cmul(*weights(k, 0, NZ), s)
+        odd = cmul(*weights(k, 1, NZ), d)
+        parts = [left, add(even, odd), cmul(*weights(k, 2, NZ), s), sub(even, odd)]
+        for t in range(4):
+            yield m, t, w[m, t, 0, there, :] + parts[t][0], w[m, t, 1, there, :] + parts[t][1]
+
+
+def rotate_out(o, cs, m, t, rows, re, im):
+    c, s = cs[0, t, rows, :], cs[1, t, rows, :]
+    o[0, m, t, rows, :] = c * re + s * im
+    o[1, m, t, rows, :] = c * im - s * re
+
+
+def leave(half, idx, o, out, sems, n):
+    rows = pl.ds(n * CHUNK, CHUNK)
+    there = pl.ds(pl.multiple_of((idx[1] ^ half) * 64 + n * CHUNK, CHUNK), CHUNK)
+    return pltpu.make_async_copy(o.at[:, :, :, rows, :], out.at[:, :, :, there, :], sems.at[n])
+
+
+def finish_own_kernel(idx, w, y, cell_far, cs_far, out, cs_other, cell, o, cs_own, sems, more):
+    near_cell = pltpu.make_async_copy(cell_far.at[idx[0]], cell, more.at[2])
+    near_cell.start()
+    copies = [fetch(idx[1] ^ i, cs_far, x, more.at[i]) for i, x in enumerate((cs_own, cs_other))]
     for copy in copies:
-        copy.wait()
-
-
-CHUNK = 16
-
-
-def finish_kernel(half, idx, w, cs, y, coef, out, o, sems):
-    place = (idx[1] ^ half) * 64
-
-    def leave(n):
-        rows = pl.ds(pl.multiple_of(n * CHUNK, CHUNK), CHUNK)
-        there = pl.ds(pl.multiple_of(place + n * CHUNK, CHUNK), CHUNK)
-        return pltpu.make_async_copy(o.at[:, :, :, rows, :], out.at[:, :, :, there, :], sems.at[n])
-
+        copy.start()
+    near_cell.wait()
     for n in range(64 // CHUNK):
-        here = slice(n * CHUNK, (n + 1) * CHUNK)
-        there = pl.ds(pl.multiple_of(place + n * CHUNK, CHUNK), CHUNK)
-        k = coef[there, :]
+        rows = slice(n * CHUNK, (n + 1) * CHUNK)
+        for m, t, re, im in gather_half(0, idx, w, y, cell, n):
+            o[0, m, t, rows, :] = re
+            o[1, m, t, rows, :] = im
+    copies[0].wait()
+    for n in range(64 // CHUNK):
+        rows = slice(n * CHUNK, (n + 1) * CHUNK)
         for m in range(2):
-            a = [
-                jnp.concatenate(
-                    [y[pl.ds(n * CHUNK * 16 + 8 * z + 2 * i + m, CHUNK, stride=16), :] for z in range(2)], axis=1
-                )
-                for i in range(4)
-            ]
-            left, right = (a[0], a[1]), (a[2], a[3])
-            s, d = add(left, right), sub(left, right)
-            even = cmul(*weights(k, 0, NZ), s)
-            odd = cmul(*weights(k, 1, NZ), d)
-            parts = [left, add(even, odd), cmul(*weights(k, 2, NZ), s), sub(even, odd)]
             for t in range(4):
-                re, im = w[m, t, 0, there, :] + parts[t][0], w[m, t, 1, there, :] + parts[t][1]
-                c, sn = cs[0, t, here, :], cs[1, t, here, :]
-                o[0, m, t, here, :] = c * re + sn * im
-                o[1, m, t, here, :] = c * im - sn * re
-        leave(n).start()
+                rotate_out(o, cs_own, m, t, rows, o[0, m, t, rows, :], o[1, m, t, rows, :])
+        leave(0, idx, o, out, sems, n).start()
     for n in range(64 // CHUNK):
-        leave(n).wait()
-
-
-def finish_own_kernel(idx, w, cs, y, coef, out, o, sems):
-    finish_kernel(0, idx, w, cs, y, coef, out, o, sems)
+        leave(0, idx, o, out, sems, n).wait()
+    copies[1].wait()
 
 
 def finish_other_kernel(idx, w, cs, y, coef, before, out, o, sems):
-    finish_kernel(1, idx, w, cs, y, coef, out, o, sems)
+    for n in range(64 // CHUNK):
+        rows = slice(n * CHUNK, (n + 1) * CHUNK)
+        for m, t, re, im in gather_half(1, idx, w, y, coef, n):
+            rotate_out(o, cs, m, t, rows, re, im)
+        leave(1, idx, o, out, sems, n).start()
+    for n in range(64 // CHUNK):
+        leave(1, idx, o, out, sems, n).wait()
 
 
 def call(kernel, idx, args, in_specs, out_shape, out_specs, grid=(1,), scratch=(), aliases=None, flops=0, nbytes=0):
@@ -606,6 +644,7 @@
             pltpu.VMEM((256, 768), bf16),
             pltpu.VMEM((2, 4, 2, LR, NZ), f32),
             pltpu.VMEM((2, 4, LR, NZ), f32),
+            pltpu.VMEM((2, 2, 2, 256, NZ), bf16),
             pltpu.SemaphoreType.DMA((len(stored),)),
             pltpu.SemaphoreType.DMA((9,)),
             pltpu.SemaphoreType.DMA((24,)),
@@ -674,14 +713,13 @@
     )
     y = exchange(y)
     near_cs = sds((2, 4, 64, NZ), f32)
-    keep, send, cs_own, cs_other, cell = call(
+    keep, send = call(
         spread_kernel,
         idx,
-        (*near(y, mA, chip_table, w), *far(cs), stored[2]),
-        [VM] * 4 + [ANY] * 2,
-        (lines, lines, near_cs, near_cs, targets[2]),
-        (VM,) * 5,
-        scratch=(pltpu.SemaphoreType.DMA((3,)),),
+        near(y, mA, chip_table, w),
+        [VM] * 4,
+        (lines, lines),
+        (VM,) * 2,
         flops=1 << 20,
         nbytes=5 << 20,
     )
@@ -689,8 +727,15 @@
     scratch = (pltpu.VMEM((2, 2, 4, 64, NZ), f32), pltpu.SemaphoreType.DMA((64 // CHUNK,)))
     whole_out = pltpu.HBM(wave.shape, f32)
     work = dict(flops=1 << 22, nbytes=6 << 20)
-    out = call(
-        finish_own_kernel, idx, near(w, cs_own, keep, cell), [VM] * 4, whole_out, ANY, scratch=scratch, **work
+    out, cs_other, cell = call(
+        finish_own_kernel,
+        idx,
+        (*near(w, keep), stored[2], *far(cs)),
+        [VM] * 2 + [ANY] * 2,
+        (whole_out, near_cs, targets[2]),
+        (ANY, VM, VM),
+        scratch=(*scratch[:1], pltpu.VMEM((2, 4, 64, NZ), f32), scratch[1], pltpu.SemaphoreType.DMA((3,))),
+        **work,
     )
     return call(
         finish_other_kernel,

time: 61.9 us -> 61.7 us (level)
  transfers between devices with their start and end apart: 4 -> 4, of which waited for: 2 -> 2; matrix products, arithmetic and copies ran while one was open for 0% -> 0% of each run, Pallas kernels for 20% -> 21%
where the time goes in v5:
time: 61.7 us; the launch traced here: 61.5 us
  blocking collectives  21.7 us (35%)
  Pallas kernels  21.3 us (35%)
  starting transfers between devices  11.2 us (18%)
  waiting for transfers between devices  7.11 us (12%)
    all_to_all x1, blocking collectives, body(): x = exchange(UV)  21.7 us
    pallas_call x9, Pallas kernels, call(): pl.pallas_call(kernel, out_shape=out_shape, grid_spec=pltpu.PrefetchScala...  21.3 us
    all_to_all x1, waiting for transfers between devices, body(): y = exchange(y)  5.57 us
    all_to_all x1, starting transfers between devices, body(): y = exchange(y)  4.76 us
    ppermute x1, starting transfers between devices, body(): received = lax.ppermute(send, 'ang', other)  3.22 us
    ppermute x1, starting transfers between devices, body(): halo = lax.ppermute(rim, 'rad', [(0, 1), (1, 0)])  2.19 us
    ppermute x1, waiting for transfers between devices, body(): received = lax.ppermute(uv[1024:], 'ang', other)  1.54 us
  transfers between devices with their start and end apart: 4, of which 2 were waited for; matrix products, arithmetic and copies ran while one was open for 0% of the time, Pallas kernels for 21%

profile of v5, /device:TPU:1, one launch (start us, length us, event | category | flops | bytes accessed | tf_op | source)
XLA Modules:
  0.0 61.5 jit_solution(1788298518999848797)
XLA Ops:
  0.0 1.5 %rim_kernel.1 = f32[16,2048]{1,0:T(8,128)S(1)} custom-call(s32[8]{0:T(128)S(1)} %compare_select_fusion.6.idx, f32[2,2,4,128,256]{4,3,2,1,0:T(8,128)} %w.3, f32[4,128,256]{2,1,0:T(8,128)} %pot.3), custom_call_target="tpu_custom_call" | custom-call | tf_op jit(solution)/shard_map/rim_kernel/pallas_call | solution.py:565
  1.5 2.2 %collective-permute-start = (f32[16,2048]{1,0:T(8,128)S(1)}, f32[16,2048]{1,0:T(8,128)S(1)}, u32[]{:S(2)}, u32[]{:S(2)}) collective-permute-start(f32[16,2048]{1,0:T(8,128)S(1)} %rim_kernel.1), channel_id=1, source_target_pairs={{0,1},{1,0},{2,3},{3,2},{4,5},{5,4},{6,7},{7,6},{8,9},{9,8},{10,11... | collective-permute-start | bytes 393224 | tf_op jit(solution)/shard_map/ppermute | solution.py:622
  3.7 5.1 %advance_kernel.1 = (f32[2,2,4,2,64,256]{5,4,3,2,1,0:T(8,128)}, f32[2,2,4,64,256]{4,3,2,1,0:T(8,128)}, f32[2048,128]{1,0:T(8,128)S(1)}, f32[2,16,16]{2,1,0:T(8,1...) custom-call(s32[8]{0:T(128)S(1)} %compare_select_fusion.6.idx, ...), custom_call_target="tpu_custom_call" | custom-call | flops 1073741824 | bytes 5242880 | tf_op jit(solution)/shard_map/advance_kernel/pallas_call | solution.py:565
  8.8 0.0 collective-permute-done.halo.halo_far
  8.8 0.0 copy-start
  8.8 0.9 %halo_kernel.1 = f32[2048,128]{1,0:T(8,128)S(1)} custom-call(s32[8]{0:T(128)S(1)} %compare_select_fusion.6.idx, f32[16,2048]{1,0:T(8,128)S(1)} %collective-permute-done.halo.halo_far, f32[2,16,16]{2,1,0:T(8,128)S(1)} %get-tuple-element.27.table, f32[128,128]{1,0:T(8,128)S(1)} %get-tuple-element.28.coef, ...), custom_call_target="tpu_custom_call", output_to_operand_aliasing={{}: (4, {})} | custom-call | flops 1048576 | bytes 1048576 | tf_op jit(solution)/shard_map/halo_kernel/pallas_call | solution.py:565
  9.8 0.1 fusion
  9.8 0.0 copy-done
  9.8 1.0 %collective-permute-start.1 = (f32[1024,128]{1,0:T(8,128)S(1)}, f32[1024,128]{1,0:T(8,128)S(1)}, u32[]{:S(2)}, u32[]{:S(2)}) collective-permute-start(f32[1024,128]{1,0:T(8,128)S(1)} %get-tuple-element.47), channel_id=1, source_target_pairs={{0,2},{2,0},{4,6},{6,4},{8,10},{10,8},{12,14},{14,12},{16,18},{18,... | collective-permute-start | bytes 1572872 | tf_op jit(solution)/shard_map/ppermute | solution.py:671
  10.9 1.5 %collective-permute-done.1.received = f32[1024,128]{1,0:T(8,128)S(1)} collective-permute-done((f32[1024,128]{1,0:T(8,128)S(1)}, f32[1024,128]{1,0:T(8,128)S(1)}, u32[]{:S(2)}, u32[]{:S(2)}) %collective-permute-start.1) | collective-permute-done | bytes 524320 | tf_op jit(solution)/shard_map/ppermute | solution.py:671
  12.4 0.7 %pair_kernel.1 = (f32[1024,128]{1,0:T(8,128)S(1)}, f32[512,128]{1,0:T(8,128)S(1)}) custom-call(s32[8]{0:T(128)S(1)} %compare_select_fusion.6.idx, f32[1024,128]{1,0:T(8,128)S(1)} %get-tuple-element.48.own, f32[1024,128]{1,0:T(8,128)S(1)} %collective-permute-done.1.received, f32[4,64,1,128]{3,2,1,0:T(1,128)S(1)} %get-tuple-element.30.chip), custom_call_target="tpu_custom_call" | custom-call | flops 1048576 | bytes 2097152 | tf_op jit(solution)/shard_map/pair_kernel/pallas_call | solution.py:565
  13.2 21.7 %all_to_all.22 = f32[32,32,128]{2,1,0:T(8,128)S(1)} all-to-all(f32[32,32,128]{2,1,0:T(8,128)S(1)} %bitcast.7), channel_id=1, replica_groups={{0,4,8,12,16,20,24,28,32,36,40,44,48,52,56,60,64,68,72,76,80,84,88,92,9..., dimensions={0} | all-to-all | bytes 1048576 | tf_op jit(solution)/shard_map/all_to_all | solution.py:682
  34.8 2.3 %middle_kernel.1 = f32[32,4,8,128]{3,2,1,0:T(8,128)} custom-call(s32[8]{0:T(128)S(1)} %compare_select_fusion.6.idx, f32[1024,128]{1,0:T(8,128)S(1)} %bitcast.6, bf16[2,128,256]{2,1,0:T(8,128)(2,1)S(1)} %get-tuple-element.33.fwd, bf16[2,256,128]{2,1,0:T(8,128)(2,1)S(1)} %get-tuple-element.34.inv, f32[1,128]{1,0:T(1,128)S(1)} %get-tuple-element.35.mid, ...), custom_call_target="tpu_custom_call" | custom-call | flops 536870912 | bytes 3145728 | tf_op jit(solution)/shard_map/middle_kernel/pallas_call | solution.py:565
  37.2 4.8 %all-to-all-start.1 = ((f32[32,32,128]{2,1,0:T(8,128)}), f32[32,32,128]{2,1,0:T(8,128)S(1)}, u32[]{:S(2)}, u32[]{:S(2)}) async-start(f32[32,32,128]{2,1,0:T(8,128)} %bitcast.8), calls=%async_computation.1 | async-start | bytes 1048576 | tf_op jit(solution)/shard_map/all_to_all | solution.py:714
  41.9 5.3 %local_kernel.1 = (f32[2,4,2,128,256]{4,3,2,1,0:T(8,128)S(1)}, f32[1024,128]{1,0:T(8,128)S(1)}, f32[2,64,1,128]{3,2,1,0:T(1,128)S(1)}) custom-call(s32[8]{0:T(128)S(1)} %compare_select_fusion.6.idx, f32[2,2,4,2,64,256]{5,4,3,2,1,0:T(8,128)} %get-tuple-element.26.f, f32[16,2048]{1,0:T(8,128)} %copy-done, f32[512,128]{1,0:T(8,128)S(1)} %get-tuple-element.31.m_rows, ...), custom_call_target="tpu_custom_call" | custom-call | flops 3221225472 | bytes 5242880 | tf_op jit(solution)/shard_map/local_kernel/pallas_call | solution.py:565
  47.3 5.6 %all-to-all-done.1 = f32[32,32,128]{2,1,0:T(8,128)S(1)} async-done(((f32[32,32,128]{2,1,0:T(8,128)}), f32[32,32,128]{2,1,0:T(8,128)S(1)}, u32[]{:S(2)}, u32[]{:S(2)}) %all-to-all-start.1) | async-done | bytes 524320 | tf_op jit(solution)/shard_map/all_to_all | solution.py:714
  52.8 0.8 %spread_kernel.1 = (f32[1024,128]{1,0:T(8,128)S(1)}, f32[1024,128]{1,0:T(8,128)S(1)}) custom-call(s32[8]{0:T(128)S(1)} %compare_select_fusion.6.idx, f32[1024,128]{1,0:T(8,128)S(1)} %bitcast.5, f32[1024,128]{1,0:T(8,128)S(1)} %get-tuple-element.39.mA, f32[2,64,1,128]{3,2,1,0:T(1,128)S(1)} %get-tuple-element.40.chip, ...), custom_call_target="tpu_custom_call" | custom-call | flops 1048576 | bytes 5242880 | tf_op jit(solution)/shard_map/spread_kernel/pallas_call | solution.py:565
  53.6 3.2 %collective-permute-start.2 = (f32[1024,128]{1,0:T(8,128)S(1)}, f32[1024,128]{1,0:T(8,128)S(1)}, u32[]{:S(2)}, u32[]{:S(2)}) collective-permute-start(f32[1024,128]{1,0:T(8,128)S(1)} %get-tuple-element.44), channel_id=1, source_target_pairs={{0,2},{2,0},{4,6},{6,4},{8,10},{10,8},{12,14},{14,12},{16,18},{18,... | collective-permute-start | bytes 1572872 | tf_op jit(solution)/shard_map/ppermute | solution.py:726
  56.8 2.8 %finish_own_kernel.1 = (f32[2,2,4,128,256]{4,3,2,1,0:T(8,128)}, f32[2,4,64,256]{3,2,1,0:T(8,128)S(1)}, f32[128,128]{1,0:T(8,128)S(1)}) custom-call(s32[8]{0:T(128)S(1)} %compare_select_fusion.6.idx, f32[2,4,2,128,256]{4,3,2,1,0:T(8,128)S(1)} %get-tuple-element.38.after.w, f32[1024,128]{1,0:T(8,128)S(1)} %get-tuple-element.41.y, ...), custom_call_target="tpu_custom_call" | custom-call | flops 4194304 | bytes 6291456 | tf_op jit(solution)/shard_map/finish_own_kernel/pallas_call | solution.py:565
  59.6 0.0 collective-permute-done.2.y
  59.6 1.9 %finish_other_kernel.1 = f32[2,2,4,128,256]{4,3,2,1,0:T(8,128)} custom-call(s32[8]{0:T(128)S(1)} %compare_select_fusion.6.idx, f32[2,4,2,128,256]{4,3,2,1,0:T(8,128)S(1)} %get-tuple-element.38.after.w, f32[2,4,64,256]{3,2,1,0:T(8,128)S(1)} %get-tuple-element.43.cs, f32[1024,128]{1,0:T(8,128)S(1)} %collective-permute-done.2.y, ...), custom_call_target="tpu_custom_call", output_to_operand_aliasing={{}: (5, {})} | custom-call | flops 4194304 | bytes 6291456 | tf_op jit(solution)/shard_map/finish_other_kernel/pallas_call | solution.py:565
  (1 shorter events, 0.0 us)
Async XLA Ops:
  1.5 7.3 %collective-permute-start = (f32[16,2048]{1,0:T(8,128)S(1)}, f32[16,2048]{1,0:T(8,128)S(1)}, u32[]{:S(2)}, u32[]{:S(2)}) collective-permute-start(f32[16,2048]{1,0:T(8,128)S(1)} %rim_kernel.1), channel_id=1, source_target_pairs={{0,1},{1,0},{2,3},{3,2},{4,5},{5,4},{6,7},{7,6},{8,9},{9,8},{10,11... | collective-permute-start | bytes 393224 | tf_op jit(solution)/shard_map/ppermute | solution.py:622
  8.8 1.0 %copy-start = (f32[16,2048]{1,0:T(8,128)}, f32[16,2048]{1,0:T(8,128)S(1)}, u32[]{:S(2)}) copy-start(f32[16,2048]{1,0:T(8,128)S(1)} %collective-permute-done.halo.halo_far) | copy-start | bytes 393220
  9.8 2.6 %collective-permute-start.1 = (f32[1024,128]{1,0:T(8,128)S(1)}, f32[1024,128]{1,0:T(8,128)S(1)}, u32[]{:S(2)}, u32[]{:S(2)}) collective-permute-start(f32[1024,128]{1,0:T(8,128)S(1)} %get-tuple-element.47), channel_id=1, source_target_pairs={{0,2},{2,0},{4,6},{6,4},{8,10},{10,8},{12,14},{14,12},{16,18},{18,... | collective-permute-start | bytes 1572872 | tf_op jit(solution)/shard_map/ppermute | solution.py:671
  37.2 15.7 %all-to-all-start.1 = ((f32[32,32,128]{2,1,0:T(8,128)}), f32[32,32,128]{2,1,0:T(8,128)S(1)}, u32[]{:S(2)}, u32[]{:S(2)}) async-start(f32[32,32,128]{2,1,0:T(8,128)} %bitcast.8), calls=%async_computation.1 | async-start | bytes 1048576 | tf_op jit(solution)/shard_map/all_to_all | solution.py:714
  53.6 6.0 %collective-permute-start.2 = (f32[1024,128]{1,0:T(8,128)S(1)}, f32[1024,128]{1,0:T(8,128)S(1)}, u32[]{:S(2)}, u32[]{:S(2)}) collective-permute-start(f32[1024,128]{1,0:T(8,128)S(1)} %get-tuple-element.44), channel_id=1, source_target_pairs={{0,2},{2,0},{4,6},{6,4},{8,10},{10,8},{12,14},{14,12},{16,18},{18,... | collective-permute-start | bytes 1572872 | tf_op jit(solution)/shard_map/ppermute | solution.py:726

commit v6 on v5

--- a/solution.py
+++ b/solution.py
@@ -481,13 +481,16 @@
     return pltpu.make_async_copy(cs.at[row], cs_out, sem)
 
 
-def spread_kernel(idx, y, mA, chip, after, keep, send):
+def spread_kernel(idx, y, mA, chip, after, cell_far, keep, send, cell, sem):
+    copy = pltpu.make_async_copy(cell_far.at[idx[0]], cell, sem)
+    copy.start()
     x = tiles(y[...])
     total = x + row_swap(x, 4)
     inner = row_times(chip, 0, total) + tiles(mA[...])
     mask = first_rows(idx[1], x.shape)
     keep[...] = jnp.where(mask, x, inner).reshape(keep.shape)
     send[...] = jnp.where(mask, inner, x).reshape(keep.shape)
+    copy.wait()
 
 
 CHUNK = 16
@@ -527,13 +530,10 @@
     return pltpu.make_async_copy(o.at[:, :, :, rows, :], out.at[:, :, :, there, :], sems.at[n])
 
 
-def finish_own_kernel(idx, w, y, cell_far, cs_far, out, cs_other, cell, o, cs_own, sems, more):
-    near_cell = pltpu.make_async_copy(cell_far.at[idx[0]], cell, more.at[2])
-    near_cell.start()
+def finish_own_kernel(idx, w, y, cell, cs_far, out, cs_other, o, cs_own, sems, more):
     copies = [fetch(idx[1] ^ i, cs_far, x, more.at[i]) for i, x in enumerate((cs_own, cs_other))]
     for copy in copies:
         copy.start()
-    near_cell.wait()
     for n in range(64 // CHUNK):
         rows = slice(n * CHUNK, (n + 1) * CHUNK)
         for m, t, re, im in gather_half(0, idx, w, y, cell, n):
@@ -713,13 +713,14 @@
     )
     y = exchange(y)
     near_cs = sds((2, 4, 64, NZ), f32)
-    keep, send = call(
+    keep, send, cell = call(
         spread_kernel,
         idx,
-        near(y, mA, chip_table, w),
-        [VM] * 4,
-        (lines, lines),
-        (VM,) * 2,
+        (*near(y, mA, chip_table, w), stored[2]),
+        [VM] * 4 + [ANY],
+        (lines, lines, targets[2]),
+        (VM,) * 3,
+        scratch=(pltpu.SemaphoreType.DMA,),
         flops=1 << 20,
         nbytes=5 << 20,
     )
@@ -727,14 +728,14 @@
     scratch = (pltpu.VMEM((2, 2, 4, 64, NZ), f32), pltpu.SemaphoreType.DMA((64 // CHUNK,)))
     whole_out = pltpu.HBM(wave.shape, f32)
     work = dict(flops=1 << 22, nbytes=6 << 20)
-    out, cs_other, cell = call(
+    out, cs_other = call(
         finish_own_kernel,
         idx,
-        (*near(w, keep), stored[2], *far(cs)),
-        [VM] * 2 + [ANY] * 2,
-        (whole_out, near_cs, targets[2]),
-        (ANY, VM, VM),
-        scratch=(*scratch[:1], pltpu.VMEM((2, 4, 64, NZ), f32), scratch[1], pltpu.SemaphoreType.DMA((3,))),
+        (*near(w, keep, cell), *far(cs)),
+        [VM] * 3 + [ANY],
+        (whole_out, near_cs),
+        (ANY, VM),
+        scratch=(*scratch[:1], pltpu.VMEM((2, 4, 64, NZ), f32), scratch[1], pltpu.SemaphoreType.DMA((2,))),
         **work,
     )
     return call(

time: 61.7 us -> 62.5 us (1.013)
  Pallas kernels: 21.3 us -> 22 us
    pallas_call x9, Pallas kernels: 21.3 us -> 22 us  [call(): pl.pallas_call(kernel, out_shape=out_shape, grid_spec=pltpu.PrefetchScala...]
where the time goes in v6:
time: 62.5 us; the launch traced here: 62.2 us
  Pallas kernels  22 us (35%)
  blocking collectives  21.7 us (35%)
  starting transfers between devices  11.2 us (18%)
  waiting for transfers between devices  7.11 us (11%)
    pallas_call x9, Pallas kernels, call(): pl.pallas_call(kernel, out_shape=out_shape, grid_spec=pltpu.PrefetchScala...  22 us
    all_to_all x1, blocking collectives, body(): x = exchange(UV)  21.7 us
    all_to_all x1, waiting for transfers between devices, body(): y = exchange(y)  5.57 us
    all_to_all x1, starting transfers between devices, body(): y = exchange(y)  4.76 us
    ppermute x1, starting transfers between devices, body(): received = lax.ppermute(send, 'ang', other)  3.22 us
    ppermute x1, starting transfers between devices, body(): halo = lax.ppermute(rim, 'rad', [(0, 1), (1, 0)])  2.19 us
    ppermute x1, waiting for transfers between devices, body(): received = lax.ppermute(uv[1024:], 'ang', other)  1.54 us
  transfers between devices with their start and end apart: 4, of which 2 were waited for; matrix products, arithmetic and copies ran while one was open for 0% of the time, Pallas kernels for 21%

profile of v6, /device:TPU:1, one launch (start us, length us, event | category | flops | bytes accessed | tf_op | source)
XLA Modules:
  0.0 62.2 jit_solution(11788716065096065172)
XLA Ops:
  0.0 1.5 %rim_kernel.1 = f32[16,2048]{1,0:T(8,128)S(1)} custom-call(s32[8]{0:T(128)S(1)} %compare_select_fusion.6.idx, f32[2,2,4,128,256]{4,3,2,1,0:T(8,128)} %w.3, f32[4,128,256]{2,1,0:T(8,128)} %pot.3), custom_call_target="tpu_custom_call" | custom-call | tf_op jit(solution)/shard_map/rim_kernel/pallas_call | solution.py:565
  1.5 2.2 %collective-permute-start = (f32[16,2048]{1,0:T(8,128)S(1)}, f32[16,2048]{1,0:T(8,128)S(1)}, u32[]{:S(2)}, u32[]{:S(2)}) collective-permute-start(f32[16,2048]{1,0:T(8,128)S(1)} %rim_kernel.1), channel_id=1, source_target_pairs={{0,1},{1,0},{2,3},{3,2},{4,5},{5,4},{6,7},{7,6},{8,9},{9,8},{10,11... | collective-permute-start | bytes 393224 | tf_op jit(solution)/shard_map/ppermute | solution.py:622
  3.7 5.1 %advance_kernel.1 = (f32[2,2,4,2,64,256]{5,4,3,2,1,0:T(8,128)}, f32[2,2,4,64,256]{4,3,2,1,0:T(8,128)}, f32[2048,128]{1,0:T(8,128)S(1)}, f32[2,16,16]{2,1,0:T(8,1...) custom-call(s32[8]{0:T(128)S(1)} %compare_select_fusion.6.idx, ...), custom_call_target="tpu_custom_call" | custom-call | flops 1073741824 | bytes 5242880 | tf_op jit(solution)/shard_map/advance_kernel/pallas_call | solution.py:565
  8.8 0.0 collective-permute-done.halo.halo_far
  8.8 0.0 copy-start
  8.8 0.9 %halo_kernel.1 = f32[2048,128]{1,0:T(8,128)S(1)} custom-call(s32[8]{0:T(128)S(1)} %compare_select_fusion.6.idx, f32[16,2048]{1,0:T(8,128)S(1)} %collective-permute-done.halo.halo_far, f32[2,16,16]{2,1,0:T(8,128)S(1)} %get-tuple-element.27.table, f32[128,128]{1,0:T(8,128)S(1)} %get-tuple-element.28.coef, ...), custom_call_target="tpu_custom_call", output_to_operand_aliasing={{}: (4, {})} | custom-call | flops 1048576 | bytes 1048576 | tf_op jit(solution)/shard_map/halo_kernel/pallas_call | solution.py:565
  9.8 0.1 fusion
  9.8 0.0 copy-done
  9.8 1.0 %collective-permute-start.1 = (f32[1024,128]{1,0:T(8,128)S(1)}, f32[1024,128]{1,0:T(8,128)S(1)}, u32[]{:S(2)}, u32[]{:S(2)}) collective-permute-start(f32[1024,128]{1,0:T(8,128)S(1)} %get-tuple-element.47), channel_id=1, source_target_pairs={{0,2},{2,0},{4,6},{6,4},{8,10},{10,8},{12,14},{14,12},{16,18},{18,... | collective-permute-start | bytes 1572872 | tf_op jit(solution)/shard_map/ppermute | solution.py:671
  10.9 1.5 %collective-permute-done.1.received = f32[1024,128]{1,0:T(8,128)S(1)} collective-permute-done((f32[1024,128]{1,0:T(8,128)S(1)}, f32[1024,128]{1,0:T(8,128)S(1)}, u32[]{:S(2)}, u32[]{:S(2)}) %collective-permute-start.1) | collective-permute-done | bytes 524320 | tf_op jit(solution)/shard_map/ppermute | solution.py:671
  12.4 0.7 %pair_kernel.1 = (f32[1024,128]{1,0:T(8,128)S(1)}, f32[512,128]{1,0:T(8,128)S(1)}) custom-call(s32[8]{0:T(128)S(1)} %compare_select_fusion.6.idx, f32[1024,128]{1,0:T(8,128)S(1)} %get-tuple-element.48.own, f32[1024,128]{1,0:T(8,128)S(1)} %collective-permute-done.1.received, f32[4,64,1,128]{3,2,1,0:T(1,128)S(1)} %get-tuple-element.30.chip), custom_call_target="tpu_custom_call" | custom-call | flops 1048576 | bytes 2097152 | tf_op jit(solution)/shard_map/pair_kernel/pallas_call | solution.py:565
  13.2 21.7 %all_to_all.22 = f32[32,32,128]{2,1,0:T(8,128)S(1)} all-to-all(f32[32,32,128]{2,1,0:T(8,128)S(1)} %bitcast.7), channel_id=1, replica_groups={{0,4,8,12,16,20,24,28,32,36,40,44,48,52,56,60,64,68,72,76,80,84,88,92,9..., dimensions={0} | all-to-all | bytes 1048576 | tf_op jit(solution)/shard_map/all_to_all | solution.py:682
  34.8 2.3 %middle_kernel.1 = f32[32,4,8,128]{3,2,1,0:T(8,128)} custom-call(s32[8]{0:T(128)S(1)} %compare_select_fusion.6.idx, f32[1024,128]{1,0:T(8,128)S(1)} %bitcast.6, bf16[2,128,256]{2,1,0:T(8,128)(2,1)S(1)} %get-tuple-element.33.fwd, bf16[2,256,128]{2,1,0:T(8,128)(2,1)S(1)} %get-tuple-element.34.inv, f32[1,128]{1,0:T(1,128)S(1)} %get-tuple-element.35.mid, ...), custom_call_target="tpu_custom_call" | custom-call | flops 536870912 | bytes 3145728 | tf_op jit(solution)/shard_map/middle_kernel/pallas_call | solution.py:565
  37.2 4.8 %all-to-all-start.1 = ((f32[32,32,128]{2,1,0:T(8,128)}), f32[32,32,128]{2,1,0:T(8,128)S(1)}, u32[]{:S(2)}, u32[]{:S(2)}) async-start(f32[32,32,128]{2,1,0:T(8,128)} %bitcast.8), calls=%async_computation.1 | async-start | bytes 1048576 | tf_op jit(solution)/shard_map/all_to_all | solution.py:714
  41.9 5.3 %local_kernel.1 = (f32[2,4,2,128,256]{4,3,2,1,0:T(8,128)S(1)}, f32[1024,128]{1,0:T(8,128)S(1)}, f32[2,64,1,128]{3,2,1,0:T(1,128)S(1)}) custom-call(s32[8]{0:T(128)S(1)} %compare_select_fusion.6.idx, f32[2,2,4,2,64,256]{5,4,3,2,1,0:T(8,128)} %get-tuple-element.26.f, f32[16,2048]{1,0:T(8,128)} %copy-done, f32[512,128]{1,0:T(8,128)S(1)} %get-tuple-element.31.m_rows, ...), custom_call_target="tpu_custom_call" | custom-call | flops 3221225472 | bytes 5242880 | tf_op jit(solution)/shard_map/local_kernel/pallas_call | solution.py:565
  47.3 5.6 %all-to-all-done.1 = f32[32,32,128]{2,1,0:T(8,128)S(1)} async-done(((f32[32,32,128]{2,1,0:T(8,128)}), f32[32,32,128]{2,1,0:T(8,128)S(1)}, u32[]{:S(2)}, u32[]{:S(2)}) %all-to-all-start.1) | async-done | bytes 524320 | tf_op jit(solution)/shard_map/all_to_all | solution.py:714
  52.8 1.4 %spread_kernel.1 = (f32[1024,128]{1,0:T(8,128)S(1)}, f32[1024,128]{1,0:T(8,128)S(1)}, f32[128,128]{1,0:T(8,128)S(1)}) custom-call(s32[8]{0:T(128)S(1)} %compare_select_fusion.6.idx, f32[1024,128]{1,0:T(8,128)S(1)} %bitcast.5, f32[1024,128]{1,0:T(8,128)S(1)} %get-tuple-element.39.mA, f32[2,64,1,128]{3,2,1,0:T(1,128)S(1)} %get-tuple-element.40.chip, ...), custom_call_target="tpu_custom_call" | custom-call | flops 1048576 | bytes 5242880 | tf_op jit(solution)/shard_map/spread_kernel/pallas_call | solution.py:565
  54.2 3.2 %collective-permute-start.2 = (f32[1024,128]{1,0:T(8,128)S(1)}, f32[1024,128]{1,0:T(8,128)S(1)}, u32[]{:S(2)}, u32[]{:S(2)}) collective-permute-start(f32[1024,128]{1,0:T(8,128)S(1)} %get-tuple-element.45), channel_id=1, source_target_pairs={{0,2},{2,0},{4,6},{6,4},{8,10},{10,8},{12,14},{14,12},{16,18},{18,... | collective-permute-start | bytes 1572872 | tf_op jit(solution)/shard_map/ppermute | solution.py:727
  57.5 2.9 %finish_own_kernel.1 = (f32[2,2,4,128,256]{4,3,2,1,0:T(8,128)}, f32[2,4,64,256]{3,2,1,0:T(8,128)S(1)}) custom-call(s32[8]{0:T(128)S(1)} %compare_select_fusion.6.idx, f32[2,4,2,128,256]{4,3,2,1,0:T(8,128)S(1)} %get-tuple-element.38.after.w, f32[1024,128]{1,0:T(8,128)S(1)} %get-tuple-element.41.y, f32[128,128]{1,0:T(8,128)S(1)} %get-tuple-element.42.cell.coef, ...), custom_call_target="tpu_custom_call" | custom-call | flops 4194304 | bytes 6291456 | tf_op jit(solution)/shard_map/finish_own_kernel/pallas_call | solution.py:565
  60.3 0.0 collective-permute-done.2.y
  60.4 1.9 %finish_other_kernel.1 = f32[2,2,4,128,256]{4,3,2,1,0:T(8,128)} custom-call(s32[8]{0:T(128)S(1)} %compare_select_fusion.6.idx, f32[2,4,2,128,256]{4,3,2,1,0:T(8,128)S(1)} %get-tuple-element.38.after.w, f32[2,4,64,256]{3,2,1,0:T(8,128)S(1)} %get-tuple-element.44.cs, f32[1024,128]{1,0:T(8,128)S(1)} %collective-permute-done.2.y, ...), custom_call_target="tpu_custom_call", output_to_operand_aliasing={{}: (5, {})} | custom-call | flops 4194304 | bytes 6291456 | tf_op jit(solution)/shard_map/finish_other_kernel/pallas_call | solution.py:565
  (1 shorter events, 0.0 us)
Async XLA Ops:
  1.5 7.3 %collective-permute-start = (f32[16,2048]{1,0:T(8,128)S(1)}, f32[16,2048]{1,0:T(8,128)S(1)}, u32[]{:S(2)}, u32[]{:S(2)}) collective-permute-start(f32[16,2048]{1,0:T(8,128)S(1)} %rim_kernel.1), channel_id=1, source_target_pairs={{0,1},{1,0},{2,3},{3,2},{4,5},{5,4},{6,7},{7,6},{8,9},{9,8},{10,11... | collective-permute-start | bytes 393224 | tf_op jit(solution)/shard_map/ppermute | solution.py:622
  8.8 1.0 %copy-start = (f32[16,2048]{1,0:T(8,128)}, f32[16,2048]{1,0:T(8,128)S(1)}, u32[]{:S(2)}) copy-start(f32[16,2048]{1,0:T(8,128)S(1)} %collective-permute-done.halo.halo_far) | copy-start | bytes 393220
  9.8 2.6 %collective-permute-start.1 = (f32[1024,128]{1,0:T(8,128)S(1)}, f32[1024,128]{1,0:T(8,128)S(1)}, u32[]{:S(2)}, u32[]{:S(2)}) collective-permute-start(f32[1024,128]{1,0:T(8,128)S(1)} %get-tuple-element.47), channel_id=1, source_target_pairs={{0,2},{2,0},{4,6},{6,4},{8,10},{10,8},{12,14},{14,12},{16,18},{18,... | collective-permute-start | bytes 1572872 | tf_op jit(solution)/shard_map/ppermute | solution.py:671
  37.2 15.7 %all-to-all-start.1 = ((f32[32,32,128]{2,1,0:T(8,128)}), f32[32,32,128]{2,1,0:T(8,128)S(1)}, u32[]{:S(2)}, u32[]{:S(2)}) async-start(f32[32,32,128]{2,1,0:T(8,128)} %bitcast.8), calls=%async_computation.1 | async-start | bytes 1048576 | tf_op jit(solution)/shard_map/all_to_all | solution.py:714
  54.2 6.1 %collective-permute-start.2 = (f32[1024,128]{1,0:T(8,128)S(1)}, f32[1024,128]{1,0:T(8,128)S(1)}, u32[]{:S(2)}, u32[]{:S(2)}) collective-permute-start(f32[1024,128]{1,0:T(8,128)S(1)} %get-tuple-element.45), channel_id=1, source_target_pairs={{0,2},{2,0},{4,6},{6,4},{8,10},{10,8},{12,14},{14,12},{16,18},{18,... | collective-permute-start | bytes 1572872 | tf_op jit(solution)/shard_map/ppermute | solution.py:727
